TPU v7x, 32 devices: a whole 2x2x4 slice. The times are simulated.
32 devices in a mesh: dp: 8 (over z, x), seq: 4 (over y, core).
Axes of the slice: x: 2, y: 2, z: 4, core: 2. Of those that a mesh axis runs over, the one named last changes fastest.
Arguments:
- hidden: bfloat16 [8, 1024, 1536], P('dp', 'seq'), may hold values from -6 to 6
- segments: int32 [8, 1024], P('dp', 'seq'), may hold values from 0 to 3, never falling along the last dimension, each value on 1 to 768 neighbouring positions
- cotangent: bfloat16 [8, 1024, 1536], P('dp', 'seq'), may hold values from -6 to 6
- norm_gain: float32 [1536], replicated, may hold values from 0.5 to 1.5
- in_weight: float32 [1536, 6448], P(('dp', 'seq')), may hold values from -0.15625 to 0.15625
- conv_weight: float32 [4, 3328], replicated, may hold values from -3 to 3
- conv_bias: float32 [3328], replicated, may hold values from -3 to 3
- step_bias: float32 [48], replicated, may hold values from -4 to -1
- log_rate: float32 [48], replicated, may hold values from -5 to 0.5
- skip_gain: float32 [48], replicated, may hold values from 0.5 to 1.5
- gate_gain: float32 [3072], replicated, may hold values from 0.5 to 1.5
- out_weight: float32 [3072, 1536], P(('dp', 'seq')), may hold values from -0.109375 to 0.109375
Outputs:
- result: bfloat16 [8, 1024, 1536], P('dp', 'seq')
- d_hidden: float32 [8, 1024, 1536], P('dp', 'seq')
- d_norm_gain: float32 [1536], replicated
- d_in_weight: float32 [1536, 6448], P(('dp', 'seq'))
- d_conv_weight: float32 [4, 3328], replicated
- d_conv_bias: float32 [3328], replicated
- d_step_bias: float32 [48], replicated
- d_log_rate: float32 [48], replicated
- d_skip_gain: float32 [48], replicated
- d_gate_gain: float32 [3072], replicated
- d_out_weight: float32 [3072, 1536], P(('dp', 'seq'))
Inputs may be any that keep to these rules, and one draw needn't show every extreme that they name: `segments`: along each sequence the numbers never fall; a document is a run of equal numbers of 1 to 768 tokens, and one run holds exactly 768.
All inputs are finite; a program needn't handle non-finite values.
Results may differ from a plain program's by a relative error of at most 0.0096.
Values may be sent and summed in bfloat16 or wider, within the bound.
No kernel may reach another device: no remote copies, remote signals or barrier semaphores. Data moves between devices by JAX's collectives and lax.ppermute only.
A program may use at most 256 MiB of HBM per device.

v0:
```python
import functools

import jax
import jax.numpy as jnp
from jax import lax
from jax.experimental import pallas as pl
from jax.experimental.layout import Layout, with_layout_constraint
from jax.experimental.pallas import tpu as pltpu
from jax.sharding import PartitionSpec as P

epsilon = 1e-05
highest = lax.Precision.HIGHEST
f32 = jnp.float32
bf16 = jnp.bfloat16
LANES = 128
HALO = 16
NEG = -1e30


def mm(a, b, dims, out=f32):
    return lax.dot_general(a, b, (dims, ((), ())), preferred_element_type=out)


NN = ((1,), (0,))
NT = ((1,), (1,))
TN = ((0,), (0,))


def exact(a, b, dims):
    return lax.dot_general(a, b, (dims, ((), ())), precision=highest, preferred_element_type=f32)


def softplus(v):
    return jnp.maximum(v, 0.0) + jnp.log1p(jnp.exp(-jnp.abs(v)))


def sigmoid(v):
    return 1.0 / (1.0 + jnp.exp(-v))


def lane_iota(shape):
    return lax.broadcasted_iota(jnp.int32, shape, len(shape) - 1)


def spread(columns, first, second, wide):
    rows = columns.shape[0]
    left = jnp.broadcast_to(columns[:, first : first + 1], (rows, LANES))
    right = jnp.broadcast_to(columns[:, second : second + 1], (rows, LANES))
    return jnp.where(wide, left, right)


def step_parts(raw, rate, q):
    row = lax.broadcasted_iota(jnp.int32, (q, q), 0)
    col = lax.broadcasted_iota(jnp.int32, (q, q), 1)
    tri = jnp.where(row >= col, 1.0, 0.0).astype(f32)
    step = softplus(raw)
    decay = -step * rate
    total = exact(tri, decay, NN)
    return step, decay, total, tri, row >= col


def convolve(ext, docs_ext, own, weights, bias, lanes, q, taps):
    running = bias + weights[0:1, lanes] * ext[pl.ds(HALO, q), lanes]
    for lag in range(1, taps):
        same = jnp.where(docs_ext[pl.ds(HALO - lag, q), :] == own, 1.0, 0.0)
        running = running + weights[lag : lag + 1, lanes] * ext[pl.ds(HALO - lag, q), lanes] * same
    return running


def scan_forward(
    q, taps, pairs, head,
    x_ref, small_ref, bct_ref, dcol_ref, drow_ref, w_ref, b_ref, sb_ref, rate_ref, skip_ref,
    y_ref, states_ref,
    state, ext, docs_ext, xs, xt, last_doc,
):
    c = pl.program_id(0)
    n = bct_ref.shape[0] // 2

    @pl.when(c == 0)
    def _():
        state[...] = jnp.zeros_like(state)
        ext[pl.ds(0, HALO), :] = jnp.zeros((HALO, ext.shape[1]), f32)
        docs_ext[pl.ds(0, HALO), :] = jnp.full((HALO, LANES), -1.0, f32)
        last_doc[...] = jnp.full(last_doc.shape, -1.0, f32)

    own = dcol_ref[...]
    ext[pl.ds(HALO, q), :] = x_ref[...].astype(f32)
    docs_ext[pl.ds(HALO, q), :] = own
    step, _, cum, _, causal = step_parts(small_ref[...] + sb_ref[...], rate_ref[...], q)
    step_t = step.T
    cum_t = cum.T
    end = cum[q - 1 : q, :]
    id_in = last_doc[0:1, :]
    final = own[q - 1 : q, :]
    linked = jnp.where(final == id_in, 1.0, 0.0)
    fade = linked * jnp.exp(end)
    entering = jnp.where(own == id_in, 1.0, 0.0) * jnp.exp(cum)
    to_end = jnp.where(own == final, 1.0, 0.0) * jnp.exp(end - cum) * step
    same_doc = jnp.broadcast_to(own[:, 0:1], (q, q)) == jnp.broadcast_to(drow_ref[0:1, :], (q, q))
    hide = jnp.where(jnp.logical_and(causal, same_doc), 0.0, NEG)
    bt = bct_ref[0:n, :]
    ct = bct_ref[n : 2 * n, :]
    scores = mm(ct, bt, TN)
    states_ref[0] = state[...]
    old = state[...].astype(bf16)
    wide = lane_iota((q, LANES)) < head
    wide_row = lane_iota((1, LANES)) < head
    for k in range(pairs):
        lanes = slice(k * LANES, (k + 1) * LANES)
        h0, h1 = 2 * k, 2 * k + 1
        conv = convolve(ext, docs_ext, own, w_ref, b_ref[:, lanes], lanes, q, taps)
        x = conv * sigmoid(conv)
        xd = x * spread(step, h0, h1, wide)
        xt[:, lanes] = (x * spread(to_end, h0, h1, wide)).astype(bf16)
        mats = []
        for h in (h0, h1):
            gap = cum[:, h : h + 1] - cum_t[h : h + 1, :] + hide
            mats.append((jnp.exp(gap) * scores).astype(bf16))
        out = mm(mats[0], jnp.where(wide, xd, 0.0).astype(bf16), NN)
        out = out + mm(mats[1], jnp.where(wide, 0.0, xd).astype(bf16), NN)
        out = out + mm(ct, old[:, lanes], TN) * spread(entering, h0, h1, wide)
        y_ref[:, lanes] = out + skip_ref[:, lanes] * x
    update = mm(bt, xt[...], NN)
    for k in range(pairs):
        lanes = slice(k * LANES, (k + 1) * LANES)
        state[:, lanes] = state[:, lanes] * spread(fade, 2 * k, 2 * k + 1, wide_row) + update[:, lanes]
    ext[pl.ds(0, HALO), :] = ext[pl.ds(q, HALO), :]
    docs_ext[pl.ds(0, HALO), :] = docs_ext[pl.ds(q, HALO), :]
    last_doc[...] = jnp.broadcast_to(final, last_doc.shape)


def scan_backward(
    q, taps, pairs, head, chunks,
    x_ref, xp_ref, small_ref, bct_ref, dcol_ref, dcolp_ref, drow_ref, w_ref, b_ref, sb_ref, rate_ref,
    skip_ref, dy_ref, states_ref,
    dx_ref, dsmall_ref, dbct_ref, dconv_ref, dhead_ref,
    dstate, ext, docs_ext, dcv, docs_after, dye, xt, col_t,
):
    step_at = pl.program_id(0)
    c = chunks - 1 - step_at
    n = bct_ref.shape[0] // 2
    width = x_ref.shape[1]

    @pl.when(step_at == 0)
    def _():
        dstate[...] = jnp.zeros_like(dstate)
        dcv[pl.ds(q, HALO), :] = jnp.zeros((HALO, width), f32)
        docs_after[pl.ds(q, HALO), :] = jnp.full((HALO, LANES), -1.0, f32)
        dconv_ref[...] = jnp.zeros_like(dconv_ref)
        dhead_ref[...] = jnp.zeros_like(dhead_ref)
        col_t[...] = jnp.zeros_like(col_t)

    first = c == 0
    own = dcol_ref[...]
    before = jnp.where(first, -1.0, dcolp_ref[...])
    ext[pl.ds(0, HALO), :] = xp_ref[...].astype(f32)
    ext[pl.ds(HALO, q), :] = x_ref[...].astype(f32)
    docs_ext[pl.ds(0, HALO), :] = before
    docs_ext[pl.ds(HALO, q), :] = own
    docs_after[pl.ds(0, q), :] = own
    raw = small_ref[...] + sb_ref[...]
    rate = rate_ref[...]
    step, decay, cum, tri, causal = step_parts(raw, rate, q)
    step_t = step.T
    cum_t = cum.T
    end = cum[q - 1 : q, :]
    id_in = before[HALO - 1 : HALO, :]
    final = own[q - 1 : q, :]
    linked = jnp.where(final == id_in, 1.0, 0.0)
    fade = linked * jnp.exp(end)
    entering = jnp.where(own == id_in, 1.0, 0.0) * jnp.exp(cum)
    tail = jnp.where(own == final, 1.0, 0.0) * jnp.exp(end - cum)
    to_end = tail * step
    same_doc = jnp.broadcast_to(own[:, 0:1], (q, q)) == jnp.broadcast_to(drow_ref[0:1, :], (q, q))
    hide = jnp.where(jnp.logical_and(causal, same_doc), 0.0, NEG)
    bt = bct_ref[0:n, :]
    ct = bct_ref[n : 2 * n, :]
    scores = mm(ct, bt, TN)
    old = states_ref[0].astype(bf16)
    after = dstate[...].astype(bf16)
    wide = lane_iota((q, LANES)) < head
    wide_row = lane_iota((1, LANES)) < head
    lane = lane_iota((q, LANES))
    d_scores = jnp.zeros((q, q), f32)
    rows = jnp.zeros((q, LANES), f32)
    d_enter = jnp.zeros((q, LANES), f32)
    d_toend = jnp.zeros((q, LANES), f32)
    d_fade = jnp.zeros((8, LANES), f32)
    part = lax.broadcasted_iota(jnp.int32, (LANES, LANES), 0) // head
    to = lane_iota((LANES, LANES))
    for k in range(pairs):
        lanes = slice(k * LANES, (k + 1) * LANES)
        h0, h1 = 2 * k, 2 * k + 1
        pick = jnp.where(part + 2 * k == to, 1.0, 0.0)
        conv = convolve(ext, docs_ext, own, w_ref, b_ref[:, lanes], lanes, q, taps)
        sig = sigmoid(conv)
        x = conv * sig
        xb = x.astype(bf16)
        dy = dy_ref[:, lanes]
        halves = (jnp.where(wide, dy, 0.0).astype(bf16), jnp.where(wide, 0.0, dy).astype(bf16))
        dxd = jnp.zeros((q, LANES), f32)
        for h, half in ((h0, halves[0]), (h1, halves[1])):
            inner = mm(half, xb, NT)
            keep = jnp.exp(cum[:, h : h + 1] - cum_t[h : h + 1, :] + hide)
            grown = keep * inner
            mat = keep * scores
            dt = step_t[h : h + 1, :]
            g = grown * scores
            d_scores = d_scores + grown * dt
            rows = jnp.where(lane == h, jnp.sum(g * dt, axis=1, keepdims=True), rows)
            col_t[h : h + 1, :] = jnp.sum(g, axis=0, keepdims=True)
            dxd = dxd + mm(mat.astype(bf16), half, TN)
        v = mm(bt, after[:, lanes], TN)
        u = mm(ct, old[:, lanes], TN)
        enter_k = spread(entering, h0, h1, wide)
        end_k = spread(to_end, h0, h1, wide)
        d_enter = d_enter + exact(dy * u, pick, NN)
        d_toend = d_toend + exact(x * v, pick, NN)
        hh = jnp.sum(dstate[:, lanes] * states_ref[0, :, lanes], axis=0, keepdims=True)
        d_fade = d_fade + exact(jnp.broadcast_to(hh, (8, LANES)), pick, NN)
        dye[:, lanes] = (dy * enter_k).astype(bf16)
        xt[:, lanes] = (x * end_k).astype(bf16)
        dx = dxd * spread(step, h0, h1, wide) + end_k * v + skip_ref[:, lanes] * dy
        dconv = dx * (sig * (1.0 + conv * (1.0 - sig)))
        dcv[pl.ds(0, q), lanes] = dconv
        sums = [jnp.sum(dconv * ext[pl.ds(HALO, q), lanes], axis=0, keepdims=True)]
        dxin = w_ref[0:1, lanes] * dconv
        for lag in range(1, taps):
            same = jnp.where(docs_ext[pl.ds(HALO - lag, q), :] == own, 1.0, 0.0)
            sums.append(jnp.sum(dconv * same * ext[pl.ds(HALO - lag, q), lanes], axis=0, keepdims=True))
            follow = jnp.where(docs_after[pl.ds(lag, q), :] == own, 1.0, 0.0)
            dxin = dxin + w_ref[lag : lag + 1, lanes] * dcv[pl.ds(lag, q), lanes] * follow
        sums.append(jnp.sum(dconv, axis=0, keepdims=True))
        sums.append(jnp.sum(dy * x, axis=0, keepdims=True))
        dx_ref[:, lanes] = dxin.astype(bf16)
        for i, s in enumerate(sums):
            dconv_ref[i : i + 1, lanes] = dconv_ref[i : i + 1, lanes] + s
    dsb = d_scores.astype(bf16)
    dbct_ref[0:n, :] = mm(ct, dsb, NN) + mm(after, xt[...], NT)
    dbct_ref[n : 2 * n, :] = mm(bt, dsb, NT) + mm(old, dye[...], NT)
    new = mm(ct, dye[...], NN)
    for k in range(pairs):
        lanes = slice(k * LANES, (k + 1) * LANES)
        dstate[:, lanes] = dstate[:, lanes] * spread(fade, 2 * k, 2 * k + 1, wide_row) + new[:, lanes]
    cols = col_t[...].T
    pulled = d_toend * to_end
    at_end = jnp.sum(pulled, axis=0, keepdims=True) + fade * d_fade[0:1, :]
    d_cum = rows - step * cols + d_enter * entering - pulled
    last_row = lax.broadcasted_iota(jnp.int32, (q, LANES), 0) == q - 1
    d_cum = d_cum + jnp.where(last_row, at_end, 0.0)
    d_decay = exact(tri, d_cum, TN)
    d_step = cols + d_toend * tail - rate * d_decay
    d_raw = d_step * sigmoid(raw)
    dsmall_ref[...] = d_raw
    dhead_ref[0:1, :] = dhead_ref[0:1, :] + jnp.sum(d_raw, axis=0, keepdims=True)
    dhead_ref[1:2, :] = dhead_ref[1:2, :] + jnp.sum(d_decay * decay, axis=0, keepdims=True)
    dcv[pl.ds(q, HALO), :] = dcv[pl.ds(0, HALO), :]
    docs_after[pl.ds(q, HALO), :] = docs_after[pl.ds(0, HALO), :]


def whole(array):
    return pl.BlockSpec(array.shape, lambda c: (0,) * array.ndim)


def run_forward(q, x_in, small, bct, dcol, drow, conv_w, conv_b, sb, rate, skip, head):
    tokens, width = x_in.shape
    n = bct.shape[0] // 2
    chunks = tokens // q
    pairs = width // LANES
    taps = conv_w.shape[0]
    return pl.pallas_call(
        functools.partial(scan_forward, q, taps, pairs, head),
        grid=(chunks,),
        in_specs=[
            pl.BlockSpec((q, width), lambda c: (c, 0)),
            pl.BlockSpec((q, LANES), lambda c: (c, 0)),
            pl.BlockSpec((2 * n, q), lambda c: (0, c)),
            pl.BlockSpec((q, LANES), lambda c: (c, 0)),
            pl.BlockSpec((8, q), lambda c: (0, c)),
            whole(conv_w), whole(conv_b), whole(sb), whole(rate), whole(skip),
        ],
        out_specs=[
            pl.BlockSpec((q, width), lambda c: (c, 0)),
            pl.BlockSpec((1, n, width), lambda c: (c, 0, 0)),
        ],
        out_shape=[
            jax.ShapeDtypeStruct((tokens, width), f32),
            jax.ShapeDtypeStruct((chunks, n, width), f32),
        ],
        scratch_shapes=[
            pltpu.VMEM((n, width), f32),
            pltpu.VMEM((HALO + q, width), f32),
            pltpu.VMEM((HALO + q, LANES), f32),
            pltpu.VMEM((8, LANES), f32),
            pltpu.VMEM((q, width), bf16),
            pltpu.VMEM((8, LANES), f32),
        ],
        name="scan_forward",
    )(x_in, small, bct, dcol, drow, conv_w, conv_b, sb, rate, skip)


def run_backward(q, x_in, small, bct, dcol, drow, conv_w, conv_b, sb, rate, skip, dy, states, head):
    tokens, width = x_in.shape
    n = bct.shape[0] // 2
    chunks = tokens // q
    pairs = width // LANES
    taps = conv_w.shape[0]
    per = q // HALO

    def at(c):
        return chunks - 1 - c

    def prior(c):
        return jnp.maximum((chunks - 1 - c) * per - 1, 0)

    return pl.pallas_call(
        functools.partial(scan_backward, q, taps, pairs, head, chunks),
        grid=(chunks,),
        in_specs=[
            pl.BlockSpec((q, width), lambda c: (at(c), 0)),
            pl.BlockSpec((HALO, width), lambda c: (prior(c), 0)),
            pl.BlockSpec((q, LANES), lambda c: (at(c), 0)),
            pl.BlockSpec((2 * n, q), lambda c: (0, at(c))),
            pl.BlockSpec((q, LANES), lambda c: (at(c), 0)),
            pl.BlockSpec((HALO, LANES), lambda c: (prior(c), 0)),
            pl.BlockSpec((8, q), lambda c: (0, at(c))),
            whole(conv_w), whole(conv_b), whole(sb), whole(rate), whole(skip),
            pl.BlockSpec((q, width), lambda c: (at(c), 0)),
            pl.BlockSpec((1, n, width), lambda c: (at(c), 0, 0)),
        ],
        out_specs=[
            pl.BlockSpec((q, width), lambda c: (at(c), 0)),
            pl.BlockSpec((q, LANES), lambda c: (at(c), 0)),
            pl.BlockSpec((2 * n, q), lambda c: (0, at(c))),
            pl.BlockSpec((8, width), lambda c: (0, 0)),
            pl.BlockSpec((8, LANES), lambda c: (0, 0)),
        ],
        out_shape=[
            jax.ShapeDtypeStruct((tokens, width), bf16),
            jax.ShapeDtypeStruct((tokens, LANES), f32),
            jax.ShapeDtypeStruct((2 * n, tokens), f32),
            jax.ShapeDtypeStruct((8, width), f32),
            jax.ShapeDtypeStruct((8, LANES), f32),
        ],
        scratch_shapes=[
            pltpu.VMEM((n, width), f32),
            pltpu.VMEM((HALO + q, width), f32),
            pltpu.VMEM((HALO + q, LANES), f32),
            pltpu.VMEM((q + HALO, width), f32),
            pltpu.VMEM((q + HALO, LANES), f32),
            pltpu.VMEM((q, width), bf16),
            pltpu.VMEM((q, width), bf16),
            pltpu.VMEM((LANES, q), f32),
        ],
        name="scan_backward",
    )(x_in, x_in, small, bct, dcol, dcol, drow, conv_w, conv_b, sb, rate, skip, dy, states)


def gate_forward(
    groups, z_rows, tall,
    normed_ref, cot_ref, joined_ref, y_ref, gain_ref, z_ref, dgn_ref, sums_ref, wz, wo,
):
    parts, held, width = wo.shape

    @pl.when(pl.program_id(0) == 0)
    def _():
        for g in range(groups):
            wz[pl.ds(g * z_rows, z_rows), :] = joined_ref[g, pl.ds(0, z_rows), :]
            for k in range(parts):
                wo[k, pl.ds(g * tall, tall), :] = joined_ref[g, pl.ds(z_rows + k * tall, tall), :]

    z = mm(normed_ref[...], wz[...], NN)
    d_gn = mm(cot_ref[:, 0:width], wo[0], NT)
    for k in range(1, parts):
        d_gn = d_gn + mm(cot_ref[:, k * width : (k + 1) * width], wo[k], NT)
    z_ref[...] = z
    dgn_ref[...] = d_gn
    gated = y_ref[...] * (z * sigmoid(z))
    square = jnp.sum(gated * gated, axis=1, keepdims=True)
    cross = jnp.sum(d_gn * gain_ref[...] * gated, axis=1, keepdims=True)
    lane = lane_iota((square.shape[0], LANES))
    sums_ref[...] = jnp.where(lane == 0, square, jnp.where(lane == 1, cross, 0.0)).T[0:8, :]


def gate_backward(
    blocks, tile, z_rows, tall, channels,
    normed_ref, cot_ref, y_ref, z_ref, dgn_ref, sums_ref, gain_ref,
    gate_ref, dz_ref, dy_ref, dgain_ref, terms_ref,
):
    step = pl.program_id(0)
    rows, width = y_ref.shape
    parts = normed_ref.shape[1] // width

    @pl.when(step == 0)
    def _():
        dgain_ref[...] = jnp.zeros_like(dgain_ref)

    @pl.when(step < blocks)
    def _():
        own = pl.ds(pl.multiple_of(step * rows, rows), rows)
        columns = jnp.concatenate([sums_ref[...], jnp.zeros((LANES - 8, rows), f32)], axis=0).T
        inv = lax.rsqrt(columns[:, 0:1] / channels + epsilon)
        slope = inv * inv * inv * (columns[:, 1:2] / channels)
        for k in range(width // LANES):
            lanes = slice(k * LANES, (k + 1) * LANES)
            y, z, d_gn, gain = y_ref[:, lanes], z_ref[:, lanes], dgn_ref[:, lanes], gain_ref[:, lanes]
            sig = sigmoid(z)
            act = z * sig
            gated = y * act
            scaled = gated * inv
            gate_ref[own, lanes] = (scaled * gain).astype(bf16)
            dgain_ref[0:1, lanes] = dgain_ref[0:1, lanes] + jnp.sum(d_gn * scaled, axis=0, keepdims=True)
            d_gated = inv * (d_gn * gain) - gated * slope
            dz_ref[own, lanes] = (d_gated * y * (sig * (1.0 + z * (1.0 - sig)))).astype(bf16)
            dy_ref[:, lanes] = d_gated * act

    def store(term, at, within, base):
        if within >= tile:
            start = pl.multiple_of(base + at * tile, 16)
            terms_ref[0, pl.ds(start, tile), :] = term
        else:
            for n in range(tile // within):
                piece = term[n * within : (n + 1) * within]
                terms_ref[at * (tile // within) + n, pl.ds(base, within), :] = piece

    @pl.when(step >= blocks)
    def _():
        i = step - blocks
        lanes = pl.ds(pl.multiple_of(i * tile, LANES), tile)
        store(mm(normed_ref[:, lanes], dz_ref[...], TN).astype(bf16), i, z_rows, 0)
        j = i // parts
        lanes = pl.ds(pl.multiple_of(j * tile, LANES), tile)
        left = gate_ref[:, lanes]
        for k in range(parts):

            @pl.when(i % parts == k)
            def _():
                right = cot_ref[:, k * width : (k + 1) * width]
                store(mm(left, right, TN).astype(bf16), j, tall, z_rows + k * tall)


def run_gate_forward(joined, z_rows, normed, cot, y, gain):
    groups, deep, width = joined.shape
    tokens, n_width = normed.shape
    parts = n_width // width
    tall = (deep - z_rows) // parts
    rows = min(256, tokens)

    def tokens_of(columns):
        return pl.BlockSpec((rows, columns), lambda c: (c, 0))

    return pl.pallas_call(
        functools.partial(gate_forward, groups, z_rows, tall),
        grid=(tokens // rows,),
        in_specs=[tokens_of(n_width), tokens_of(n_width), whole(joined), tokens_of(width), whole(gain)],
        out_specs=[tokens_of(width), tokens_of(width), pl.BlockSpec((8, rows), lambda c: (0, c))],
        out_shape=[
            jax.ShapeDtypeStruct((tokens, width), f32),
            jax.ShapeDtypeStruct((tokens, width), f32),
            jax.ShapeDtypeStruct((8, tokens), f32),
        ],
        scratch_shapes=[
            pltpu.VMEM((groups * z_rows, width), bf16),
            pltpu.VMEM((parts, groups * tall, width), bf16),
        ],
        name="gate_forward",
    )(normed, cot, joined, y, gain)


def run_gate_backward(groups, z_rows, tall, channels, normed, cot, y, z, d_gn, sums, gain):
    tokens, n_width = normed.shape
    width = y.shape[1]
    parts = n_width // width
    rows = min(256, tokens)
    blocks = tokens // rows
    tile = 3 * LANES
    deep = z_rows + parts * tall

    def tokens_of(columns):
        return pl.BlockSpec((rows, columns), lambda c: (jnp.minimum(c, blocks - 1), 0))

    return pl.pallas_call(
        functools.partial(gate_backward, blocks, tile, z_rows, tall, channels),
        grid=(blocks + n_width // tile,),
        in_specs=[
            whole(normed), whole(cot), tokens_of(width), tokens_of(width), tokens_of(width),
            pl.BlockSpec((8, rows), lambda c: (0, jnp.minimum(c, blocks - 1))), whole(gain),
        ],
        out_specs=[
            pl.BlockSpec((tokens, width), lambda c: (0, 0)),
            pl.BlockSpec((tokens, width), lambda c: (0, 0)),
            tokens_of(width),
            pl.BlockSpec((8, width), lambda c: (0, 0)),
            pl.BlockSpec((groups, deep, width), lambda c: (0, 0, 0)),
        ],
        out_shape=[
            jax.ShapeDtypeStruct((tokens, width), bf16),
            jax.ShapeDtypeStruct((tokens, width), bf16),
            jax.ShapeDtypeStruct((tokens, width), f32),
            jax.ShapeDtypeStruct((8, width), f32),
            jax.ShapeDtypeStruct((groups, deep, width), bf16),
        ],
        name="gate_backward",
    )(normed, cot, y, z, d_gn, sums, gain)


def swapped(block, bit):
    size = lax.axis_size("seq")
    return lax.ppermute(block, "seq", [(i, i ^ bit) for i in range(size)])


def bits_of(size):
    bits, bit = [], 1
    while bit < size:
        bits.append(bit)
        bit *= 2
    return bits


def joined_by(held, bit):
    other = swapped(held, bit)
    upper = (lax.axis_index("seq") & bit) != 0
    both = jnp.where(upper, jnp.stack([other, held], axis=1), jnp.stack([held, other], axis=1))
    return both.reshape((-1,) + both.shape[2:])


def opened(block):
    bits = bits_of(lax.axis_size("seq"))
    return joined_by(block[None], bits[-1]) if bits else block[None]


def gathered(block, held=None):
    held = opened(block) if held is None else held
    for bit in reversed(bits_of(lax.axis_size("seq"))[:-1]):
        held = joined_by(held, bit)
    return held.reshape((-1,) + held.shape[2:])


def scattered(parts, between=lambda held: held):
    index = lax.axis_index("seq")
    size = lax.axis_size("seq")
    rest = parts.shape[1:]
    lead = parts.shape[0]
    held = parts.reshape((size, lead // size) + rest)
    for bit in bits_of(size):
        half = held.reshape((held.shape[0] // 2, 2) + held.shape[1:])
        upper = (index & bit) != 0
        mine = jnp.where(upper, half[:, 1], half[:, 0])
        theirs = jnp.where(upper, half[:, 0], half[:, 1]).astype(bf16)
        held = between(mine.astype(f32) + swapped(theirs, bit).astype(f32))
    return held[0]


def added_over(block, bits):
    for bit in bits:
        block = block + crossed(block, bit)
    return block


def moved_by(block, step):
    count = lax.axis_size("dp")
    route = [(i, i + 2 * step) for i in range(count) if 0 <= i + 2 * step < count]
    return lax.ppermute(block, "dp", route)


def crossed(block, bits):
    return lax.ppermute(block, "dp", [(i, i ^ bits) for i in range(lax.axis_size("dp"))])


def gathered_rows(block, waits):
    count = lax.axis_size("dp")
    length = count // 2
    if not is_small(count):
        return lax.all_gather(block, "dp", axis=0, tiled=True), block
    at = lax.axis_index("dp")
    place, side = at // 2, at % 2
    rows = block.shape[0]
    whole_rows = jnp.zeros((count * rows, block.shape[1]), block.dtype)

    def put(into, piece, pair, half):
        return lax.dynamic_update_slice(into, piece, ((pair * 2 + half) * rows, 0))

    whole_rows = put(whole_rows, block, place, side)
    other = crossed(block, 1)
    whole_rows = put(whole_rows, other, place, 1 - side)
    up, down, ready = block, block, []
    for hop in range(1, length):
        up, down = after((moved_by(up, 1), moved_by(down, -1)), (other, waits[hop - 1 : hop]))
        ready.append((down, up))
        piece, pair = None, None
        for spot in range(length):
            near = min(spot, length - 1 - spot)
            if hop <= 2 * near:
                away, from_below = (hop + 1) // 2, hop % 2 == 0
            else:
                away, from_below = hop - near, spot > length - 1 - spot
            chosen = ready[away - 1][1 if from_below else 0]
            source = spot - away if from_below else spot + away
            here = place == spot
            piece = chosen if piece is None else jnp.where(here, chosen, piece)
            pair = source if pair is None else jnp.where(here, source, pair)
        whole_rows = put(whole_rows, piece, pair, side)
        other = crossed(piece, 1)
        whole_rows = put(whole_rows, other, pair, 1 - side)
    return whole_rows, ready[min(1, length - 2)]


def is_small(count):
    return count <= 8 and count & (count - 1) == 0


def halved_rows(term):
    count = lax.axis_size("dp")
    if not is_small(count):
        return term
    at = lax.axis_index("dp")
    pairs = term.reshape(count // 2, 2, -1, term.shape[1])

    def side(which):
        return lax.dynamic_index_in_dim(pairs, which, 1, keepdims=False)

    came = crossed(side((at & 1) ^ 1), 1)
    return (side(at & 1).astype(f32) + came.astype(f32)).astype(bf16)


def shared_rows(lines):
    count = lax.axis_size("dp")
    if not is_small(count):
        return [lax.psum_scatter(lines, "dp", scatter_dimension=0, tiled=True)]
    at = lax.axis_index("dp")

    def part(owner):
        return lax.dynamic_index_in_dim(lines, owner // 2, 0, keepdims=False)

    return [part(at)] + [crossed(part(at ^ bits), bits) for bits in range(2, count, 2)]


def after(value, other):
    return lax.optimization_barrier((value, other))[0]


def turned(blocks):
    size = lax.axis_size("seq")
    index = lax.axis_index("seq")
    if size & (size - 1):
        return lax.all_to_all(blocks, "seq", 0, 0, tiled=True)
    out = blocks
    for bits in range(1, size):
        piece = lax.dynamic_slice_in_dim(blocks, index ^ bits, 1, 0)
        piece = lax.ppermute(piece, "seq", [(i, i ^ bits) for i in range(size)])
        out = lax.dynamic_update_slice_in_dim(out, piece, index ^ bits, 0)
    return out


def folded(rows, lead, width):
    cut = rows.reshape(lead, rows.shape[0] // lead, rows.shape[1] // width, width)
    cut = cut.transpose(0, 2, 1, 3).reshape(lead, -1, width)
    return cut[0] if lead == 1 else cut


def unfolded(pieces, width):
    lead, stacked, narrow = pieces.shape
    cut = pieces.reshape(lead, width // narrow, stacked * narrow // width, narrow)
    return cut.transpose(0, 2, 1, 3).reshape(-1, width)


def exchanged(parts):
    size = lax.axis_size("seq")
    index = lax.axis_index("seq")
    held = parts.reshape((size, -1) + parts.shape[1:])

    def part(owner):
        return lax.dynamic_index_in_dim(held, owner, 0, keepdims=False)

    came = [
        lax.ppermute(part(index ^ bits).astype(bf16), "seq", [(i, i ^ bits) for i in range(size)])
        for bits in range(1, size)
    ]
    return sum([piece.astype(f32) for piece in came], part(index))


def by_rows(array):
    return with_layout_constraint(array, Layout(major_to_minor=(0, 1)))


def padded(rows, width):
    return jnp.pad(rows, ((0, 0), (0, width - rows.shape[1])))


def shards(
    hidden, segments, cotangent, norm_gain, in_weight, conv_weight, conv_bias, step_bias, log_rate,
    skip_gain, gate_gain, out_weight,
):
    n_seqs, block, n_width = hidden.shape
    size = lax.axis_size("seq")
    groups = lax.axis_size("dp")
    index = lax.axis_index("seq")
    tokens = size * block
    n_inner = gate_gain.shape[0]
    n_heads = step_bias.shape[0]
    n_taps = conv_weight.shape[0]
    n_mixed = conv_bias.shape[0]
    n_state = (n_mixed - n_inner) // 2
    head = n_inner // n_heads
    own_inner = n_inner // size
    own_heads = n_heads // size
    own_bc = 2 * n_state // size
    q = min(128, block)
    in_rows = in_weight.shape[0]

    in_low = in_weight.astype(bf16)
    z_cols = in_low[:, :n_inner].reshape(in_rows, size, own_inner)
    x_cols = in_low[:, n_inner : 2 * n_inner].reshape(in_rows, size, own_inner)
    bc_cols = in_low[:, 2 * n_inner : n_inner + n_mixed].reshape(in_rows, size, own_bc)
    dt_cols = in_low[:, n_inner + n_mixed :].reshape(in_rows, size, own_heads)
    gap = jnp.zeros((in_rows, size, LANES - own_heads - own_bc), bf16)
    laid = jnp.concatenate([x_cols, dt_cols, gap, bc_cols, z_cols], axis=2).transpose(1, 0, 2)
    mine = lax.all_to_all(laid, "seq", 0, 0, tiled=True)
    flat = hidden.reshape(block, n_width).astype(f32)
    inv = lax.rsqrt(jnp.mean(flat * flat, axis=-1, keepdims=True) + epsilon)
    unit = flat * inv
    normed_own = (unit * norm_gain).astype(bf16)
    docs = gathered(segments).reshape(tokens).astype(f32)
    order = [(f, (f % groups) * size + f // groups) for f in range(groups * size)]
    back = [(b, a) for a, b in order]
    out_moved = lax.ppermute(out_weight.astype(bf16), ("dp", "seq"), order)
    mine, normed_own = lax.optimization_barrier((after(mine, docs), normed_own))
    mine = mine.reshape(size * in_rows, -1)
    n_first = own_inner + LANES
    cot_own = cotangent.reshape(block, n_width)
    normed_held = opened(normed_own)
    cot_held = opened(after(cot_own, mine))
    w_first, hopped = gathered_rows(mine[:, :n_first], [normed_held, cot_held])
    z_block = jnp.concatenate([mine[:, n_first:], folded(after(out_moved, hopped), 1, own_inner)], axis=0)

    normed = gathered(normed_own, normed_held)
    joined = lax.all_gather(z_block, "dp", axis=0, tiled=True).reshape(groups, -1, own_inner)
    z_rows = size * in_rows
    w_z = joined[:, :z_rows].reshape(-1, own_inner)
    w_out = unfolded(joined[:, z_rows:], n_width)
    cot = gathered(cot_own, cot_held)
    dcol = jnp.broadcast_to(docs[:, None], (tokens, LANES))
    drow = jnp.broadcast_to(docs[None, :], (8, tokens))

    def own_part(vector, parts):
        return lax.dynamic_slice_in_dim(vector, index * parts, parts, vector.ndim - 1)

    w_x, w_small = w_first[:, :own_inner], w_first[:, own_inner:]
    small = mm(normed, w_small, NN)
    x_in = mm(normed, w_x, NN).astype(bf16)
    conv_x = own_part(conv_weight[:, :n_inner], own_inner)
    bias_x = own_part(conv_bias[None, :n_inner], own_inner)
    conv_bc = own_part(conv_weight[:, n_inner:], own_bc)
    bias_bc = own_part(conv_bias[None, n_inner:], own_bc)
    sb = padded(own_part(step_bias[None], own_heads), LANES)
    rate = padded(jnp.exp(own_part(log_rate[None], own_heads)), LANES)
    skip = jnp.repeat(own_part(skip_gain[None], own_heads), head, axis=1)
    gain = own_part(gate_gain[None], own_inner)

    head_lanes = jnp.arange(LANES) < own_heads
    bc_in = small[:, LANES - own_bc :].astype(bf16).astype(f32)
    small_dt = jnp.where(head_lanes, small, 0.0)

    def earlier(rows, lag):
        return jnp.pad(rows, ((lag, 0), (0, 0)))[:tokens]

    def later(rows, lag):
        return jnp.pad(rows, ((0, lag), (0, 0)))[lag:]

    same = [None] + [
        jnp.where(jnp.pad(docs, (lag, 0), constant_values=-1.0)[:tokens] == docs, 1.0, 0.0)[:, None]
        for lag in range(1, n_taps)
    ]
    bc_conv = bias_bc + conv_bc[0:1] * bc_in
    for lag in range(1, n_taps):
        bc_conv = bc_conv + conv_bc[lag : lag + 1] * earlier(bc_in, lag) * same[lag]
    bc_sig = jax.nn.sigmoid(bc_conv)
    bct = gathered(by_rows((bc_conv * bc_sig).astype(bf16).T))

    y, states = run_forward(
        q, x_in, small_dt, bct, dcol, drow, conv_x, bias_x, sb, rate, skip, head
    )

    out_rows = own_inner // groups
    tiled = z_rows % 16 == 0 and out_rows % 16 == 0
    if tiled:
        lead, deep, tall, gate_in = groups, z_rows, out_rows, joined
    else:
        lead, deep, tall = 1, groups * z_rows, own_inner
        gate_in = jnp.concatenate([w_z, folded(w_out, 1, own_inner)], axis=0)[None]
    z, d_gn, sums = run_gate_forward(gate_in, deep, normed, cot, y, gain)
    sums = lax.psum(sums[:2], "seq")
    sums = jnp.pad(sums, ((0, 6), (0, 0)))
    gate_low, d_z, d_y, d_gain, terms = run_gate_backward(
        lead, deep, tall, n_inner, normed, cot, y, z, d_gn, sums, gain
    )
    d_gain = d_gain[0]
    if not tiled:
        z_term = terms[0, :deep].reshape(groups, z_rows, own_inner)
        out_term = terms[0, deep:].reshape(n_width // own_inner, groups, out_rows, own_inner)
        out_term = out_term.transpose(1, 0, 2, 3).reshape(groups, -1, own_inner)
        terms = jnp.concatenate([z_term, out_term], axis=1)
    terms = terms.reshape(-1, own_inner)
    parts = lax.psum_scatter(terms, "dp", scatter_dimension=0, tiled=True)

    d_x, d_dt, d_bct, d_conv_x, d_heads = run_backward(
        q, x_in, small_dt, bct, dcol, drow, conv_x, bias_x, sb, rate, skip, d_y, states, head
    )
    x_term = mm(normed, d_x, TN).astype(bf16)
    x_term, d_bct = lax.optimization_barrier((x_term, d_bct))
    x_lines = halved_rows(x_term)
    d_bc = by_rows(exchanged(d_bct)).T
    d_bcc = d_bc * (bc_sig * (1.0 + bc_conv * (1.0 - bc_sig)))
    d_bc_in = conv_bc[0:1] * d_bcc
    w_sums = [jnp.sum(d_bcc * bc_in, axis=0)]
    for lag in range(1, n_taps):
        held = d_bcc * same[lag]
        d_bc_in = d_bc_in + conv_bc[lag : lag + 1] * later(held, lag)
        w_sums.append(jnp.sum(held * earlier(bc_in, lag), axis=0))
    w_sums.append(jnp.sum(d_bcc, axis=0))
    d_small = jnp.concatenate([d_dt[:, : LANES - own_bc], d_bc_in], axis=1).astype(bf16)
    d_first = jnp.concatenate([d_x, d_small], axis=1)
    small_lines = halved_rows(mm(normed, d_small, TN).astype(bf16))
    branch = scattered(mm(after(gate_low, d_bc), w_out, NN).astype(bf16))
    result = (flat + branch).reshape(n_seqs, block, n_width).astype(bf16)
    d_first = after(d_first, x_lines)
    d_normed = mm(d_first, w_first, NT) + mm(d_z, w_z, NT)
    d_norm_gain = jnp.sum(d_normed * normed.astype(f32), axis=0) / norm_gain
    d_skip = jnp.sum(d_conv_x[n_taps + 1].reshape(own_heads, head), axis=1)
    packed = jnp.concatenate(
        [
            d_conv_x[: n_taps + 1].reshape(-1),
            jnp.stack(w_sums).reshape(-1),
            d_gain,
            d_heads[0, :own_heads],
            d_heads[1, :own_heads],
            d_skip,
            d_norm_gain,
        ]
    )
    lines = jnp.concatenate([x_lines, small_lines], axis=-1)
    packed = added_over(packed, reversed(bits_of(groups)[1:]))
    lines, packed = lax.optimization_barrier((lines, packed))
    shares = shared_rows(lines)
    packed = gathered(added_over(packed, bits_of(groups)[:1])[None])
    parts, result = lax.optimization_barrier((after(parts, shares[:2]), result))
    d_norm = after(d_normed.astype(bf16), parts)
    d_norm = lax.psum_scatter(d_norm, "seq", scatter_dimension=0, tiled=True).astype(f32)

    def own_rows(part):
        out = turned(part.reshape(size, in_rows, -1))
        return out.transpose(1, 0, 2).astype(f32)

    out_part = unfolded(parts[None, z_rows:], n_width)
    d_out_weight = lax.ppermute(out_part, ("dp", "seq"), back).astype(f32)
    in_z = own_rows(parts[:z_rows])
    shares, in_z, d_out_weight = lax.optimization_barrier((shares, in_z, d_out_weight))
    first_part = sum(share.astype(f32) for share in shares)
    in_first = own_rows(first_part.astype(bf16))
    d_in_weight = jnp.concatenate(
        [
            in_z.reshape(in_rows, n_inner),
            in_first[:, :, :own_inner].reshape(in_rows, n_inner),
            in_first[:, :, n_first - own_bc :].reshape(in_rows, 2 * n_state),
            in_first[:, :, own_inner : own_inner + own_heads].reshape(in_rows, n_heads),
        ],
        axis=1,
    )

    lifted = d_norm * norm_gain
    d_flat = inv * lifted - flat * (
        inv * inv * inv * jnp.mean(lifted * flat, axis=-1, keepdims=True)
    )
    d_hidden = (cot_own.astype(f32) + d_flat).reshape(n_seqs, block, n_width)

    at = 0

    def take(count):
        nonlocal at
        at += count
        return packed[:, at - count : at]

    got_x = take((n_taps + 1) * own_inner).reshape(size, n_taps + 1, own_inner)
    got_bc = take((n_taps + 1) * own_bc).reshape(size, n_taps + 1, own_bc)
    got_x = got_x.transpose(1, 0, 2).reshape(n_taps + 1, n_inner)
    got_bc = got_bc.transpose(1, 0, 2).reshape(n_taps + 1, 2 * n_state)
    conv_all = jnp.concatenate([got_x, got_bc], axis=1)
    d_gate_gain = take(own_inner).reshape(n_inner)
    d_step_bias = take(own_heads).reshape(n_heads)
    d_log_rate = take(own_heads).reshape(n_heads)
    d_skip_gain = take(own_heads).reshape(n_heads)
    d_norm_all = jnp.sum(take(n_width), axis=0)
    return (
        result,
        d_hidden,
        d_norm_all,
        d_in_weight,
        conv_all[:n_taps],
        conv_all[n_taps],
        d_step_bias,
        d_log_rate,
        d_skip_gain,
        d_gate_gain,
        d_out_weight,
    )


def solution(mesh):
    tokens = P("dp", "seq", None)
    rows = P(("dp", "seq"), None)
    return jax.shard_map(
        shards,
        mesh=mesh,
        in_specs=(tokens, P("dp", "seq"), tokens, P(), rows, P(), P(), P(), P(), P(), P(), rows),
        out_specs=(tokens, tokens, P(), rows, P(), P(), P(), P(), P(), P(), rows),
        check_vma=False,
    )
```

profile of v0, /device:TPU:2, one launch (start us, length us, event | category | flops | bytes accessed | tf_op | source)
XLA Modules:
  0.0 392.6 jit_solution(16283955984480177738)
XLA Ops:
  12.5 3.6 all-to-all-start
  18.1 8.1 %all-to-all-done = bf16[4,48,1664]{2,1,0:T(8,128)(2,1)S(1)} async-done(((bf16[4,48,1664]{2,1,0:T(8,128)(2,1)}), bf16[4,48,1664]{2,1,0:T(8,128)(2,1)S(1)}, u32[]{:S(2)}, u32[]{:S(2)}) %all-to-all-start) | async-done | bytes 639008 | tf_op jit(solution)/shard_map/all_to_all | solution.py:718
  30.1 3.5 collective-permute-start.7
  38.4 8.2 %collective-permute-done.2 = bf16[1,256,1536]{2,1,0:T(8,128)(2,1)S(1)} collective-permute-done((bf16[1,256,1536]{2,1,0:T(8,128)(2,1)S(1)}, bf16[1,256,1536]{2,1,0:T(8,128)(2,1)S(1)}, u32[]{:S(2)}, u32[]{:S(2)}) %collective-permute-start.2) | collective-permute-done | bytes 786464 | tf_op jit(solution)/shard_map/ppermute | solution.py:509
  49.3 3.5 collective-permute-start.10
  54.2 6.5 %collective-permute-start.18 = (bf16[96,1536]{1,0:T(8,128)(2,1)S(1)}, bf16[96,1536]{1,0:T(8,128)(2,1)}, u32[]{:S(2)}, u32[]{:S(2)}) collective-permute-start(bf16[96,1536]{1,0:T(8,128)(2,1)S(1)} %convert_element_type.205), channel_id=1, source_target_pairs={{0,0},{1,4},{2,8},{3,12},{4,16},{5,20},{6,24},{7,28},{8,1},{9,5},{... | collective-permute-start | bytes 884744 | tf_op jit(solution)/shard_map/ppermute | solution.py:726
  64.6 4.6 %collective-permute-done.18 = bf16[96,1536]{1,0:T(8,128)(2,1)} collective-permute-done((bf16[96,1536]{1,0:T(8,128)(2,1)S(1)}, bf16[96,1536]{1,0:T(8,128)(2,1)}, u32[]{:S(2)}, u32[]{:S(2)}) %collective-permute-start.18) | collective-permute-done | bytes 294944 | tf_op jit(solution)/shard_map/ppermute | solution.py:726
  75.1 7.7 %collective-permute-start.3 = (bf16[2,256,1536]{2,1,0:T(8,128)(2,1)}, bf16[2,256,1536]{2,1,0:T(8,128)(2,1)}, u32[]{:S(2)}, u32[]{:S(2)}) collective-permute-start(bf16[2,256,1536]{2,1,0:T(8,128)(2,1)} %maximum_select_fusion.2), channel_id=1, source_target_pairs={{0,1},{1,0},{2,3},{3,2},{4,5},{5,4},{6,7},{7,6},{8,9},{9,8},{10,11... | collective-permute-start | bytes 4718600 | tf_op jit(solution)/shard_map/ppermute | solution.py:509
  82.9 2.0 collective-permute-start.13
  88.1 2.1 constant_dynamic-update-slice_fusion.6
  90.2 5.1 %collective-permute-start.12 = (bf16[192,896]{1,0:T(8,128)(2,1)}, bf16[192,896]{1,0:T(8,128)(2,1)}, u32[]{:S(2)}, u32[]{:S(2)}) collective-permute-start(bf16[192,896]{1,0:T(8,128)(2,1)} %get-tuple-element.110), channel_id=1, source_target_pairs={{0,4},{4,0},{8,12},{12,8},{16,20},{20,16},{24,28},{28,24},{1,5},{5... | collective-permute-start | bytes 1032200 | tf_op jit(solution)/shard_map/ppermute | solution.py:567
  110.7 1.9 constant_dynamic-update-slice_fusion.4
  112.6 7.7 %collective-permute-start.15 = (bf16[192,896]{1,0:T(8,128)(2,1)S(1)}, bf16[192,896]{1,0:T(8,128)(2,1)S(1)}, u32[]{:S(2)}, u32[]{:S(2)}) collective-permute-start(bf16[192,896]{1,0:T(8,128)(2,1)S(1)} %get-tuple-element.108), channel_id=1, source_target_pairs={{0,4},{4,0},{8,12},{12,8},{16,20},{20,16},{24,28},{28,24},{1,5},{5... | collective-permute-start | bytes 1032200 | tf_op jit(solution)/shard_map/ppermute | solution.py:567
  120.8 11.3 %collective-permute-done.15 = bf16[192,896]{1,0:T(8,128)(2,1)S(1)} collective-permute-done((bf16[192,896]{1,0:T(8,128)(2,1)S(1)}, bf16[192,896]{1,0:T(8,128)(2,1)S(1)}, u32[]{:S(2)}, u32[]{:S(2)}) %collective-permute-start.15) | collective-permute-done | bytes 344096 | tf_op jit(solution)/shard_map/ppermute | solution.py:567
  132.2 3.1 maximum_select_fusion
  137.9 3.7 fusion.8.x_ref.xp_ref
  141.6 1.9 maximum_select_fusion.1
  147.8 13.5 %scan_forward.1 = (f32[1024,768]{1,0:T(8,128)}, f32[8,128,768]{2,1,0:T(8,128)}) custom-call(bf16[1024,768]{1,0:T(8,128)(2,1)} %fusion.8.x_ref.xp_ref, f32[1024,128]{1,0:T(8,128)} %broadcast_select_fusion.1.small_ref, bf16[256,1024]{1,0:T(8,128)(2,1)} %bitcast.212, f32[1024,128]{1,0:T(8,128)} %broadcast_in_dim.78.dcol_ref.dcolp_ref, ...), custom_call_target="tpu_custom_call" | custom-call | tf_op jit(solution)/shard_map/scan_forward/pallas_call | solution.py:271
  161.2 5.0 %all-gather.2.cloned.1.call-done = bf16[3072,768]{1,0:T(8,128)(2,1)} async-done(((bf16[384,768]{1,0:T(8,128)(2,1)}), bf16[3072,768]{1,0:T(8,128)(2,1)}) %all-gather.2.cloned.1.call-update) | async-done | bytes 4718608 | tf_op jit(solution)/shard_map/all_gather | solution.py:737
  166.2 10.8 %gate_forward.1 = (f32[1024,768]{1,0:T(8,128)}, f32[1024,768]{1,0:T(8,128)}, f32[8,1024]{1,0:T(8,128)}) custom-call(bf16[1024,1536]{1,0:T(8,128)(2,1)} %bitcast.194, bf16[1024,1536]{1,0:T(8,128)(2,1)} %bitcast.198, bf16[8,384,768]{2,1,0:T(8,128)(2,1)} %bitcast.200, f32[1024,768]{1,0:T(8,128)} %get-tuple-element.63.y_ref, f32[1,768]{1,0:T(1,128)} %dynamic_slice.80.gain_ref), custom_call_target="tpu_custom_call" | custom-call | tf_op jit(solution)/shard_map/gate_forward/pallas_call | solution.py:452
  177.8 5.7 %psum.7 = f32[2,1024]{1,0:T(2,128)S(1)} all-reduce(f32[2,1024]{1,0:T(2,128)S(1)} %slice.195), channel_id=1, replica_groups=mesh['dp'=8,'seq'=4] {'seq'}, use_global_device_ids=true, to_apply=%region_1.2 | all-reduce | flops 2048 | bytes 16384 | tf_op jit(solution)/shard_map/psum | solution.py:792
  184.1 18.9 %gate_backward.1 = (bf16[1024,768]{1,0:T(8,128)(2,1)}, bf16[1024,768]{1,0:T(8,128)(2,1)}, f32[1024,768]{1,0:T(8,128)}, f32[8,768]{1,0:T(8,128)}, bf16[8,384,768]{2,1,0:T(8,128)(2,1)}) custom-call(bf16[1024,1536]{1,0:T(8,128)(2,1)} %bitcast.195, bf16[1024,1536]{1,0:T(8,128)(2,1)} %bitcast.199, f32[1024,768]{1,0:T(8,128)} %get-tuple-element.63.y_ref, ...), custom_call_target="tpu_custom_call" | custom-call | tf_op jit(solution)/shard_map/gate_backward/pallas_call | solution.py:482
  203.4 30.8 %scan_backward.1 = (bf16[1024,768]{1,0:T(8,128)(2,1)}, f32[1024,128]{1,0:T(8,128)}, f32[256,1024]{1,0:T(8,128)}, f32[8,768]{1,0:T(8,128)}, f32[8,128]{1,0:T(8,128)}) custom-call(bf16[1024,768]{1,0:T(8,128)(2,1)} %fusion.8.x_ref.xp_ref, bf16[1024,768]{1,0:T(8,128)(2,1)} %fusion.8.x_ref.xp_ref, f32[1024,128]{1,0:T(8,128)} %broadcast_select_fusion.1.small_ref, ...), custom_call_target="tpu_custom_call" | custom-call | tf_op jit(solution)/shard_map/scan_backward/pallas_call | solution.py:316
  234.2 4.5 %convolution_convert_fusion.1 = bf16[1536,768]{1,0:T(8,128)(2,1)S(1)} fusion(bf16[1024,1536]{1,0:T(8,128)(2,1)S(1)} %bitcast.196, bf16[1024,768]{1,0:T(8,128)(2,1)} %get-tuple-element.71), kind=kOutput, calls=%fused_computation.3 | convolution fusion | flops 2417098752 | bytes 7077888 | tf_op jit(solution)/shard_map/dot_general | solution.py:21
  244.0 2.4 copy.123
  247.4 1.9 multiply_reduce_fusion.1
  249.3 2.8 convolution_convert_fusion
  254.8 4.9 %fusion.61 = f32[1024,1536]{1,0:T(8,128)} fusion(bf16[1024,768]{1,0:T(8,128)(2,1)S(1)} %copy-done.52, bf16[1536,768]{1,0:T(8,128)(2,1)S(1)} %bitcast.228), kind=kOutput, calls=%fused_computation.168 | convolution fusion | flops 2415919104 | bytes 10223616 | tf_op jit(solution)/shard_map/dot_general | solution.py:21
  261.0 1.9 copy.119
  269.5 2.1 fusion.52
  273.2 2.1 convolution_convert_fusion.2
  278.0 6.1 %collective-permute-done.19 = bf16[4,192,768]{2,1,0:T(8,128)(2,1)} collective-permute-done((bf16[4,192,768]{2,1,0:T(8,128)(2,1)}, bf16[4,192,768]{2,1,0:T(8,128)(2,1)}, u32[]{:S(2)}, u32[]{:S(2)}) %collective-permute-start.19) | collective-permute-done | bytes 1179680 | tf_op jit(solution)/shard_map/ppermute | solution.py:567
  284.1 2.6 fusion.3
  286.7 2.1 fusion
  293.2 6.9 %fusion.55 = (bf16[1024,1536]{1,0:T(8,128)(2,1)}, f32[1536]{0:T(1024)S(1)}) fusion(bf16[2,2,256,1536]{3,2,1,0:T(8,128)(2,1)S(1)} %copy-done.1, f32[1024,1536]{1,0:T(8,128)} %fusion.61, bf16[1024,896]{1,0:T(8,128)(2,1)S(1)} %pad_maximum_fusion, bf16[1536,896]{1,0:T(8,128)(2,1)S(1)} %copy-done.13), kind=kOutput, calls=%fused_computation.162 | convolution fusion | flops 2826435072 | bytes 17176576 | tf_op jit(solution)/shard_map/dot_general | solution.py:21
  303.5 4.4 %collective-permute-done.24 = f32[6500]{0:T(1024)S(1)} collective-permute-done((f32[6500]{0:T(1024)S(1)}, f32[6500]{0:T(1024)S(1)}, u32[]{:S(2)}, u32[]{:S(2)}) %collective-permute-start.24) | collective-permute-done | bytes 26032 | tf_op jit(solution)/shard_map/ppermute | solution.py:567
  310.3 2.1 collective-permute-done.25
  312.9 2.5 fusion.18
  315.3 5.4 %collective-permute-done.26 = bf16[192,896]{1,0:T(8,128)(2,1)S(1)} collective-permute-done((bf16[192,896]{1,0:T(8,128)(2,1)S(1)}, bf16[192,896]{1,0:T(8,128)(2,1)S(1)}, u32[]{:S(2)}, u32[]{:S(2)}) %collective-permute-start.26) | collective-permute-done | bytes 344096 | tf_op jit(solution)/shard_map/ppermute | solution.py:567
  322.3 3.2 collective-permute-done.29
  326.0 2.2 collective-permute-start.32
  334.4 3.1 collective-permute-start.37
  338.2 2.1 dynamic_update_slice.50
  340.3 2.2 dynamic_update_slice.51
  342.5 2.2 dynamic_update_slice.52
  344.7 24.0 %collective-permute-done.37 = bf16[96,1536]{1,0:T(8,128)(2,1)S(1)} collective-permute-done((bf16[96,1536]{1,0:T(8,128)(2,1)}, bf16[96,1536]{1,0:T(8,128)(2,1)S(1)}, u32[]{:S(2)}, u32[]{:S(2)}) %collective-permute-start.37) | collective-permute-done | bytes 294944 | tf_op jit(solution)/shard_map/ppermute | solution.py:855
  375.2 1.9 collective-permute-start.40
  377.1 2.7 collective-permute-done.39
  (325 shorter events, 109.6 us)
Async XLA Ops:
  7.2 9.6 %collective-permute-start = (s32[1,1,256]{2,1,0:T(1,128)}, s32[1,1,256]{2,1,0:T(1,128)S(1)}, u32[]{:S(2)}, u32[]{:S(2)}) collective-permute-start(s32[1,1,256]{2,1,0:T(1,128)} %bitcast.253), channel_id=1, source_target_pairs={{0,2},{1,3},{2,0},{3,1},{4,6},{5,7},{6,4},{7,5},{8,10},{9,11},{10,... | collective-permute-start | bytes 3080 | tf_op jit(solution)/shard_map/ppermute | solution.py:509
  12.5 13.6 %all-to-all-start = ((bf16[4,48,1664]{2,1,0:T(8,128)(2,1)}), bf16[4,48,1664]{2,1,0:T(8,128)(2,1)S(1)}, u32[]{:S(2)}, u32[]{:S(2)}) async-start(bf16[4,48,1664]{2,1,0:T(8,128)(2,1)} %copy.113), calls=%async_computation | async-start | bytes 1277952 | tf_op jit(solution)/shard_map/all_to_all | solution.py:718
  16.1 150.0 %all-gather.2.cloned.1.call-start = ((), (), s32[]{:S(2)}) async-start(), calls=%async_computation.3 | async-start | bytes 5308416 | tf_op jit(solution)/shard_map/all_gather | solution.py:737
  16.8 1.3 collective-permute-start.1
  26.2 20.4 %collective-permute-start.2 = (bf16[1,256,1536]{2,1,0:T(8,128)(2,1)S(1)}, bf16[1,256,1536]{2,1,0:T(8,128)(2,1)S(1)}, u32[]{:S(2)}, u32[]{:S(2)}) collective-permute-start(bf16[1,256,1536]{2,1,0:T(8,128)(2,1)S(1)} %bitcast.209), channel_id=1, source_target_pairs={{0,2},{1,3},{2,0},{3,1},{4,6},{5,7},{6,4},{7,5},{8,10},{9,11},{10,... | collective-permute-start | bytes 2359304 | tf_op jit(solution)/shard_map/ppermute | solution.py:509
  27.0 9.6 %collective-permute-start.6 = (bf16[192,896]{1,0:T(8,128)(2,1)S(1)}, bf16[192,896]{1,0:T(8,128)(2,1)}, u32[]{:S(2)}, u32[]{:S(2)}) collective-permute-start(bf16[192,896]{1,0:T(8,128)(2,1)S(1)} %get-tuple-element.124), channel_id=1, source_target_pairs={{0,4},{4,0},{8,12},{12,8},{16,20},{20,16},{24,28},{28,24},{1,5},{5... | collective-permute-start | bytes 1032200 | tf_op jit(solution)/shard_map/ppermute | solution.py:567
  28.6 33.8 %collective-permute-start.4 = (bf16[1,256,1536]{2,1,0:T(8,128)(2,1)S(1)}, bf16[1,256,1536]{2,1,0:T(8,128)(2,1)S(1)}, u32[]{:S(2)}, u32[]{:S(2)}) collective-permute-start(bf16[1,256,1536]{2,1,0:T(8,128)(2,1)S(1)} %copy-done.8), channel_id=1, source_target_pairs={{0,2},{1,3},{2,0},{3,1},{4,6},{5,7},{6,4},{7,5},{8,10},{9,11},{10,... | collective-permute-start | bytes 2359304 | tf_op jit(solution)/shard_map/ppermute | solution.py:509
  30.1 17.9 %collective-permute-start.7 = (bf16[192,896]{1,0:T(8,128)(2,1)S(1)}, bf16[192,896]{1,0:T(8,128)(2,1)S(1)}, u32[]{:S(2)}, u32[]{:S(2)}) collective-permute-start(bf16[192,896]{1,0:T(8,128)(2,1)S(1)} %get-tuple-element.124), channel_id=1, source_target_pairs={{0,8},{4,12},{8,16},{12,20},{16,24},{20,28},{1,9},{5,13},{9,17},{1... | collective-permute-start | bytes 1032200 | tf_op jit(solution)/shard_map/ppermute | solution.py:563
  33.6 14.4 %collective-permute-start.8 = (bf16[192,896]{1,0:T(8,128)(2,1)S(1)}, bf16[192,896]{1,0:T(8,128)(2,1)S(1)}, u32[]{:S(2)}, u32[]{:S(2)}) collective-permute-start(bf16[192,896]{1,0:T(8,128)(2,1)S(1)} %get-tuple-element.124), channel_id=1, source_target_pairs={{8,0},{12,4},{16,8},{20,12},{24,16},{28,20},{9,1},{13,5},{17,9},{2... | collective-permute-start | bytes 1032200 | tf_op jit(solution)/shard_map/ppermute | solution.py:563
  48.8 15.0 %collective-permute-start.9 = (bf16[192,896]{1,0:T(8,128)(2,1)S(1)}, bf16[192,896]{1,0:T(8,128)(2,1)S(1)}, u32[]{:S(2)}, u32[]{:S(2)}) collective-permute-start(bf16[192,896]{1,0:T(8,128)(2,1)S(1)} %get-tuple-element.112), channel_id=1, source_target_pairs={{0,4},{4,0},{8,12},{12,8},{16,20},{20,16},{24,28},{28,24},{1,5},{5... | collective-permute-start | bytes 1032200 | tf_op jit(solution)/shard_map/ppermute | solution.py:567
  49.3 14.5 %collective-permute-start.10 = (bf16[192,896]{1,0:T(8,128)(2,1)S(1)}, bf16[192,896]{1,0:T(8,128)(2,1)S(1)}, u32[]{:S(2)}, u32[]{:S(2)}) collective-permute-start(bf16[192,896]{1,0:T(8,128)(2,1)S(1)} %collective-permute-done.7), channel_id=1, source_target_pairs={{0,8},{4,12},{8,16},{12,20},{16,24},{20,28},{1,9},{5,13},{9,17},{1... | collective-permute-start | bytes 1032200 | tf_op jit(solution)/shard_map/ppermute | solution.py:563
  52.8 11.7 %collective-permute-start.11 = (bf16[192,896]{1,0:T(8,128)(2,1)S(1)}, bf16[192,896]{1,0:T(8,128)(2,1)}, u32[]{:S(2)}, u32[]{:S(2)}) collective-permute-start(bf16[192,896]{1,0:T(8,128)(2,1)S(1)} %collective-permute-done.8), channel_id=1, source_target_pairs={{8,0},{12,4},{16,8},{20,12},{24,16},{28,20},{9,1},{13,5},{17,9},{2... | collective-permute-start | bytes 1032200 | tf_op jit(solution)/shard_map/ppermute | solution.py:563
  54.2 15.0 %collective-permute-start.18 = (bf16[96,1536]{1,0:T(8,128)(2,1)S(1)}, bf16[96,1536]{1,0:T(8,128)(2,1)}, u32[]{:S(2)}, u32[]{:S(2)}) collective-permute-start(bf16[96,1536]{1,0:T(8,128)(2,1)S(1)} %convert_element_type.205), channel_id=1, source_target_pairs={{0,0},{1,4},{2,8},{3,12},{4,16},{5,20},{6,24},{7,28},{8,1},{9,5},{... | collective-permute-start | bytes 884744 | tf_op jit(solution)/shard_map/ppermute | solution.py:726
  73.8 247.7 %reduce-scatter.3.cloned.1.call-start = ((), (), s32[]{:S(2)}) async-start(), calls=%async_computation.4 | async-start | bytes 5308416 | tf_op jit(solution)/shard_map/reduce_scatter | solution.py:804
  75.1 57.0 %collective-permute-start.3 = (bf16[2,256,1536]{2,1,0:T(8,128)(2,1)}, bf16[2,256,1536]{2,1,0:T(8,128)(2,1)}, u32[]{:S(2)}, u32[]{:S(2)}) collective-permute-start(bf16[2,256,1536]{2,1,0:T(8,128)(2,1)} %maximum_select_fusion.2), channel_id=1, source_target_pairs={{0,1},{1,0},{2,3},{3,2},{4,5},{5,4},{6,7},{7,6},{8,9},{9,8},{10,11... | collective-permute-start | bytes 4718600 | tf_op jit(solution)/shard_map/ppermute | solution.py:509
  82.9 24.3 %collective-permute-start.13 = (bf16[192,896]{1,0:T(8,128)(2,1)S(1)}, bf16[192,896]{1,0:T(8,128)(2,1)}, u32[]{:S(2)}, u32[]{:S(2)}) collective-permute-start(bf16[192,896]{1,0:T(8,128)(2,1)S(1)} %collective-permute-done.10), channel_id=1, source_target_pairs={{0,8},{4,12},{8,16},{12,20},{16,24},{20,28},{1,9},{5,13},{9,17},{1... | collective-permute-start | bytes 1032200 | tf_op jit(solution)/shard_map/ppermute | solution.py:563
  84.9 24.1 %collective-permute-start.14 = (bf16[192,896]{1,0:T(8,128)(2,1)}, bf16[192,896]{1,0:T(8,128)(2,1)}, u32[]{:S(2)}, u32[]{:S(2)}) collective-permute-start(bf16[192,896]{1,0:T(8,128)(2,1)} %collective-permute-done.11), channel_id=1, source_target_pairs={{8,0},{12,4},{16,8},{20,12},{24,16},{28,20},{9,1},{13,5},{17,9},{2... | collective-permute-start | bytes 1032200 | tf_op jit(solution)/shard_map/ppermute | solution.py:563
  90.2 17.0 %collective-permute-start.12 = (bf16[192,896]{1,0:T(8,128)(2,1)}, bf16[192,896]{1,0:T(8,128)(2,1)}, u32[]{:S(2)}, u32[]{:S(2)}) collective-permute-start(bf16[192,896]{1,0:T(8,128)(2,1)} %get-tuple-element.110), channel_id=1, source_target_pairs={{0,4},{4,0},{8,12},{12,8},{16,20},{20,16},{24,28},{28,24},{1,5},{5... | collective-permute-start | bytes 1032200 | tf_op jit(solution)/shard_map/ppermute | solution.py:567
  107.1 29.7 %copy-start.33 = (f32[1024]{0:T(1024)}, f32[1024]{0:T(1024)S(1)}, u32[]{:S(2)}) copy-start(f32[1024]{0:T(1024)S(1)} %get-tuple-element.143) | copy-start | bytes 12292
  107.1 29.7 %copy-start.35 = (f32[1024]{0:T(1024)}, f32[1024]{0:T(1024)S(1)}, u32[]{:S(2)}) copy-start(f32[1024]{0:T(1024)S(1)} %get-tuple-element.144) | copy-start | bytes 12292
  107.1 34.4 %collective-permute-start.5 = (bf16[2,256,1536]{2,1,0:T(8,128)(2,1)}, bf16[2,256,1536]{2,1,0:T(8,128)(2,1)S(1)}, u32[]{:S(2)}, u32[]{:S(2)}) collective-permute-start(bf16[2,256,1536]{2,1,0:T(8,128)(2,1)} %maximum_select_fusion.4), channel_id=1, source_target_pairs={{0,1},{1,0},{2,3},{3,2},{4,5},{5,4},{6,7},{7,6},{8,9},{9,8},{10,11... | collective-permute-start | bytes 4718600 | tf_op jit(solution)/shard_map/ppermute | solution.py:509
  112.6 19.5 %collective-permute-start.15 = (bf16[192,896]{1,0:T(8,128)(2,1)S(1)}, bf16[192,896]{1,0:T(8,128)(2,1)S(1)}, u32[]{:S(2)}, u32[]{:S(2)}) collective-permute-start(bf16[192,896]{1,0:T(8,128)(2,1)S(1)} %get-tuple-element.108), channel_id=1, source_target_pairs={{0,4},{4,0},{8,12},{12,8},{16,20},{20,16},{24,28},{28,24},{1,5},{5... | collective-permute-start | bytes 1032200 | tf_op jit(solution)/shard_map/ppermute | solution.py:567
  137.9 5.8 %collective-permute-start.16 = (bf16[1,64,1024]{2,1,0:T(8,128)(2,1)S(1)}, bf16[1,64,1024]{2,1,0:T(8,128)(2,1)S(1)}, u32[]{:S(2)}, u32[]{:S(2)}) collective-permute-start(bf16[1,64,1024]{2,1,0:T(8,128)(2,1)S(1)} %bitcast.230), channel_id=1, source_target_pairs={{0,2},{1,3},{2,0},{3,1},{4,6},{5,7},{6,4},{7,5},{8,10},{9,11},{10,... | collective-permute-start | bytes 393224 | tf_op jit(solution)/shard_map/ppermute | solution.py:509
  143.7 1.6 collective-permute-start.17
  203.0 179.4 %reduce-scatter.5.cloned.1.call-start = ((), (), s32[]{:S(2)}) async-start(), calls=%async_computation.5 | async-start | bytes 3932160 | tf_op jit(solution)/shard_map/reduce_scatter | solution.py:848
  203.4 30.8 %copy-start.1 = (bf16[2,2,256,1536]{3,2,1,0:T(8,128)(2,1)S(1)}, bf16[2,2,256,1536]{3,2,1,0:T(8,128)(2,1)}, u32[]{:S(2)}) copy-start(bf16[2,2,256,1536]{3,2,1,0:T(8,128)(2,1)} %copy-done) | copy-start | bytes 9437188
  238.9 8.1 %collective-permute-start.20 = (bf16[64,1024]{1,0:T(8,128)(2,1)S(1)}, bf16[64,1024]{1,0:T(8,128)(2,1)S(1)}, u32[]{:S(2)}, u32[]{:S(2)}) collective-permute-start(bf16[64,1024]{1,0:T(8,128)(2,1)S(1)} %get-tuple-element.121), channel_id=1, source_target_pairs={{0,1},{1,0},{2,3},{3,2},{4,5},{5,4},{6,7},{7,6},{8,9},{9,8},{10,11... | collective-permute-start | bytes 393224 | tf_op jit(solution)/shard_map/ppermute | solution.py:676
  238.9 8.0 %collective-permute-start.21 = (bf16[64,1024]{1,0:T(8,128)(2,1)S(1)}, bf16[64,1024]{1,0:T(8,128)(2,1)S(1)}, u32[]{:S(2)}, u32[]{:S(2)}) collective-permute-start(bf16[64,1024]{1,0:T(8,128)(2,1)S(1)} %get-tuple-element.123), channel_id=1, source_target_pairs={{0,2},{1,3},{2,0},{3,1},{4,6},{5,7},{6,4},{7,5},{8,10},{9,11},{10,... | collective-permute-start | bytes 393224 | tf_op jit(solution)/shard_map/ppermute | solution.py:676
  240.7 6.4 %collective-permute-start.22 = (bf16[64,1024]{1,0:T(8,128)(2,1)S(1)}, bf16[64,1024]{1,0:T(8,128)(2,1)S(1)}, u32[]{:S(2)}, u32[]{:S(2)}) collective-permute-start(bf16[64,1024]{1,0:T(8,128)(2,1)S(1)} %get-tuple-element.122), channel_id=1, source_target_pairs={{0,3},{1,2},{2,1},{3,0},{4,7},{5,6},{6,5},{7,4},{8,11},{9,10},{10,... | collective-permute-start | bytes 393224 | tf_op jit(solution)/shard_map/ppermute | solution.py:676
  242.3 41.8 %collective-permute-start.19 = (bf16[4,192,768]{2,1,0:T(8,128)(2,1)}, bf16[4,192,768]{2,1,0:T(8,128)(2,1)}, u32[]{:S(2)}, u32[]{:S(2)}) collective-permute-start(bf16[4,192,768]{2,1,0:T(8,128)(2,1)} %dynamic-slice_bitcast_fusion), channel_id=1, source_target_pairs={{0,4},{4,0},{8,12},{12,8},{16,20},{20,16},{24,28},{28,24},{1,5},{5... | collective-permute-start | bytes 3538952 | tf_op jit(solution)/shard_map/ppermute | solution.py:567
  254.3 32.4 %collective-permute-start.27 = (bf16[2,256,1536]{2,1,0:T(8,128)(2,1)}, bf16[2,256,1536]{2,1,0:T(8,128)(2,1)}, u32[]{:S(2)}, u32[]{:S(2)}) collective-permute-start(bf16[2,256,1536]{2,1,0:T(8,128)(2,1)} %select_bitcast_fusion), channel_id=1, source_target_pairs={{0,1},{1,0},{2,3},{3,2},{4,5},{5,4},{6,7},{7,6},{8,9},{9,8},{10,11... | collective-permute-start | bytes 4718600 | tf_op jit(solution)/shard_map/ppermute | solution.py:509
  276.1 26.5 %collective-permute-start.23 = (bf16[4,192,128]{2,1,0:T(8,128)(2,1)}, bf16[4,192,128]{2,1,0:T(8,128)(2,1)}, u32[]{:S(2)}, u32[]{:S(2)}) collective-permute-start(bf16[4,192,128]{2,1,0:T(8,128)(2,1)} %dynamic-slice_bitcast_fusion.5), channel_id=1, source_target_pairs={{0,4},{4,0},{8,12},{12,8},{16,20},{20,16},{24,28},{28,24},{1,5},{5... | collective-permute-start | bytes 589832 | tf_op jit(solution)/shard_map/ppermute | solution.py:567
  291.5 21.3 %collective-permute-start.28 = (bf16[1,256,1536]{2,1,0:T(8,128)(2,1)}, bf16[1,256,1536]{2,1,0:T(8,128)(2,1)}, u32[]{:S(2)}, u32[]{:S(2)}) collective-permute-start(bf16[1,256,1536]{2,1,0:T(8,128)(2,1)} %fusion.19), channel_id=1, source_target_pairs={{0,2},{1,3},{2,0},{3,1},{4,6},{5,7},{6,4},{7,5},{8,10},{9,11},{10,... | collective-permute-start | bytes 2359304 | tf_op jit(solution)/shard_map/ppermute | solution.py:509
  301.0 6.9 %collective-permute-start.24 = (f32[6500]{0:T(1024)S(1)}, f32[6500]{0:T(1024)S(1)}, u32[]{:S(2)}, u32[]{:S(2)}) collective-permute-start(f32[6500]{0:T(1024)S(1)} %concatenate.167), channel_id=1, source_target_pairs={{0,16},{4,20},{8,24},{12,28},{16,0},{20,4},{24,8},{28,12},{1,17},{... | collective-permute-start | bytes 78008 | tf_op jit(solution)/shard_map/ppermute | solution.py:567
  307.9 4.5 %collective-permute-start.25 = (f32[6500]{0:T(1024)S(1)}, f32[6500]{0:T(1024)S(1)}, u32[]{:S(2)}, u32[]{:S(2)}) collective-permute-start(f32[6500]{0:T(1024)S(1)} %add.287), channel_id=1, source_target_pairs={{0,8},{4,12},{8,0},{12,4},{16,24},{20,28},{24,16},{28,20},{1,9},{5... | collective-permute-start | bytes 78008 | tf_op jit(solution)/shard_map/ppermute | solution.py:567
  312.5 8.2 %collective-permute-start.26 = (bf16[192,896]{1,0:T(8,128)(2,1)S(1)}, bf16[192,896]{1,0:T(8,128)(2,1)S(1)}, u32[]{:S(2)}, u32[]{:S(2)}) collective-permute-start(bf16[192,896]{1,0:T(8,128)(2,1)S(1)} %get-tuple-element.119), channel_id=1, source_target_pairs={{0,8},{4,12},{8,0},{12,4},{16,24},{20,28},{24,16},{28,20},{1,9},{5... | collective-permute-start | bytes 1032200 | tf_op jit(solution)/shard_map/ppermute | solution.py:567
  321.5 3.9 %collective-permute-start.29 = (f32[6500]{0:T(1024)S(1)}, f32[6500]{0:T(1024)S(1)}, u32[]{:S(2)}, u32[]{:S(2)}) collective-permute-start(f32[6500]{0:T(1024)S(1)} %add.288), channel_id=1, source_target_pairs={{0,4},{4,0},{8,12},{12,8},{16,20},{20,16},{24,28},{28,24},{1,5},{5... | collective-permute-start | bytes 78008 | tf_op jit(solution)/shard_map/ppermute | solution.py:567
  325.5 3.9 collective-permute-start.30
  326.0 43.6 %collective-permute-start.32 = (bf16[192,896]{1,0:T(8,128)(2,1)S(1)}, bf16[192,896]{1,0:T(8,128)(2,1)}, u32[]{:S(2)}, u32[]{:S(2)}) collective-permute-start(bf16[192,896]{1,0:T(8,128)(2,1)S(1)} %get-tuple-element.118), channel_id=1, source_target_pairs={{0,16},{4,20},{8,24},{12,28},{16,0},{20,4},{24,8},{28,12},{1,17},{... | collective-permute-start | bytes 1032200 | tf_op jit(solution)/shard_map/ppermute | solution.py:567
  328.2 41.4 %collective-permute-start.33 = (bf16[192,896]{1,0:T(8,128)(2,1)S(1)}, bf16[192,896]{1,0:T(8,128)(2,1)}, u32[]{:S(2)}, u32[]{:S(2)}) collective-permute-start(bf16[192,896]{1,0:T(8,128)(2,1)S(1)} %get-tuple-element.117), channel_id=1, source_target_pairs={{0,24},{4,28},{8,16},{12,20},{16,8},{20,12},{24,0},{28,4},{1,25},{... | collective-permute-start | bytes 1032200 | tf_op jit(solution)/shard_map/ppermute | solution.py:567
  329.5 2.0 collective-permute-start.31
  331.0 3.4 collective-permute-start.34
  332.0 8.3 %collective-permute-start.35 = (bf16[1,48,768]{2,0,1:T(2,128)(2,1)}, bf16[1,48,768]{2,0,1:T(2,128)(2,1)S(1)}, u32[]{:S(2)}, u32[]{:S(2)}) collective-permute-start(bf16[1,48,768]{2,0,1:T(2,128)(2,1)} %get-tuple-element.134), channel_id=1, source_target_pairs={{0,2},{1,3},{2,0},{3,1},{4,6},{5,7},{6,4},{7,5},{8,10},{9,11},{10,... | collective-permute-start | bytes 221192 | tf_op jit(solution)/shard_map/ppermute | solution.py:650
  332.9 9.6 %collective-permute-start.36 = (bf16[1,48,768]{2,0,1:T(2,128)(2,1)S(1)}, bf16[1,48,768]{2,0,1:T(2,128)(2,1)S(1)}, u32[]{:S(2)}, u32[]{:S(2)}) collective-permute-start(bf16[1,48,768]{2,0,1:T(2,128)(2,1)S(1)} %get-tuple-element.133), channel_id=1, source_target_pairs={{0,3},{1,2},{2,1},{3,0},{4,7},{5,6},{6,5},{7,4},{8,11},{9,10},{10,... | collective-permute-start | bytes 221192 | tf_op jit(solution)/shard_map/ppermute | solution.py:650
  334.4 34.3 %collective-permute-start.37 = (bf16[96,1536]{1,0:T(8,128)(2,1)}, bf16[96,1536]{1,0:T(8,128)(2,1)S(1)}, u32[]{:S(2)}, u32[]{:S(2)}) collective-permute-start(bf16[96,1536]{1,0:T(8,128)(2,1)} %bitcast.98), channel_id=1, source_target_pairs={{0,0},{4,1},{8,2},{12,3},{16,4},{20,5},{24,6},{28,7},{1,8},{5,9},{... | collective-permute-start | bytes 884744 | tf_op jit(solution)/shard_map/ppermute | solution.py:855
  371.0 3.3 collective-permute-start.38
  374.3 5.5 %collective-permute-start.39 = (bf16[1,48,896]{2,1,0:T(8,128)(2,1)S(1)}, bf16[1,48,896]{2,1,0:T(8,128)(2,1)S(1)}, u32[]{:S(2)}, u32[]{:S(2)}) collective-permute-start(bf16[1,48,896]{2,1,0:T(8,128)(2,1)S(1)} %get-tuple-element.131), channel_id=1, source_target_pairs={{0,2},{1,3},{2,0},{3,1},{4,6},{5,7},{6,4},{7,5},{8,10},{9,11},{10,... | collective-permute-start | bytes 258056 | tf_op jit(solution)/shard_map/ppermute | solution.py:650
  375.2 5.5 %collective-permute-start.40 = (bf16[1,48,896]{2,1,0:T(8,128)(2,1)S(1)}, bf16[1,48,896]{2,1,0:T(8,128)(2,1)S(1)}, u32[]{:S(2)}, u32[]{:S(2)}) collective-permute-start(bf16[1,48,896]{2,1,0:T(8,128)(2,1)S(1)} %get-tuple-element.130), channel_id=1, source_target_pairs={{0,3},{1,2},{2,1},{3,0},{4,7},{5,6},{6,5},{7,4},{8,11},{9,10},{10,... | collective-permute-start | bytes 258056 | tf_op jit(solution)/shard_map/ppermute | solution.py:650
  (54 other events, 295.2 us)
Sparse Core Ops, SparseCore 0:
  73.9 92.2 all-gather.1
  203.1 110.4 reduce-scatter.2
  321.7 41.1 reduce-scatter.4
where the time goes:
time: 398 us; the launch traced here: 393 us
  waiting for transfers between devices  91.6 us (23%)
  Pallas kernels  73.9 us (19%)
  starting transfers between devices  70.7 us (18%)
  local copies, waits for them, and re-layouts  63.1 us (16%)
  other arithmetic  46 us (12%)
  matrix products  26 us (7%)
  between operations  15.5 us (4%)
  blocking collectives  5.73 us (1%)
    ppermute x12, waiting for transfers between devices, crossed(): lax.ppermute(block, 'dp', [(i, i ^ bits) for i in range(lax.axis_size('dp...  34.3 us
    pallas_call x1, Pallas kernels, run_backward(): pl.pallas_call(functools.partial(scan_backward, q, taps, pairs, head, chu...  30.8 us
    dot_general x7, matrix products, mm(): return lax.dot_general(a, b, (dims, ((), ())), preferred_element_type=out)  26 us
    ppermute x1, waiting for transfers between devices, shards(): d_out_weight = lax.ppermute(out_part, ('dp', 'seq'), back).astype(f32)  24 us
    ppermute x12, starting transfers between devices, crossed(): lax.ppermute(block, 'dp', [(i, i ^ bits) for i in range(lax.axis_size('dp...  23.7 us
    pallas_call x1, Pallas kernels, run_gate_backward(): pl.pallas_call(functools.partial(gate_backward, blocks, tile, z_rows, tal...  18.9 us
    ppermute x12, starting transfers between devices, swapped(): return lax.ppermute(block, 'seq', [(i, i ^ bit) for i in range(size)])  14.6 us
    pallas_call x1, Pallas kernels, run_forward(): pl.pallas_call(functools.partial(scan_forward, q, taps, pairs, head), gri...  13.5 us
  transfers between devices with their start and end apart: 45, of which 19 were waited for; matrix products, arithmetic and copies ran while one was open for 31% of the time, Pallas kernels for 11%

commit v1 on v0

--- a/solution.py
+++ b/solution.py
@@ -383,60 +383,35 @@
 
 
 def gate_backward(
-    blocks, tile, z_rows, tall, channels,
-    normed_ref, cot_ref, y_ref, z_ref, dgn_ref, sums_ref, gain_ref,
-    gate_ref, dz_ref, dy_ref, dgain_ref, terms_ref,
+    channels,
+    y_ref, z_ref, dgn_ref, sums_ref, gain_ref,
+    gate_ref, dz_ref, dy_ref, dgain_ref,
 ):
-    step = pl.program_id(0)
     rows, width = y_ref.shape
-    parts = normed_ref.shape[1] // width
-
-    @pl.when(step == 0)
+
+    @pl.when(pl.program_id(0) == 0)
     def _():
         dgain_ref[...] = jnp.zeros_like(dgain_ref)
 
-    @pl.when(step < blocks)
-    def _():
-        own = pl.ds(pl.multiple_of(step * rows, rows), rows)
-        columns = jnp.concatenate([sums_ref[...], jnp.zeros((LANES - 8, rows), f32)], axis=0).T
-        inv = lax.rsqrt(columns[:, 0:1] / channels + epsilon)
-        slope = inv * inv * inv * (columns[:, 1:2] / channels)
-        for k in range(width // LANES):
-            lanes = slice(k * LANES, (k + 1) * LANES)
-            y, z, d_gn, gain = y_ref[:, lanes], z_ref[:, lanes], dgn_ref[:, lanes], gain_ref[:, lanes]
-            sig = sigmoid(z)
-            act = z * sig
-            gated = y * act
-            scaled = gated * inv
-            gate_ref[own, lanes] = (scaled * gain).astype(bf16)
-            dgain_ref[0:1, lanes] = dgain_ref[0:1, lanes] + jnp.sum(d_gn * scaled, axis=0, keepdims=True)
-            d_gated = inv * (d_gn * gain) - gated * slope
-            dz_ref[own, lanes] = (d_gated * y * (sig * (1.0 + z * (1.0 - sig)))).astype(bf16)
-            dy_ref[:, lanes] = d_gated * act
-
-    def store(term, at, within, base):
-        if within >= tile:
-            start = pl.multiple_of(base + at * tile, 16)
-            terms_ref[0, pl.ds(start, tile), :] = term
-        else:
-            for n in range(tile // within):
-                piece = term[n * within : (n + 1) * within]
-                terms_ref[at * (tile // within) + n, pl.ds(base, within), :] = piece
-
-    @pl.when(step >= blocks)
-    def _():
-        i = step - blocks
-        lanes = pl.ds(pl.multiple_of(i * tile, LANES), tile)
-        store(mm(normed_ref[:, lanes], dz_ref[...], TN).astype(bf16), i, z_rows, 0)
-        j = i // parts
-        lanes = pl.ds(pl.multiple_of(j * tile, LANES), tile)
-        left = gate_ref[:, lanes]
-        for k in range(parts):
-
-            @pl.when(i % parts == k)
-            def _():
-                right = cot_ref[:, k * width : (k + 1) * width]
-                store(mm(left, right, TN).astype(bf16), j, tall, z_rows + k * tall)
+    columns = jnp.concatenate([sums_ref[...], jnp.zeros((LANES - 8, rows), f32)], axis=0).T
+    inv = lax.rsqrt(columns[:, 0:1] / channels + epsilon)
+    slope = inv * inv * inv * (columns[:, 1:2] / channels)
+
+    def column(k, _):
+        lanes = pl.ds(pl.multiple_of(k * LANES, LANES), LANES)
+        y, z, d_gn, gain = y_ref[:, lanes], z_ref[:, lanes], dgn_ref[:, lanes], gain_ref[:, lanes]
+        sig = sigmoid(z)
+        act = z * sig
+        gated = y * act
+        scaled = gated * inv
+        gate_ref[:, lanes] = (scaled * gain).astype(bf16)
+        dgain_ref[0:1, lanes] = dgain_ref[0:1, lanes] + jnp.sum(d_gn * scaled, axis=0, keepdims=True)
+        d_gated = inv * (d_gn * gain) - gated * slope
+        dz_ref[:, lanes] = (d_gated * y * (sig * (1.0 + z * (1.0 - sig)))).astype(bf16)
+        dy_ref[:, lanes] = d_gated * act
+        return 0
+
+    lax.fori_loop(0, width // LANES, column, 0)
 
 
 def run_gate_forward(joined, z_rows, normed, cot, y, gain):
@@ -467,41 +442,23 @@
     )(normed, cot, joined, y, gain)
 
 
-def run_gate_backward(groups, z_rows, tall, channels, normed, cot, y, z, d_gn, sums, gain):
-    tokens, n_width = normed.shape
-    width = y.shape[1]
-    parts = n_width // width
+def run_gate_backward(channels, y, z, d_gn, sums, gain):
+    tokens, width = y.shape
     rows = min(256, tokens)
-    blocks = tokens // rows
-    tile = 3 * LANES
-    deep = z_rows + parts * tall
-
-    def tokens_of(columns):
-        return pl.BlockSpec((rows, columns), lambda c: (jnp.minimum(c, blocks - 1), 0))
-
+    part = pl.BlockSpec((rows, width), lambda c: (c, 0))
     return pl.pallas_call(
-        functools.partial(gate_backward, blocks, tile, z_rows, tall, channels),
-        grid=(blocks + n_width // tile,),
-        in_specs=[
-            whole(normed), whole(cot), tokens_of(width), tokens_of(width), tokens_of(width),
-            pl.BlockSpec((8, rows), lambda c: (0, jnp.minimum(c, blocks - 1))), whole(gain),
-        ],
-        out_specs=[
-            pl.BlockSpec((tokens, width), lambda c: (0, 0)),
-            pl.BlockSpec((tokens, width), lambda c: (0, 0)),
-            tokens_of(width),
-            pl.BlockSpec((8, width), lambda c: (0, 0)),
-            pl.BlockSpec((groups, deep, width), lambda c: (0, 0, 0)),
-        ],
+        functools.partial(gate_backward, channels),
+        grid=(tokens // rows,),
+        in_specs=[part, part, part, pl.BlockSpec((8, rows), lambda c: (0, c)), whole(gain)],
+        out_specs=[part, part, part, pl.BlockSpec((8, width), lambda c: (0, 0))],
         out_shape=[
             jax.ShapeDtypeStruct((tokens, width), bf16),
             jax.ShapeDtypeStruct((tokens, width), bf16),
             jax.ShapeDtypeStruct((tokens, width), f32),
             jax.ShapeDtypeStruct((8, width), f32),
-            jax.ShapeDtypeStruct((groups, deep, width), bf16),
         ],
         name="gate_backward",
-    )(normed, cot, y, z, d_gn, sums, gain)
+    )(y, z, d_gn, sums, gain)
 
 
 def swapped(block, bit):
@@ -709,10 +666,20 @@
     in_rows = in_weight.shape[0]
 
     in_low = in_weight.astype(bf16)
-    z_cols = in_low[:, :n_inner].reshape(in_rows, size, own_inner)
-    x_cols = in_low[:, n_inner : 2 * n_inner].reshape(in_rows, size, own_inner)
+    runs = 2 if groups % 2 == 0 else 1
+
+    def dealt(columns):
+        cut = columns.reshape(columns.shape[0], runs, size, -1)
+        return cut.transpose(0, 2, 1, 3).reshape(columns.shape[0], size, -1)
+
+    def undealt(columns):
+        cut = columns.reshape(columns.shape[0], size, runs, -1)
+        return cut.transpose(0, 2, 1, 3).reshape(columns.shape[0], -1)
+
+    z_cols = dealt(in_low[:, :n_inner])
+    x_cols = dealt(in_low[:, n_inner : 2 * n_inner])
     bc_cols = in_low[:, 2 * n_inner : n_inner + n_mixed].reshape(in_rows, size, own_bc)
-    dt_cols = in_low[:, n_inner + n_mixed :].reshape(in_rows, size, own_heads)
+    dt_cols = dealt(in_low[:, n_inner + n_mixed :])
     gap = jnp.zeros((in_rows, size, LANES - own_heads - own_bc), bf16)
     laid = jnp.concatenate([x_cols, dt_cols, gap, bc_cols, z_cols], axis=2).transpose(1, 0, 2)
     mine = lax.all_to_all(laid, "seq", 0, 0, tiled=True)
@@ -721,20 +688,24 @@
     unit = flat * inv
     normed_own = (unit * norm_gain).astype(bf16)
     docs = gathered(segments).reshape(tokens).astype(f32)
-    order = [(f, (f % groups) * size + f // groups) for f in range(groups * size)]
+    half = groups // runs
+    order = []
+    for f in range(groups * size):
+        run, owner, spot = f // (half * size), f // half % size, f % half
+        order.append((f, (run * half + spot) * size + owner))
     back = [(b, a) for a, b in order]
     out_moved = lax.ppermute(out_weight.astype(bf16), ("dp", "seq"), order)
-    mine, normed_own = lax.optimization_barrier((after(mine, docs), normed_own))
+    mine, normed_own = lax.optimization_barrier((after(mine, (docs, out_moved)), normed_own))
     mine = mine.reshape(size * in_rows, -1)
     n_first = own_inner + LANES
     cot_own = cotangent.reshape(block, n_width)
     normed_held = opened(normed_own)
     cot_held = opened(after(cot_own, mine))
     w_first, hopped = gathered_rows(mine[:, :n_first], [normed_held, cot_held])
-    z_block = jnp.concatenate([mine[:, n_first:], folded(after(out_moved, hopped), 1, own_inner)], axis=0)
+    z_block = jnp.concatenate([mine[:, n_first:], folded(out_moved, 1, own_inner)], axis=0)
 
     normed = gathered(normed_own, normed_held)
-    joined = lax.all_gather(z_block, "dp", axis=0, tiled=True).reshape(groups, -1, own_inner)
+    joined = lax.all_gather(after(z_block, hopped), "dp", axis=0, tiled=True).reshape(groups, -1, own_inner)
     z_rows = size * in_rows
     w_z = joined[:, :z_rows].reshape(-1, own_inner)
     w_out = unfolded(joined[:, z_rows:], n_width)
@@ -745,17 +716,20 @@
     def own_part(vector, parts):
         return lax.dynamic_slice_in_dim(vector, index * parts, parts, vector.ndim - 1)
 
+    def own_heads_of(vector):
+        return lax.dynamic_index_in_dim(dealt(vector), index, 1, keepdims=False)
+
     w_x, w_small = w_first[:, :own_inner], w_first[:, own_inner:]
     small = mm(normed, w_small, NN)
     x_in = mm(normed, w_x, NN).astype(bf16)
-    conv_x = own_part(conv_weight[:, :n_inner], own_inner)
-    bias_x = own_part(conv_bias[None, :n_inner], own_inner)
+    conv_x = own_heads_of(conv_weight[:, :n_inner])
+    bias_x = own_heads_of(conv_bias[None, :n_inner])
     conv_bc = own_part(conv_weight[:, n_inner:], own_bc)
     bias_bc = own_part(conv_bias[None, n_inner:], own_bc)
-    sb = padded(own_part(step_bias[None], own_heads), LANES)
-    rate = padded(jnp.exp(own_part(log_rate[None], own_heads)), LANES)
-    skip = jnp.repeat(own_part(skip_gain[None], own_heads), head, axis=1)
-    gain = own_part(gate_gain[None], own_inner)
+    sb = padded(own_heads_of(step_bias[None]), LANES)
+    rate = padded(jnp.exp(own_heads_of(log_rate[None])), LANES)
+    skip = jnp.repeat(own_heads_of(skip_gain[None]), head, axis=1)
+    gain = own_heads_of(gate_gain[None])
 
     head_lanes = jnp.arange(LANES) < own_heads
     bc_in = small[:, LANES - own_bc :].astype(bf16).astype(f32)
@@ -791,16 +765,14 @@
     z, d_gn, sums = run_gate_forward(gate_in, deep, normed, cot, y, gain)
     sums = lax.psum(sums[:2], "seq")
     sums = jnp.pad(sums, ((0, 6), (0, 0)))
-    gate_low, d_z, d_y, d_gain, terms = run_gate_backward(
-        lead, deep, tall, n_inner, normed, cot, y, z, d_gn, sums, gain
-    )
+    gate_low, d_z, d_y, d_gain = run_gate_backward(n_inner, y, z, d_gn, sums, gain)
     d_gain = d_gain[0]
-    if not tiled:
-        z_term = terms[0, :deep].reshape(groups, z_rows, own_inner)
-        out_term = terms[0, deep:].reshape(n_width // own_inner, groups, out_rows, own_inner)
-        out_term = out_term.transpose(1, 0, 2, 3).reshape(groups, -1, own_inner)
-        terms = jnp.concatenate([z_term, out_term], axis=1)
-    terms = terms.reshape(-1, own_inner)
+    terms = [mm(normed, d_z, TN)]
+    for k in range(0, n_width, own_inner):
+        terms.append(mm(gate_low, cot[:, k : k + own_inner], TN))
+    terms = [term.astype(bf16).reshape(groups, -1, own_inner) for term in terms]
+    terms = jnp.concatenate(terms, axis=1).reshape(-1, own_inner)
+    terms, d_y = lax.optimization_barrier((terms, d_y))
     parts = lax.psum_scatter(terms, "dp", scatter_dimension=0, tiled=True)
 
     d_x, d_dt, d_bct, d_conv_x, d_heads = run_backward(
@@ -823,6 +795,7 @@
     small_lines = halved_rows(mm(normed, d_small, TN).astype(bf16))
     branch = scattered(mm(after(gate_low, d_bc), w_out, NN).astype(bf16))
     result = (flat + branch).reshape(n_seqs, block, n_width).astype(bf16)
+    x_shares = shared_rows(x_lines)
     d_first = after(d_first, x_lines)
     d_normed = mm(d_first, w_first, NT) + mm(d_z, w_z, NT)
     d_norm_gain = jnp.sum(d_normed * normed.astype(f32), axis=0) / norm_gain
@@ -839,11 +812,11 @@
         ]
     )
     lines = jnp.concatenate([x_lines, small_lines], axis=-1)
-    packed = added_over(packed, reversed(bits_of(groups)[1:]))
-    lines, packed = lax.optimization_barrier((lines, packed))
-    shares = shared_rows(lines)
-    packed = gathered(added_over(packed, bits_of(groups)[:1])[None])
-    parts, result = lax.optimization_barrier((after(parts, shares[:2]), result))
+    packed = added_over(after(packed, x_shares[:2]), reversed(bits_of(groups)[1:]))
+    parts, result = lax.optimization_barrier((after(parts, x_shares[:2]), result))
+    packed = added_over(after(packed, (x_shares[:3], parts)), bits_of(groups)[:1])
+    packed = gathered(after(packed, x_shares)[None])
+    small_shares = shared_rows(small_lines)
     d_norm = after(d_normed.astype(bf16), parts)
     d_norm = lax.psum_scatter(d_norm, "seq", scatter_dimension=0, tiled=True).astype(f32)
 
@@ -854,15 +827,16 @@
     out_part = unfolded(parts[None, z_rows:], n_width)
     d_out_weight = lax.ppermute(out_part, ("dp", "seq"), back).astype(f32)
     in_z = own_rows(parts[:z_rows])
-    shares, in_z, d_out_weight = lax.optimization_barrier((shares, in_z, d_out_weight))
-    first_part = sum(share.astype(f32) for share in shares)
+    x_shares, in_z, d_out_weight = lax.optimization_barrier((x_shares, in_z, d_out_weight))
+    first_part = [sum(piece.astype(f32) for piece in own) for own in (x_shares, small_shares)]
+    first_part = jnp.concatenate(first_part, axis=1)
     in_first = own_rows(first_part.astype(bf16))
     d_in_weight = jnp.concatenate(
         [
-            in_z.reshape(in_rows, n_inner),
-            in_first[:, :, :own_inner].reshape(in_rows, n_inner),
+            undealt(in_z),
+            undealt(in_first[:, :, :own_inner]),
             in_first[:, :, n_first - own_bc :].reshape(in_rows, 2 * n_state),
-            in_first[:, :, own_inner : own_inner + own_heads].reshape(in_rows, n_heads),
+            undealt(in_first[:, :, own_inner : own_inner + own_heads]),
         ],
         axis=1,
     )
@@ -882,13 +856,13 @@
 
     got_x = take((n_taps + 1) * own_inner).reshape(size, n_taps + 1, own_inner)
     got_bc = take((n_taps + 1) * own_bc).reshape(size, n_taps + 1, own_bc)
-    got_x = got_x.transpose(1, 0, 2).reshape(n_taps + 1, n_inner)
+    got_x = undealt(got_x.transpose(1, 0, 2))
     got_bc = got_bc.transpose(1, 0, 2).reshape(n_taps + 1, 2 * n_state)
     conv_all = jnp.concatenate([got_x, got_bc], axis=1)
-    d_gate_gain = take(own_inner).reshape(n_inner)
-    d_step_bias = take(own_heads).reshape(n_heads)
-    d_log_rate = take(own_heads).reshape(n_heads)
-    d_skip_gain = take(own_heads).reshape(n_heads)
+    d_gate_gain = undealt(take(own_inner)[None])[0]
+    d_step_bias = undealt(take(own_heads)[None])[0]
+    d_log_rate = undealt(take(own_heads)[None])[0]
+    d_skip_gain = undealt(take(own_heads)[None])[0]
     d_norm_all = jnp.sum(take(n_width), axis=0)
     return (
         result,

time: 398 us -> 407 us (1.023)
  the two profiles are of different devices: /device:TPU:2 before, /device:TPU:0 now
where the time goes in v1:
time: 407 us; the launch traced here: 400 us
  waiting for transfers between devices  82.5 us (20%)
  local copies, waits for them, and re-layouts  80.2 us (20%)
  starting transfers between devices  64.2 us (16%)
  Pallas kernels  64.1 us (16%)
  other arithmetic  49.2 us (12%)
  matrix products  36.6 us (9%)
  between operations  15.4 us (4%)
  blocking collectives  7.71 us (2%)
    ppermute x15, waiting for transfers between devices, crossed(): lax.ppermute(block, 'dp', [(i, i ^ bits) for i in range(lax.axis_size('dp...  53.9 us
    dot_general x10, matrix products, mm(): return lax.dot_general(a, b, (dims, ((), ())), preferred_element_type=out)  36.6 us
    pallas_call x1, Pallas kernels, run_backward(): pl.pallas_call(functools.partial(scan_backward, q, taps, pairs, head, chu...  30.7 us
    ppermute x15, starting transfers between devices, crossed(): lax.ppermute(block, 'dp', [(i, i ^ bits) for i in range(lax.axis_size('dp...  20.6 us
    ppermute x6, starting transfers between devices, moved_by(): return lax.ppermute(block, 'dp', route)  18.4 us
    pallas_call x1, Pallas kernels, run_forward(): pl.pallas_call(functools.partial(scan_forward, q, taps, pairs, head), gri...  13.4 us
    ppermute x12, starting transfers between devices, swapped(): return lax.ppermute(block, 'seq', [(i, i ^ bit) for i in range(size)])  12 us
    pallas_call x1, Pallas kernels, run_gate_forward(): pl.pallas_call(functools.partial(gate_forward, groups, z_rows, tall), gri...  10.9 us
  transfers between devices with their start and end apart: 48, of which 19 were waited for; matrix products, arithmetic and copies ran while one was open for 37% of the time, Pallas kernels for 11%

profile of v1, /device:TPU:0, one launch (start us, length us, event | category | flops | bytes accessed | tf_op | source)
XLA Modules:
  0.0 399.9 jit_solution(5295849871121162920)
XLA Ops:
  7.2 3.1 collective-permute-start
  14.4 3.5 all-to-all-start
  20.3 2.9 collective-permute-start.1
  24.0 8.2 %all-to-all-done = bf16[4,48,1664]{2,1,0:T(8,128)(2,1)S(1)} async-done(((bf16[4,48,1664]{2,1,0:T(8,128)(2,1)}), bf16[4,48,1664]{2,1,0:T(8,128)(2,1)S(1)}, u32[]{:S(2)}, u32[]{:S(2)}) %all-to-all-start) | async-done | bytes 639008 | tf_op jit(solution)/shard_map/all_to_all | solution.py:685
  32.2 2.4 collective-permute-start.3
  40.0 5.8 %collective-permute-start.6 = (bf16[192,896]{1,0:T(8,128)(2,1)}, bf16[192,896]{1,0:T(8,128)(2,1)}, u32[]{:S(2)}, u32[]{:S(2)}) collective-permute-start(bf16[192,896]{1,0:T(8,128)(2,1)} %get-tuple-element.128), channel_id=1, source_target_pairs={{0,8},{4,12},{8,16},{12,20},{16,24},{20,28},{1,9},{5,13},{9,17},{1... | collective-permute-start | bytes 1032200 | tf_op jit(solution)/shard_map/ppermute | solution.py:520
  49.9 3.1 collective-permute-done.3
  54.4 2.0 collective-permute-done.7
  57.7 5.3 %collective-permute-start.9 = (bf16[192,896]{1,0:T(8,128)(2,1)}, bf16[192,896]{1,0:T(8,128)(2,1)}, u32[]{:S(2)}, u32[]{:S(2)}) collective-permute-start(bf16[192,896]{1,0:T(8,128)(2,1)} %collective-permute-done.6), channel_id=1, source_target_pairs={{0,8},{4,12},{8,16},{12,20},{16,24},{20,28},{1,9},{5,13},{9,17},{1... | collective-permute-start | bytes 1032200 | tf_op jit(solution)/shard_map/ppermute | solution.py:520
  66.5 2.7 collective-permute-done.11
  70.5 2.0 collective-permute-done.8
  93.5 3.3 collective-permute-start.13
  100.0 2.0 constant_dynamic-update-slice_fusion.9
  117.1 2.5 collective-permute-start.15
  120.1 15.3 %collective-permute-done.15 = bf16[192,896]{1,0:T(8,128)(2,1)S(1)} collective-permute-done((bf16[192,896]{1,0:T(8,128)(2,1)S(1)}, bf16[192,896]{1,0:T(8,128)(2,1)S(1)}, u32[]{:S(2)}, u32[]{:S(2)}) %collective-permute-start.15) | collective-permute-done | bytes 344096 | tf_op jit(solution)/shard_map/ppermute | solution.py:524
  136.1 2.4 maximum_select_fusion
  138.8 2.6 fusion.30
  142.5 5.3 %fusion.8.x_ref.xp_ref = bf16[1024,768]{1,0:T(8,128)(2,1)} fusion(bf16[1024,1536]{1,0:T(8,128)(2,1)S(1)} %bitcast.257, bf16[1536,896]{1,0:T(8,128)(2,1)} %constant_dynamic-update-slice_fusion.6), kind=kOutput, calls=%fused_computation.23 | convolution fusion | flops 2416705536 | bytes 7077888 | tf_op jit(solution)/shard_map/dot_general | solution.py:21
  154.0 13.4 %scan_forward.1 = (f32[1024,768]{1,0:T(8,128)}, f32[8,128,768]{2,1,0:T(8,128)}) custom-call(bf16[1024,768]{1,0:T(8,128)(2,1)} %fusion.8.x_ref.xp_ref, f32[1024,128]{1,0:T(8,128)} %broadcast_select_fusion.1.small_ref, bf16[256,1024]{1,0:T(8,128)(2,1)} %bitcast.276, f32[1024,128]{1,0:T(8,128)} %broadcast_in_dim.73.dcol_ref.dcolp_ref, ...), custom_call_target="tpu_custom_call" | custom-call | tf_op jit(solution)/shard_map/scan_forward/pallas_call | solution.py:271
  167.5 10.9 %gate_forward.1 = (f32[1024,768]{1,0:T(8,128)}, f32[1024,768]{1,0:T(8,128)}, f32[8,1024]{1,0:T(8,128)}) custom-call(bf16[1024,1536]{1,0:T(8,128)(2,1)} %bitcast.258, bf16[1024,1536]{1,0:T(8,128)(2,1)} %bitcast.267, bf16[8,384,768]{2,1,0:T(8,128)(2,1)} %bitcast.263, f32[1024,768]{1,0:T(8,128)} %get-tuple-element.65.y_ref, f32[1,768]{1,0:T(1,128)} %fusion.65.gain_ref), custom_call_target="tpu_custom_call" | custom-call | tf_op jit(solution)/shard_map/gate_forward/pallas_call | solution.py:427
  179.1 7.7 %psum.7 = f32[2,1024]{1,0:T(2,128)S(1)} all-reduce(f32[2,1024]{1,0:T(2,128)S(1)} %slice.201), channel_id=1, replica_groups=mesh['dp'=8,'seq'=4] {'seq'}, use_global_device_ids=true, to_apply=%region_1.2 | all-reduce | flops 2048 | bytes 16384 | tf_op jit(solution)/shard_map/psum | solution.py:766
  187.4 9.1 %gate_backward.1 = (bf16[1024,768]{1,0:T(8,128)(2,1)}, bf16[1024,768]{1,0:T(8,128)(2,1)}, f32[1024,768]{1,0:T(8,128)}, f32[8,768]{1,0:T(8,128)}) custom-call(f32[1024,768]{1,0:T(8,128)} %get-tuple-element.65.y_ref, f32[1024,768]{1,0:T(8,128)} %get-tuple-element.67.z_ref, f32[1024,768]{1,0:T(8,128)} %get-tuple-element.68.dgn_ref, f32[8,1024]{1,0:T(8,128)} %pad.58.sums_ref, ...), custom_call_target="tpu_custom_call" | custom-call | tf_op jit(solution)/shard_map/gate_backward/pallas_call | solution.py:449
  196.6 3.0 fusion.23
  202.0 2.9 convolution_convert_fusion.2
  204.9 2.3 pad_maximum_fusion
  207.4 30.7 %scan_backward.1 = (bf16[1024,768]{1,0:T(8,128)(2,1)}, f32[1024,128]{1,0:T(8,128)}, f32[256,1024]{1,0:T(8,128)}, f32[8,768]{1,0:T(8,128)}, f32[8,128]{1,0:T(8,128)}) custom-call(bf16[1024,768]{1,0:T(8,128)(2,1)} %fusion.8.x_ref.xp_ref, bf16[1024,768]{1,0:T(8,128)(2,1)} %fusion.8.x_ref.xp_ref, f32[1024,128]{1,0:T(8,128)} %broadcast_select_fusion.1.small_ref, ...), custom_call_target="tpu_custom_call" | custom-call | tf_op jit(solution)/shard_map/scan_backward/pallas_call | solution.py:316
  238.1 5.5 %convolution_convert_fusion.1 = bf16[1536,768]{1,0:T(8,128)(2,1)} fusion(bf16[1024,1536]{1,0:T(8,128)(2,1)S(1)} %bitcast.260, bf16[1024,768]{1,0:T(8,128)(2,1)} %get-tuple-element.76), kind=kOutput, calls=%fused_computation.4 | convolution fusion | flops 2417098752 | bytes 7077888 | tf_op jit(solution)/shard_map/dot_general | solution.py:21
  250.1 2.4 dynamic-slice_bitcast_fusion
  254.1 2.8 fusion.75
  256.9 4.7 %fusion.80 = f32[1024,1536]{1,0:T(8,128)} fusion(bf16[1024,768]{1,0:T(8,128)(2,1)S(1)} %copy-done.47, bf16[1536,768]{1,0:T(8,128)(2,1)S(1)} %bitcast.289), kind=kOutput, calls=%fused_computation.200 | convolution fusion | flops 2415919104 | bytes 10223616 | tf_op jit(solution)/shard_map/dot_general | solution.py:21
  262.9 2.4 copy.85
  266.8 2.1 multiply_reduce_fusion.1
  268.8 3.2 convolution_convert_fusion
  286.8 10.4 %collective-permute-done.37 = bf16[4,192,128]{2,1,0:T(8,128)(2,1)} collective-permute-done((bf16[4,192,128]{2,1,0:T(8,128)(2,1)}, bf16[4,192,128]{2,1,0:T(8,128)(2,1)}, u32[]{:S(2)}, u32[]{:S(2)}) %collective-permute-start.37) | collective-permute-done | bytes 196640 | tf_op jit(solution)/shard_map/ppermute | solution.py:524
  303.6 2.0 fusion
  309.4 6.8 %multiply_reduce_fusion = (f32[1536]{0:T(1024)S(1)}, bf16[1024,1536]{1,0:T(8,128)(2,1)}) fusion(bf16[2,2,256,1536]{3,2,1,0:T(8,128)(2,1)S(1)} %copy-done.1, f32[1024,1536]{1,0:T(8,128)S(1)} %bitcast.347, bf16[1024,896]{1,0:T(8,128)(2,1)S(1)} %pad_maximum_fusion.1, bf16[1536,896]{1,0:T(8,128)(2,1)} %constant_dynamic-update-slice_fusion.6), kind=kOutput, calls=%fused_computation | convolution fusion | flops 2826435072 | bytes 17176576 | tf_op jit(solution)/shard_map/dot_general | solution.py:21
  316.3 7.1 %collective-permute-done.20 = bf16[192,768]{1,0:T(8,128)(2,1)} collective-permute-done((bf16[192,768]{1,0:T(8,128)(2,1)}, bf16[192,768]{1,0:T(8,128)(2,1)}, u32[]{:S(2)}, u32[]{:S(2)}) %collective-permute-start.20) | collective-permute-done | bytes 294944 | tf_op jit(solution)/shard_map/ppermute | solution.py:524
  324.8 2.5 collective-permute-start.38
  327.4 2.4 collective-permute-start.40
  330.8 2.4 collective-permute-start.30
  333.2 3.7 fusion.18
  337.1 9.5 %collective-permute-done.39 = bf16[192,128]{1,0:T(8,128)(2,1)S(1)} collective-permute-done((bf16[192,128]{1,0:T(8,128)(2,1)S(1)}, bf16[192,128]{1,0:T(8,128)(2,1)S(1)}, u32[]{:S(2)}, u32[]{:S(2)}) %collective-permute-start.39) | collective-permute-done | bytes 49184 | tf_op jit(solution)/shard_map/ppermute | solution.py:524
  347.4 6.5 %collective-permute-done.28 = bf16[192,768]{1,0:T(8,128)(2,1)S(1)} collective-permute-done((bf16[192,768]{1,0:T(8,128)(2,1)}, bf16[192,768]{1,0:T(8,128)(2,1)S(1)}, u32[]{:S(2)}, u32[]{:S(2)}) %collective-permute-start.28) | collective-permute-done | bytes 294944 | tf_op jit(solution)/shard_map/ppermute | solution.py:524
  355.4 2.4 collective-permute-done.29
  363.4 3.4 collective-permute-start.34
  372.2 2.3 collective-permute-done.34
  374.6 3.1 collective-permute-done.35
  380.0 2.6 collective-permute-start.42
  (361 shorter events, 139.8 us)
Async XLA Ops:
  7.2 13.1 %collective-permute-start = (s32[1,1,256]{2,1,0:T(1,128)}, s32[1,1,256]{2,1,0:T(1,128)S(1)}, u32[]{:S(2)}, u32[]{:S(2)}) collective-permute-start(s32[1,1,256]{2,1,0:T(1,128)} %bitcast.336), channel_id=1, source_target_pairs={{0,2},{1,3},{2,0},{3,1},{4,6},{5,7},{6,4},{7,5},{8,10},{9,11},{10,... | collective-permute-start | bytes 3080 | tf_op jit(solution)/shard_map/ppermute | solution.py:466
  14.4 17.8 %all-to-all-start = ((bf16[4,48,1664]{2,1,0:T(8,128)(2,1)}), bf16[4,48,1664]{2,1,0:T(8,128)(2,1)S(1)}, u32[]{:S(2)}, u32[]{:S(2)}) async-start(bf16[4,48,1664]{2,1,0:T(8,128)(2,1)} %bitcast.4), calls=%async_computation | async-start | bytes 1277952 | tf_op jit(solution)/shard_map/all_to_all | solution.py:685
  17.9 149.6 %all-gather.2.cloned.1.call-start = ((), (), s32[]{:S(2)}) async-start(), calls=%async_computation.3 | async-start | bytes 5308416 | tf_op jit(solution)/shard_map/all_gather | solution.py:708
  19.0 5.0 %collective-permute-start.2 = (bf16[96,1536]{1,0:T(8,128)(2,1)S(1)}, bf16[96,1536]{1,0:T(8,128)(2,1)S(1)}, u32[]{:S(2)}, u32[]{:S(2)}) collective-permute-start(bf16[96,1536]{1,0:T(8,128)(2,1)S(1)} %convert_element_type.222), channel_id=1, source_target_pairs={{0,0},{1,4},{2,8},{3,12},{4,1},{5,5},{6,9},{7,13},{8,2},{9,6},{10,... | collective-permute-start | bytes 884744 | tf_op jit(solution)/shard_map/ppermute | solution.py:697
  20.3 3.7 collective-permute-start.1
  32.2 20.8 %collective-permute-start.3 = (bf16[1,256,1536]{2,1,0:T(8,128)(2,1)S(1)}, bf16[1,256,1536]{2,1,0:T(8,128)(2,1)S(1)}, u32[]{:S(2)}, u32[]{:S(2)}) collective-permute-start(bf16[1,256,1536]{2,1,0:T(8,128)(2,1)S(1)} %bitcast.273), channel_id=1, source_target_pairs={{0,2},{1,3},{2,0},{3,1},{4,6},{5,7},{6,4},{7,5},{8,10},{9,11},{10,... | collective-permute-start | bytes 2359304 | tf_op jit(solution)/shard_map/ppermute | solution.py:466
  37.4 10.7 %collective-permute-start.5 = (bf16[192,896]{1,0:T(8,128)(2,1)}, bf16[192,896]{1,0:T(8,128)(2,1)}, u32[]{:S(2)}, u32[]{:S(2)}) collective-permute-start(bf16[192,896]{1,0:T(8,128)(2,1)} %get-tuple-element.128), channel_id=1, source_target_pairs={{0,4},{4,0},{8,12},{12,8},{16,20},{20,16},{24,28},{28,24},{1,5},{5... | collective-permute-start | bytes 1032200 | tf_op jit(solution)/shard_map/ppermute | solution.py:524
  38.9 30.2 %collective-permute-start.11 = (bf16[1,256,1536]{2,1,0:T(8,128)(2,1)S(1)}, bf16[1,256,1536]{2,1,0:T(8,128)(2,1)S(1)}, u32[]{:S(2)}, u32[]{:S(2)}) collective-permute-start(bf16[1,256,1536]{2,1,0:T(8,128)(2,1)S(1)} %copy-done.9), channel_id=1, source_target_pairs={{0,2},{1,3},{2,0},{3,1},{4,6},{5,7},{6,4},{7,5},{8,10},{9,11},{10,... | collective-permute-start | bytes 2359304 | tf_op jit(solution)/shard_map/ppermute | solution.py:466
  40.0 14.4 %collective-permute-start.6 = (bf16[192,896]{1,0:T(8,128)(2,1)}, bf16[192,896]{1,0:T(8,128)(2,1)}, u32[]{:S(2)}, u32[]{:S(2)}) collective-permute-start(bf16[192,896]{1,0:T(8,128)(2,1)} %get-tuple-element.128), channel_id=1, source_target_pairs={{0,8},{4,12},{8,16},{12,20},{16,24},{20,28},{1,9},{5,13},{9,17},{1... | collective-permute-start | bytes 1032200 | tf_op jit(solution)/shard_map/ppermute | solution.py:520
  45.9 10.6 %collective-permute-start.7 = (bf16[192,896]{1,0:T(8,128)(2,1)}, bf16[192,896]{1,0:T(8,128)(2,1)}, u32[]{:S(2)}, u32[]{:S(2)}) collective-permute-start(bf16[192,896]{1,0:T(8,128)(2,1)} %get-tuple-element.128), channel_id=1, source_target_pairs={{8,0},{12,4},{16,8},{20,12},{24,16},{28,20},{9,1},{13,5},{17,9},{2... | collective-permute-start | bytes 1032200 | tf_op jit(solution)/shard_map/ppermute | solution.py:520
  56.5 16.0 %collective-permute-start.10 = (bf16[192,896]{1,0:T(8,128)(2,1)}, bf16[192,896]{1,0:T(8,128)(2,1)S(1)}, u32[]{:S(2)}, u32[]{:S(2)}) collective-permute-start(bf16[192,896]{1,0:T(8,128)(2,1)} %collective-permute-done.7), channel_id=1, source_target_pairs={{8,0},{12,4},{16,8},{20,12},{24,16},{28,20},{9,1},{13,5},{17,9},{2... | collective-permute-start | bytes 1032200 | tf_op jit(solution)/shard_map/ppermute | solution.py:520
  57.7 14.8 %collective-permute-start.9 = (bf16[192,896]{1,0:T(8,128)(2,1)}, bf16[192,896]{1,0:T(8,128)(2,1)}, u32[]{:S(2)}, u32[]{:S(2)}) collective-permute-start(bf16[192,896]{1,0:T(8,128)(2,1)} %collective-permute-done.6), channel_id=1, source_target_pairs={{0,8},{4,12},{8,16},{12,20},{16,24},{20,28},{1,9},{5,13},{9,17},{1... | collective-permute-start | bytes 1032200 | tf_op jit(solution)/shard_map/ppermute | solution.py:520
  64.9 7.6 %collective-permute-start.8 = (bf16[192,896]{1,0:T(8,128)(2,1)}, bf16[192,896]{1,0:T(8,128)(2,1)}, u32[]{:S(2)}, u32[]{:S(2)}) collective-permute-start(bf16[192,896]{1,0:T(8,128)(2,1)} %get-tuple-element.116), channel_id=1, source_target_pairs={{0,4},{4,0},{8,12},{12,8},{16,20},{20,16},{24,28},{28,24},{1,5},{5... | collective-permute-start | bytes 1032200 | tf_op jit(solution)/shard_map/ppermute | solution.py:524
  72.5 264.4 %reduce-scatter.3.cloned.1.call-start = ((), (), s32[]{:S(2)}) async-start(), calls=%async_computation.4 | async-start | bytes 5308416 | tf_op jit(solution)/shard_map/reduce_scatter | solution.py:776
  93.5 42.6 %collective-permute-start.4 = (bf16[2,256,1536]{2,1,0:T(8,128)(2,1)}, bf16[2,256,1536]{2,1,0:T(8,128)(2,1)}, u32[]{:S(2)}, u32[]{:S(2)}) collective-permute-start(bf16[2,256,1536]{2,1,0:T(8,128)(2,1)} %maximum_select_fusion.2), channel_id=1, source_target_pairs={{0,1},{1,0},{2,3},{3,2},{4,5},{5,4},{6,7},{7,6},{8,9},{9,8},{10,11... | collective-permute-start | bytes 4718600 | tf_op jit(solution)/shard_map/ppermute | solution.py:466
  93.5 19.9 %collective-permute-start.13 = (bf16[192,896]{1,0:T(8,128)(2,1)}, bf16[192,896]{1,0:T(8,128)(2,1)}, u32[]{:S(2)}, u32[]{:S(2)}) collective-permute-start(bf16[192,896]{1,0:T(8,128)(2,1)} %collective-permute-done.9), channel_id=1, source_target_pairs={{0,8},{4,12},{8,16},{12,20},{16,24},{20,28},{1,9},{5,13},{9,17},{1... | collective-permute-start | bytes 1032200 | tf_op jit(solution)/shard_map/ppermute | solution.py:520
  96.8 16.6 %collective-permute-start.14 = (bf16[192,896]{1,0:T(8,128)(2,1)S(1)}, bf16[192,896]{1,0:T(8,128)(2,1)}, u32[]{:S(2)}, u32[]{:S(2)}) collective-permute-start(bf16[192,896]{1,0:T(8,128)(2,1)S(1)} %collective-permute-done.10), channel_id=1, source_target_pairs={{8,0},{12,4},{16,8},{20,12},{24,16},{28,20},{9,1},{13,5},{17,9},{2... | collective-permute-start | bytes 1032200 | tf_op jit(solution)/shard_map/ppermute | solution.py:520
  102.0 11.4 %collective-permute-start.12 = (bf16[192,896]{1,0:T(8,128)(2,1)}, bf16[192,896]{1,0:T(8,128)(2,1)}, u32[]{:S(2)}, u32[]{:S(2)}) collective-permute-start(bf16[192,896]{1,0:T(8,128)(2,1)} %get-tuple-element.114), channel_id=1, source_target_pairs={{0,4},{4,0},{8,12},{12,8},{16,20},{20,16},{24,28},{28,24},{1,5},{5... | collective-permute-start | bytes 1032200 | tf_op jit(solution)/shard_map/ppermute | solution.py:524
  112.7 35.2 %collective-permute-start.18 = (bf16[2,256,1536]{2,1,0:T(8,128)(2,1)}, bf16[2,256,1536]{2,1,0:T(8,128)(2,1)S(1)}, u32[]{:S(2)}, u32[]{:S(2)}) collective-permute-start(bf16[2,256,1536]{2,1,0:T(8,128)(2,1)} %maximum_select_fusion.4), channel_id=1, source_target_pairs={{0,1},{1,0},{2,3},{3,2},{4,5},{5,4},{6,7},{7,6},{8,9},{9,8},{10,11... | collective-permute-start | bytes 4718600 | tf_op jit(solution)/shard_map/ppermute | solution.py:466
  117.1 18.3 %collective-permute-start.15 = (bf16[192,896]{1,0:T(8,128)(2,1)S(1)}, bf16[192,896]{1,0:T(8,128)(2,1)S(1)}, u32[]{:S(2)}, u32[]{:S(2)}) collective-permute-start(bf16[192,896]{1,0:T(8,128)(2,1)S(1)} %get-tuple-element.112), channel_id=1, source_target_pairs={{0,4},{4,0},{8,12},{12,8},{16,20},{20,16},{24,28},{28,24},{1,5},{5... | collective-permute-start | bytes 1032200 | tf_op jit(solution)/shard_map/ppermute | solution.py:524
  142.5 7.4 %collective-permute-start.16 = (bf16[1,64,1024]{2,1,0:T(8,128)(2,1)S(1)}, bf16[1,64,1024]{2,1,0:T(8,128)(2,1)S(1)}, u32[]{:S(2)}, u32[]{:S(2)}) collective-permute-start(bf16[1,64,1024]{2,1,0:T(8,128)(2,1)S(1)} %bitcast.296), channel_id=1, source_target_pairs={{0,2},{1,3},{2,0},{3,1},{4,6},{5,7},{6,4},{7,5},{8,10},{9,11},{10,... | collective-permute-start | bytes 393224 | tf_op jit(solution)/shard_map/ppermute | solution.py:466
  150.0 1.6 collective-permute-start.17
  207.3 182.7 %reduce-scatter.5.cloned.1.call-start = ((), (), s32[]{:S(2)}) async-start(), calls=%async_computation.5 | async-start | bytes 3932160 | tf_op jit(solution)/shard_map/reduce_scatter | solution.py:821
  245.5 21.2 %collective-permute-start.21 = (bf16[64,1024]{1,0:T(8,128)(2,1)}, bf16[64,1024]{1,0:T(8,128)(2,1)S(1)}, u32[]{:S(2)}, u32[]{:S(2)}) collective-permute-start(bf16[64,1024]{1,0:T(8,128)(2,1)} %get-tuple-element.125), channel_id=1, source_target_pairs={{0,1},{1,0},{2,3},{3,2},{4,5},{5,4},{6,7},{7,6},{8,9},{9,8},{10,11... | collective-permute-start | bytes 393224 | tf_op jit(solution)/shard_map/ppermute | solution.py:633
  245.5 21.3 %collective-permute-start.22 = (bf16[64,1024]{1,0:T(8,128)(2,1)}, bf16[64,1024]{1,0:T(8,128)(2,1)}, u32[]{:S(2)}, u32[]{:S(2)}) collective-permute-start(bf16[64,1024]{1,0:T(8,128)(2,1)} %get-tuple-element.127), channel_id=1, source_target_pairs={{0,2},{1,3},{2,0},{3,1},{4,6},{5,7},{6,4},{7,5},{8,10},{9,11},{10,... | collective-permute-start | bytes 393224 | tf_op jit(solution)/shard_map/ppermute | solution.py:633
  245.8 21.0 %collective-permute-start.23 = (bf16[64,1024]{1,0:T(8,128)(2,1)}, bf16[64,1024]{1,0:T(8,128)(2,1)}, u32[]{:S(2)}, u32[]{:S(2)}) collective-permute-start(bf16[64,1024]{1,0:T(8,128)(2,1)} %get-tuple-element.126), channel_id=1, source_target_pairs={{0,3},{1,2},{2,1},{3,0},{4,7},{5,6},{6,5},{7,4},{8,11},{9,10},{10,... | collective-permute-start | bytes 393224 | tf_op jit(solution)/shard_map/ppermute | solution.py:633
  252.6 46.3 %collective-permute-start.19 = (bf16[4,192,768]{2,1,0:T(8,128)(2,1)}, bf16[4,192,768]{2,1,0:T(8,128)(2,1)}, u32[]{:S(2)}, u32[]{:S(2)}) collective-permute-start(bf16[4,192,768]{2,1,0:T(8,128)(2,1)} %dynamic-slice_bitcast_fusion), channel_id=1, source_target_pairs={{0,4},{4,0},{8,12},{12,8},{16,20},{20,16},{24,28},{28,24},{1,5},{5... | collective-permute-start | bytes 3538952 | tf_op jit(solution)/shard_map/ppermute | solution.py:524
  274.3 29.3 %collective-permute-start.24 = (bf16[2,256,1536]{2,1,0:T(8,128)(2,1)}, bf16[2,256,1536]{2,1,0:T(8,128)(2,1)}, u32[]{:S(2)}, u32[]{:S(2)}) collective-permute-start(bf16[2,256,1536]{2,1,0:T(8,128)(2,1)} %select_bitcast_fusion), channel_id=1, source_target_pairs={{0,1},{1,0},{2,3},{3,2},{4,5},{5,4},{6,7},{7,6},{8,9},{9,8},{10,11... | collective-permute-start | bytes 4718600 | tf_op jit(solution)/shard_map/ppermute | solution.py:466
  278.0 19.2 %collective-permute-start.37 = (bf16[4,192,128]{2,1,0:T(8,128)(2,1)}, bf16[4,192,128]{2,1,0:T(8,128)(2,1)}, u32[]{:S(2)}, u32[]{:S(2)}) collective-permute-start(bf16[4,192,128]{2,1,0:T(8,128)(2,1)} %dynamic-slice_bitcast_fusion.5), channel_id=1, source_target_pairs={{0,4},{4,0},{8,12},{12,8},{16,20},{20,16},{24,28},{28,24},{1,5},{5... | collective-permute-start | bytes 589832 | tf_op jit(solution)/shard_map/ppermute | solution.py:524
  301.6 21.8 %collective-permute-start.20 = (bf16[192,768]{1,0:T(8,128)(2,1)}, bf16[192,768]{1,0:T(8,128)(2,1)}, u32[]{:S(2)}, u32[]{:S(2)}) collective-permute-start(bf16[192,768]{1,0:T(8,128)(2,1)} %get-tuple-element.123), channel_id=1, source_target_pairs={{0,8},{4,12},{8,0},{12,4},{16,24},{20,28},{24,16},{28,20},{1,9},{5... | collective-permute-start | bytes 884744 | tf_op jit(solution)/shard_map/ppermute | solution.py:524
  308.3 22.5 %collective-permute-start.25 = (bf16[1,256,1536]{2,1,0:T(8,128)(2,1)}, bf16[1,256,1536]{2,1,0:T(8,128)(2,1)}, u32[]{:S(2)}, u32[]{:S(2)}) collective-permute-start(bf16[1,256,1536]{2,1,0:T(8,128)(2,1)} %fusion.29), channel_id=1, source_target_pairs={{0,2},{1,3},{2,0},{3,1},{4,6},{5,7},{6,4},{7,5},{8,10},{9,11},{10,... | collective-permute-start | bytes 2359304 | tf_op jit(solution)/shard_map/ppermute | solution.py:466
  323.4 6.3 %collective-permute-start.26 = (f32[6500]{0:T(1024)S(1)}, f32[6500]{0:T(1024)S(1)}, u32[]{:S(2)}, u32[]{:S(2)}) collective-permute-start(f32[6500]{0:T(1024)S(1)} %concatenate.175), channel_id=1, source_target_pairs={{0,16},{4,20},{8,24},{12,28},{16,0},{20,4},{24,8},{28,12},{1,17},{... | collective-permute-start | bytes 78008 | tf_op jit(solution)/shard_map/ppermute | solution.py:524
  324.8 12.2 %collective-permute-start.38 = (bf16[192,128]{1,0:T(8,128)(2,1)S(1)}, bf16[192,128]{1,0:T(8,128)(2,1)S(1)}, u32[]{:S(2)}, u32[]{:S(2)}) collective-permute-start(bf16[192,128]{1,0:T(8,128)(2,1)S(1)} %get-tuple-element.141), channel_id=1, source_target_pairs={{0,8},{4,12},{8,0},{12,4},{16,24},{20,28},{24,16},{28,20},{1,9},{5... | collective-permute-start | bytes 147464 | tf_op jit(solution)/shard_map/ppermute | solution.py:524
  327.3 19.3 %collective-permute-start.39 = (bf16[192,128]{1,0:T(8,128)(2,1)S(1)}, bf16[192,128]{1,0:T(8,128)(2,1)S(1)}, u32[]{:S(2)}, u32[]{:S(2)}) collective-permute-start(bf16[192,128]{1,0:T(8,128)(2,1)S(1)} %get-tuple-element.143), channel_id=1, source_target_pairs={{0,16},{4,20},{8,24},{12,28},{16,0},{20,4},{24,8},{28,12},{1,17},{... | collective-permute-start | bytes 147464 | tf_op jit(solution)/shard_map/ppermute | solution.py:524
  327.4 19.2 %collective-permute-start.40 = (bf16[192,128]{1,0:T(8,128)(2,1)S(1)}, bf16[192,128]{1,0:T(8,128)(2,1)S(1)}, u32[]{:S(2)}, u32[]{:S(2)}) collective-permute-start(bf16[192,128]{1,0:T(8,128)(2,1)S(1)} %get-tuple-element.142), channel_id=1, source_target_pairs={{0,24},{4,28},{8,16},{12,20},{16,8},{20,12},{24,0},{28,4},{1,25},{... | collective-permute-start | bytes 147464 | tf_op jit(solution)/shard_map/ppermute | solution.py:524
  329.8 24.2 %collective-permute-start.28 = (bf16[192,768]{1,0:T(8,128)(2,1)}, bf16[192,768]{1,0:T(8,128)(2,1)S(1)}, u32[]{:S(2)}, u32[]{:S(2)}) collective-permute-start(bf16[192,768]{1,0:T(8,128)(2,1)} %get-tuple-element.122), channel_id=1, source_target_pairs={{0,16},{4,20},{8,24},{12,28},{16,0},{20,4},{24,8},{28,12},{1,17},{... | collective-permute-start | bytes 884744 | tf_op jit(solution)/shard_map/ppermute | solution.py:524
  330.8 27.0 %collective-permute-start.30 = (bf16[192,768]{1,0:T(8,128)(2,1)}, bf16[192,768]{1,0:T(8,128)(2,1)S(1)}, u32[]{:S(2)}, u32[]{:S(2)}) collective-permute-start(bf16[192,768]{1,0:T(8,128)(2,1)} %get-tuple-element.121), channel_id=1, source_target_pairs={{0,24},{4,28},{8,16},{12,20},{16,8},{20,12},{24,0},{28,4},{1,25},{... | collective-permute-start | bytes 884744 | tf_op jit(solution)/shard_map/ppermute | solution.py:524
  337.0 10.5 %collective-permute-start.27 = (f32[6500]{0:T(1024)S(1)}, f32[6500]{0:T(1024)S(1)}, u32[]{:S(2)}, u32[]{:S(2)}) collective-permute-start(f32[6500]{0:T(1024)S(1)} %add.303), channel_id=1, source_target_pairs={{0,8},{4,12},{8,0},{12,4},{16,24},{20,28},{24,16},{28,20},{1,9},{5... | collective-permute-start | bytes 78008 | tf_op jit(solution)/shard_map/ppermute | solution.py:524
  354.0 3.9 collective-permute-start.29
  357.9 4.6 %collective-permute-start.31 = (f32[1,1,6500]{2,1,0:T(1,128)S(1)}, f32[1,1,6500]{2,1,0:T(1,128)S(1)}, u32[]{:S(2)}, u32[]{:S(2)}) collective-permute-start(f32[1,1,6500]{2,1,0:T(1,128)S(1)} %broadcast_in_dim_broadcast_in_dim.3), channel_id=1, source_target_pairs={{0,2},{1,3},{2,0},{3,1},{4,6},{5,7},{6,4},{7,5},{8,10},{9,11},{10,... | collective-permute-start | bytes 78008 | tf_op jit(solution)/shard_map/ppermute | solution.py:466
  359.3 4.1 %collective-permute-start.33 = (bf16[1,48,768]{2,1,0:T(8,128)(2,1)S(1)}, bf16[1,48,768]{2,1,0:T(8,128)(2,1)S(1)}, u32[]{:S(2)}, u32[]{:S(2)}) collective-permute-start(bf16[1,48,768]{2,1,0:T(8,128)(2,1)S(1)} %constant_dynamic-slice_fusion.2), channel_id=1, source_target_pairs={{0,1},{1,0},{2,3},{3,2},{4,5},{5,4},{6,7},{7,6},{8,9},{9,8},{10,11... | collective-permute-start | bytes 221192 | tf_op jit(solution)/shard_map/ppermute | solution.py:607
  359.6 18.2 %collective-permute-start.36 = (bf16[96,1536]{1,0:T(8,128)(2,1)S(1)}, bf16[96,1536]{1,0:T(8,128)(2,1)S(1)}, u32[]{:S(2)}, u32[]{:S(2)}) collective-permute-start(bf16[96,1536]{1,0:T(8,128)(2,1)S(1)} %bitcast.313), channel_id=1, source_target_pairs={{0,0},{4,1},{8,2},{12,3},{1,4},{5,5},{9,6},{13,7},{2,8},{6,9},{10,... | collective-permute-start | bytes 884744 | tf_op jit(solution)/shard_map/ppermute | solution.py:828
  362.5 4.3 %collective-permute-start.32 = (f32[2,1,6500]{2,1,0:T(1,128)S(1)}, f32[2,1,6500]{2,1,0:T(1,128)S(1)}, u32[]{:S(2)}, u32[]{:S(2)}) collective-permute-start(f32[2,1,6500]{2,1,0:T(1,128)S(1)} %broadcast_select_fusion.3), channel_id=1, source_target_pairs={{0,1},{1,0},{2,3},{3,2},{4,5},{5,4},{6,7},{7,6},{8,9},{9,8},{10,11... | collective-permute-start | bytes 156008 | tf_op jit(solution)/shard_map/ppermute | solution.py:466
  363.4 11.1 %collective-permute-start.34 = (bf16[1,48,768]{2,1,0:T(8,128)(2,1)S(1)}, bf16[1,48,768]{2,1,0:T(8,128)(2,1)S(1)}, u32[]{:S(2)}, u32[]{:S(2)}) collective-permute-start(bf16[1,48,768]{2,1,0:T(8,128)(2,1)S(1)} %get-tuple-element.138), channel_id=1, source_target_pairs={{0,2},{1,3},{2,0},{3,1},{4,6},{5,7},{6,4},{7,5},{8,10},{9,11},{10,... | collective-permute-start | bytes 221192 | tf_op jit(solution)/shard_map/ppermute | solution.py:607
  366.8 10.9 %collective-permute-start.35 = (bf16[1,48,768]{2,1,0:T(8,128)(2,1)S(1)}, bf16[1,48,768]{2,1,0:T(8,128)(2,1)S(1)}, u32[]{:S(2)}, u32[]{:S(2)}) collective-permute-start(bf16[1,48,768]{2,1,0:T(8,128)(2,1)S(1)} %get-tuple-element.137), channel_id=1, source_target_pairs={{0,3},{1,2},{2,1},{3,0},{4,7},{5,6},{6,5},{7,4},{8,11},{9,10},{10,... | collective-permute-start | bytes 221192 | tf_op jit(solution)/shard_map/ppermute | solution.py:607
  379.8 3.8 collective-permute-start.41
  380.0 5.6 %collective-permute-start.42 = (bf16[1,48,896]{2,1,0:T(8,128)(2,1)S(1)}, bf16[1,48,896]{2,1,0:T(8,128)(2,1)S(1)}, u32[]{:S(2)}, u32[]{:S(2)}) collective-permute-start(bf16[1,48,896]{2,1,0:T(8,128)(2,1)S(1)} %get-tuple-element.136), channel_id=1, source_target_pairs={{0,2},{1,3},{2,0},{3,1},{4,6},{5,7},{6,4},{7,5},{8,10},{9,11},{10,... | collective-permute-start | bytes 258056 | tf_op jit(solution)/shard_map/ppermute | solution.py:607
  382.6 4.6 %collective-permute-start.43 = (bf16[1,48,896]{2,1,0:T(8,128)(2,1)S(1)}, bf16[1,48,896]{2,1,0:T(8,128)(2,1)S(1)}, u32[]{:S(2)}, u32[]{:S(2)}) collective-permute-start(bf16[1,48,896]{2,1,0:T(8,128)(2,1)S(1)} %get-tuple-element.134), channel_id=1, source_target_pairs={{0,3},{1,2},{2,1},{3,0},{4,7},{5,6},{6,5},{7,4},{8,11},{9,10},{10,... | collective-permute-start | bytes 258056 | tf_op jit(solution)/shard_map/ppermute | solution.py:607
  (53 other events, 390.6 us)
Sparse Core Ops, SparseCore 0:
  72.6 88.9 all-gather.1
  207.4 116.8 reduce-scatter.2
  337.1 43.4 reduce-scatter.4

commit v2 on v0

--- a/solution.py
+++ b/solution.py
@@ -453,15 +453,17 @@
         functools.partial(gate_forward, groups, z_rows, tall),
         grid=(tokens // rows,),
         in_specs=[tokens_of(n_width), tokens_of(n_width), whole(joined), tokens_of(width), whole(gain)],
-        out_specs=[tokens_of(width), tokens_of(width), pl.BlockSpec((8, rows), lambda c: (0, c))],
+        out_specs=[
+            tokens_of(width), tokens_of(width), pl.BlockSpec((8, rows), lambda c: (0, c)),
+            pl.BlockSpec((groups * z_rows, width), lambda c: (0, 0)),
+            pl.BlockSpec((parts, groups * tall, width), lambda c: (0, 0, 0)),
+        ],
         out_shape=[
             jax.ShapeDtypeStruct((tokens, width), f32),
             jax.ShapeDtypeStruct((tokens, width), f32),
             jax.ShapeDtypeStruct((8, tokens), f32),
-        ],
-        scratch_shapes=[
-            pltpu.VMEM((groups * z_rows, width), bf16),
-            pltpu.VMEM((parts, groups * tall, width), bf16),
+            jax.ShapeDtypeStruct((groups * z_rows, width), bf16),
+            jax.ShapeDtypeStruct((parts, groups * tall, width), bf16),
         ],
         name="gate_forward",
     )(normed, cot, joined, y, gain)
@@ -724,20 +726,18 @@
     order = [(f, (f % groups) * size + f // groups) for f in range(groups * size)]
     back = [(b, a) for a, b in order]
     out_moved = lax.ppermute(out_weight.astype(bf16), ("dp", "seq"), order)
-    mine, normed_own = lax.optimization_barrier((after(mine, docs), normed_own))
+    mine, normed_own = lax.optimization_barrier((after(mine, (docs, out_moved)), normed_own))
     mine = mine.reshape(size * in_rows, -1)
     n_first = own_inner + LANES
     cot_own = cotangent.reshape(block, n_width)
     normed_held = opened(normed_own)
     cot_held = opened(after(cot_own, mine))
     w_first, hopped = gathered_rows(mine[:, :n_first], [normed_held, cot_held])
-    z_block = jnp.concatenate([mine[:, n_first:], folded(after(out_moved, hopped), 1, own_inner)], axis=0)
+    z_block = jnp.concatenate([mine[:, n_first:], folded(out_moved, 1, own_inner)], axis=0)
 
     normed = gathered(normed_own, normed_held)
-    joined = lax.all_gather(z_block, "dp", axis=0, tiled=True).reshape(groups, -1, own_inner)
+    joined = lax.all_gather(after(z_block, hopped), "dp", axis=0, tiled=True).reshape(groups, -1, own_inner)
     z_rows = size * in_rows
-    w_z = joined[:, :z_rows].reshape(-1, own_inner)
-    w_out = unfolded(joined[:, z_rows:], n_width)
     cot = gathered(cot_own, cot_held)
     dcol = jnp.broadcast_to(docs[:, None], (tokens, LANES))
     drow = jnp.broadcast_to(docs[None, :], (8, tokens))
@@ -787,8 +787,11 @@
         lead, deep, tall, gate_in = groups, z_rows, out_rows, joined
     else:
         lead, deep, tall = 1, groups * z_rows, own_inner
-        gate_in = jnp.concatenate([w_z, folded(w_out, 1, own_inner)], axis=0)[None]
-    z, d_gn, sums = run_gate_forward(gate_in, deep, normed, cot, y, gain)
+        w_out = unfolded(joined[:, z_rows:], n_width)
+        gate_in = [joined[:, :z_rows].reshape(-1, own_inner), folded(w_out, 1, own_inner)]
+        gate_in = jnp.concatenate(gate_in, axis=0)[None]
+    z, d_gn, sums, w_z, w_out = run_gate_forward(gate_in, deep, normed, cot, y, gain)
+    w_out = jnp.concatenate(list(w_out), axis=1)
     sums = lax.psum(sums[:2], "seq")
     sums = jnp.pad(sums, ((0, 6), (0, 0)))
     gate_low, d_z, d_y, d_gain, terms = run_gate_backward(
@@ -823,7 +826,6 @@
     small_lines = halved_rows(mm(normed, d_small, TN).astype(bf16))
     branch = scattered(mm(after(gate_low, d_bc), w_out, NN).astype(bf16))
     result = (flat + branch).reshape(n_seqs, block, n_width).astype(bf16)
-    d_first = after(d_first, x_lines)
     d_normed = mm(d_first, w_first, NT) + mm(d_z, w_z, NT)
     d_norm_gain = jnp.sum(d_normed * normed.astype(f32), axis=0) / norm_gain
     d_skip = jnp.sum(d_conv_x[n_taps + 1].reshape(own_heads, head), axis=1)
@@ -842,8 +844,7 @@
     packed = added_over(packed, reversed(bits_of(groups)[1:]))
     lines, packed = lax.optimization_barrier((lines, packed))
     shares = shared_rows(lines)
-    packed = gathered(added_over(packed, bits_of(groups)[:1])[None])
-    parts, result = lax.optimization_barrier((after(parts, shares[:2]), result))
+    parts, result = lax.optimization_barrier((after(parts, lines), result))
     d_norm = after(d_normed.astype(bf16), parts)
     d_norm = lax.psum_scatter(d_norm, "seq", scatter_dimension=0, tiled=True).astype(f32)
 
@@ -855,6 +856,7 @@
     d_out_weight = lax.ppermute(out_part, ("dp", "seq"), back).astype(f32)
     in_z = own_rows(parts[:z_rows])
     shares, in_z, d_out_weight = lax.optimization_barrier((shares, in_z, d_out_weight))
+    packed = gathered(added_over(after(packed, shares), bits_of(groups)[:1])[None])
     first_part = sum(share.astype(f32) for share in shares)
     in_first = own_rows(first_part.astype(bf16))
     d_in_weight = jnp.concatenate(

time: 398 us -> 392 us (0.985)
  starting transfers between devices: 70.7 us -> 63.2 us
  local copies, waits for them, and re-layouts: 63.1 us -> 67.5 us
    ppermute x12, starting transfers between devices: 23.7 us -> 10.4 us  [crossed(): lax.ppermute(block, 'dp', [(i, i ^ bits) for i in range(lax.axis_size('dp...]
    ppermute x12, waiting for transfers between devices: 34.3 us -> 26.1 us  [crossed(): lax.ppermute(block, 'dp', [(i, i ^ bits) for i in range(lax.axis_size('dp...]
    all_to_all x1, waiting for transfers between devices: 8.07 us -> 0.01 us  [shards(): mine = lax.all_to_all(laid, 'seq', 0, 0, tiled=True)]
    all_gather x1, waiting for transfers between devices: 4.97 us -> 11.6 us  [shards(): lax.all_gather(after(z_block, hopped), 'dp', axis=0, tiled=True)]
    ppermute x6, starting transfers between devices: 13 us -> 18.7 us  [moved_by(): return lax.ppermute(block, 'dp', route)]
    ppermute x1, waiting for transfers between devices: 24 us -> 28.6 us  [shards(): d_out_weight = lax.ppermute(out_part, ('dp', 'seq'), back).astype(f32)]
    ppermute x6, waiting for transfers between devices: 1.8 us -> 6.41 us  [moved_by(): return lax.ppermute(block, 'dp', route)]
    unnamed x116 -> x119, local copies, waits for them, and re-layouts: 6.97 us -> 8.2 us
  transfers between devices with their start and end apart: 45 -> 45, of which waited for: 19 -> 18; matrix products, arithmetic and copies ran while one was open for 31% -> 33% of each run, Pallas kernels for 11% -> 11%
where the time goes in v2:
time: 392 us; the launch traced here: 388 us
  waiting for transfers between devices  88.8 us (23%)
  Pallas kernels  75.3 us (19%)
  local copies, waits for them, and re-layouts  67.5 us (17%)
  starting transfers between devices  63.2 us (16%)
  other arithmetic  43.5 us (11%)
  matrix products  29.2 us (7%)
  between operations  15.1 us (4%)
  blocking collectives  5.73 us (1%)
    pallas_call x1, Pallas kernels, run_backward(): pl.pallas_call(functools.partial(scan_backward, q, taps, pairs, head, chu...  30.8 us
    dot_general x7, matrix products, mm(): return lax.dot_general(a, b, (dims, ((), ())), preferred_element_type=out)  29.2 us
    ppermute x1, waiting for transfers between devices, shards(): d_out_weight = lax.ppermute(out_part, ('dp', 'seq'), back).astype(f32)  28.6 us
    ppermute x12, waiting for transfers between devices, crossed(): lax.ppermute(block, 'dp', [(i, i ^ bits) for i in range(lax.axis_size('dp...  26.1 us
    pallas_call x1, Pallas kernels, run_gate_backward(): pl.pallas_call(functools.partial(gate_backward, blocks, tile, z_rows, tal...  18.8 us
    ppermute x6, starting transfers between devices, moved_by(): return lax.ppermute(block, 'dp', route)  18.7 us
    ppermute x12, starting transfers between devices, swapped(): return lax.ppermute(block, 'seq', [(i, i ^ bit) for i in range(size)])  16.7 us
    pallas_call x1, Pallas kernels, run_forward(): pl.pallas_call(functools.partial(scan_forward, q, taps, pairs, head), gri...  13.4 us
  transfers between devices with their start and end apart: 45, of which 18 were waited for; matrix products, arithmetic and copies ran while one was open for 33% of the time, Pallas kernels for 11%

profile of v2, /device:TPU:2, one launch (start us, length us, event | category | flops | bytes accessed | tf_op | source)
XLA Modules:
  0.0 388.2 jit_solution(4522126405782386383)
XLA Ops:
  12.5 3.6 all-to-all-start
  16.3 4.5 %collective-permute-start.2 = (bf16[96,1536]{1,0:T(8,128)(2,1)S(1)}, bf16[96,1536]{1,0:T(8,128)(2,1)S(1)}, u32[]{:S(2)}, u32[]{:S(2)}) collective-permute-start(bf16[96,1536]{1,0:T(8,128)(2,1)S(1)} %convert_element_type.199), channel_id=1, source_target_pairs={{0,0},{1,4},{2,8},{3,12},{4,16},{5,20},{6,24},{7,28},{8,1},{9,5},{... | collective-permute-start | bytes 884744 | tf_op jit(solution)/shard_map/ppermute | solution.py:728
  22.5 5.1 %collective-permute-done.2 = bf16[96,1536]{1,0:T(8,128)(2,1)S(1)} collective-permute-done((bf16[96,1536]{1,0:T(8,128)(2,1)S(1)}, bf16[96,1536]{1,0:T(8,128)(2,1)S(1)}, u32[]{:S(2)}, u32[]{:S(2)}) %collective-permute-start.2) | collective-permute-done | bytes 294944 | tf_op jit(solution)/shard_map/ppermute | solution.py:728
  27.6 10.6 %collective-permute-start.3 = (bf16[1,256,1536]{2,1,0:T(8,128)(2,1)S(1)}, bf16[1,256,1536]{2,1,0:T(8,128)(2,1)S(1)}, u32[]{:S(2)}, u32[]{:S(2)}) collective-permute-start(bf16[1,256,1536]{2,1,0:T(8,128)(2,1)S(1)} %bitcast.199), channel_id=1, source_target_pairs={{0,2},{1,3},{2,0},{3,1},{4,6},{5,7},{6,4},{7,5},{8,10},{9,11},{10,... | collective-permute-start | bytes 2359304 | tf_op jit(solution)/shard_map/ppermute | solution.py:511
  42.8 6.0 %collective-permute-start.8 = (bf16[192,896]{1,0:T(8,128)(2,1)}, bf16[192,896]{1,0:T(8,128)(2,1)}, u32[]{:S(2)}, u32[]{:S(2)}) collective-permute-start(bf16[192,896]{1,0:T(8,128)(2,1)} %get-tuple-element.128), channel_id=1, source_target_pairs={{0,8},{4,12},{8,16},{12,20},{16,24},{20,28},{1,9},{5,13},{9,17},{1... | collective-permute-start | bytes 1032200 | tf_op jit(solution)/shard_map/ppermute | solution.py:565
  55.9 4.4 %collective-permute-done.9 = bf16[192,896]{1,0:T(8,128)(2,1)} collective-permute-done((bf16[192,896]{1,0:T(8,128)(2,1)}, bf16[192,896]{1,0:T(8,128)(2,1)}, u32[]{:S(2)}, u32[]{:S(2)}) %collective-permute-start.9) | collective-permute-done | bytes 344096 | tf_op jit(solution)/shard_map/ppermute | solution.py:565
  60.3 3.6 collective-permute-start.11
  65.3 1.9 constant_dynamic-update-slice_fusion.8
  72.8 3.7 collective-permute-done.10
  77.8 5.0 %collective-permute-start.14 = (bf16[192,896]{1,0:T(8,128)(2,1)S(1)}, bf16[192,896]{1,0:T(8,128)(2,1)}, u32[]{:S(2)}, u32[]{:S(2)}) collective-permute-start(bf16[192,896]{1,0:T(8,128)(2,1)S(1)} %collective-permute-done.11), channel_id=1, source_target_pairs={{0,8},{4,12},{8,16},{12,20},{16,24},{20,28},{1,9},{5,13},{9,17},{1... | collective-permute-start | bytes 1032200 | tf_op jit(solution)/shard_map/ppermute | solution.py:565
  86.0 2.1 constant_dynamic-update-slice_fusion.6
  100.6 2.7 collective-permute-done.13
  103.3 2.0 collective-permute-done.15
  107.0 1.9 constant_dynamic-update-slice_fusion.4
  109.5 7.4 %collective-permute-done.16 = bf16[192,896]{1,0:T(8,128)(2,1)S(1)} collective-permute-done((bf16[192,896]{1,0:T(8,128)(2,1)S(1)}, bf16[192,896]{1,0:T(8,128)(2,1)S(1)}, u32[]{:S(2)}, u32[]{:S(2)}) %collective-permute-start.16) | collective-permute-done | bytes 344096 | tf_op jit(solution)/shard_map/ppermute | solution.py:569
  117.6 2.5 maximum_select_fusion
  120.4 2.7 fusion.28
  126.6 5.3 %fusion.16.x_ref.xp_ref = bf16[1024,768]{1,0:T(8,128)(2,1)} fusion(bf16[1024,1536]{1,0:T(8,128)(2,1)S(1)} %bitcast.189, bf16[1536,896]{1,0:T(8,128)(2,1)} %constant_dynamic-update-slice_fusion.3), kind=kOutput, calls=%fused_computation.28 | convolution fusion | flops 2416705536 | bytes 7077888 | tf_op jit(solution)/shard_map/dot_general | solution.py:21
  131.9 1.9 maximum_select_fusion.1
  138.1 13.4 %scan_forward.1 = (f32[1024,768]{1,0:T(8,128)}, f32[8,128,768]{2,1,0:T(8,128)}) custom-call(bf16[1024,768]{1,0:T(8,128)(2,1)} %fusion.16.x_ref.xp_ref, f32[1024,128]{1,0:T(8,128)} %broadcast_select_fusion.1.small_ref, bf16[256,1024]{1,0:T(8,128)(2,1)} %bitcast.202, f32[1024,128]{1,0:T(8,128)} %broadcast_in_dim.78.dcol_ref.dcolp_ref, ...), custom_call_target="tpu_custom_call" | custom-call | tf_op jit(solution)/shard_map/scan_forward/pallas_call | solution.py:271
  151.5 11.6 %all-gather.2.cloned.1.call-done = bf16[3072,768]{1,0:T(8,128)(2,1)} async-done(((bf16[384,768]{1,0:T(8,128)(2,1)}), bf16[3072,768]{1,0:T(8,128)(2,1)}) %all-gather.2.cloned.1.call-update) | async-done | bytes 4718608 | tf_op jit(solution)/shard_map/all_gather | solution.py:739
  163.2 12.2 %gate_forward.1 = (f32[1024,768]{1,0:T(8,128)}, f32[1024,768]{1,0:T(8,128)}, f32[8,1024]{1,0:T(8,128)}, bf16[1536,768]{1,0:T(8,128)(2,1)}, bf16[2,768,768]{2,1,0:T(8,128)(2,1)}) custom-call(bf16[1024,1536]{1,0:T(8,128)(2,1)} %bitcast.190, bf16[1024,1536]{1,0:T(8,128)(2,1)} %bitcast.194, bf16[8,384,768]{2,1,0:T(8,128)(2,1)} %bitcast.205, ...), custom_call_target="tpu_custom_call" | custom-call | tf_op jit(solution)/shard_map/gate_forward/pallas_call | solution.py:452
  176.2 5.7 %psum.7 = f32[2,1024]{1,0:T(2,128)S(1)} all-reduce(f32[2,1024]{1,0:T(2,128)S(1)} %slice.189), channel_id=1, replica_groups=mesh['dp'=8,'seq'=4] {'seq'}, use_global_device_ids=true, to_apply=%region_1.2 | all-reduce | flops 2048 | bytes 16384 | tf_op jit(solution)/shard_map/psum | solution.py:795
  182.5 18.8 %gate_backward.1 = (bf16[1024,768]{1,0:T(8,128)(2,1)}, bf16[1024,768]{1,0:T(8,128)(2,1)}, f32[1024,768]{1,0:T(8,128)}, f32[8,768]{1,0:T(8,128)}, bf16[8,384,768]{2,1,0:T(8,128)(2,1)}) custom-call(bf16[1024,1536]{1,0:T(8,128)(2,1)} %bitcast.191, bf16[1024,1536]{1,0:T(8,128)(2,1)} %bitcast.195, f32[1024,768]{1,0:T(8,128)} %get-tuple-element.65.y_ref, ...), custom_call_target="tpu_custom_call" | custom-call | tf_op jit(solution)/shard_map/gate_backward/pallas_call | solution.py:484
  201.7 30.8 %scan_backward.1 = (bf16[1024,768]{1,0:T(8,128)(2,1)}, f32[1024,128]{1,0:T(8,128)}, f32[256,1024]{1,0:T(8,128)}, f32[8,768]{1,0:T(8,128)}, f32[8,128]{1,0:T(8,128)}) custom-call(bf16[1024,768]{1,0:T(8,128)(2,1)} %fusion.16.x_ref.xp_ref, bf16[1024,768]{1,0:T(8,128)(2,1)} %fusion.16.x_ref.xp_ref, f32[1024,128]{1,0:T(8,128)} %broadcast_select_fusion.1.small_ref, ...), custom_call_target="tpu_custom_call" | custom-call | tf_op jit(solution)/shard_map/scan_backward/pallas_call | solution.py:316
  232.5 5.4 %convolution_convert_fusion.1 = bf16[1536,768]{1,0:T(8,128)(2,1)} fusion(bf16[1024,1536]{1,0:T(8,128)(2,1)S(1)} %bitcast.192, bf16[1024,768]{1,0:T(8,128)(2,1)} %get-tuple-element.73), kind=kOutput, calls=%fused_computation.3 | convolution fusion | flops 2417098752 | bytes 7077888 | tf_op jit(solution)/shard_map/dot_general | solution.py:21
  237.8 1.9 fusion.45
  241.6 1.9 copy.116
  249.4 2.0 slice_bitcast_fusion.3
  254.3 2.1 multiply_reduce_fusion.1
  256.5 2.9 convolution_convert_fusion
  263.9 4.7 %fusion.70 = f32[1024,1536]{1,0:T(8,128)} fusion(bf16[1024,768]{1,0:T(8,128)(2,1)S(1)} %copy-done.54, bf16[1536,768]{1,0:T(8,128)(2,1)S(1)} %copy-done.53), kind=kOutput, calls=%fused_computation.178 | convolution fusion | flops 2415919104 | bytes 10223616 | tf_op jit(solution)/shard_map/dot_general | solution.py:21
  272.6 2.2 fusion
  279.4 7.1 %fusion.65 = (bf16[1024,1536]{1,0:T(8,128)(2,1)}, f32[1536]{0:T(1024)S(1)}) fusion(bf16[2,2,256,1536]{3,2,1,0:T(8,128)(2,1)S(1)} %copy-done.1, f32[1024,1536]{1,0:T(8,128)S(1)} %copy-done.57, bf16[1536,896]{1,0:T(8,128)(2,1)} %constant_dynamic-update-slice_fusion.3, bf16[1024,64]{1,0:T(8,128)(2,1)S(1)} %copy-done.22, bf16[1024,64]{1,0:T(8,128)(2,1)S(1)} %copy-done.21, ...), kind=kOutput, calls=%fused_computation.173 | convolution fusion | flops 2831940096 | bytes 17176576 | tf_op jit(solution)/shard_map/dot_general | solution.py:21
  288.4 5.1 %collective-permute-done.24 = f32[6500]{0:T(1024)S(1)} collective-permute-done((f32[6500]{0:T(1024)S(1)}, f32[6500]{0:T(1024)S(1)}, u32[]{:S(2)}, u32[]{:S(2)}) %collective-permute-start.24) | collective-permute-done | bytes 26032 | tf_op jit(solution)/shard_map/ppermute | solution.py:569
  293.5 4.0 %collective-permute-done.25 = f32[6500]{0:T(1024)S(1)} collective-permute-done((f32[6500]{0:T(1024)S(1)}, f32[6500]{0:T(1024)S(1)}, u32[]{:S(2)}, u32[]{:S(2)}) %collective-permute-start.25) | collective-permute-done | bytes 26032 | tf_op jit(solution)/shard_map/ppermute | solution.py:569
  299.2 2.1 fusion.6
  302.5 2.4 fusion.26
  305.0 2.4 reduce-scatter.3.cloned.1.call-done
  314.5 2.1 collective-permute-start.30
  317.6 3.6 collective-permute-start.34
  321.2 3.4 dynamic_update_slice.50
  324.6 3.4 dynamic_update_slice.51
  328.0 3.4 dynamic_update_slice.52
  331.5 28.6 %collective-permute-done.34 = bf16[96,1536]{1,0:T(8,128)(2,1)S(1)} collective-permute-done((bf16[96,1536]{1,0:T(8,128)(2,1)S(1)}, bf16[96,1536]{1,0:T(8,128)(2,1)S(1)}, u32[]{:S(2)}, u32[]{:S(2)}) %collective-permute-start.34) | collective-permute-done | bytes 294944 | tf_op jit(solution)/shard_map/ppermute | solution.py:856
  363.0 2.6 collective-permute-done.35
  365.9 3.6 collective-permute-done.36
  369.8 1.8 collective-permute-start.40
  (325 shorter events, 105.0 us)
Async XLA Ops:
  7.2 14.1 %collective-permute-start = (s32[1,1,256]{2,1,0:T(1,128)}, s32[1,1,256]{2,1,0:T(1,128)S(1)}, u32[]{:S(2)}, u32[]{:S(2)}) collective-permute-start(s32[1,1,256]{2,1,0:T(1,128)} %bitcast.243), channel_id=1, source_target_pairs={{0,2},{1,3},{2,0},{3,1},{4,6},{5,7},{6,4},{7,5},{8,10},{9,11},{10,... | collective-permute-start | bytes 3080 | tf_op jit(solution)/shard_map/ppermute | solution.py:511
  12.5 15.1 %all-to-all-start = ((bf16[4,48,1664]{2,1,0:T(8,128)(2,1)}), bf16[4,48,1664]{2,1,0:T(8,128)(2,1)S(1)}, u32[]{:S(2)}, u32[]{:S(2)}) async-start(bf16[4,48,1664]{2,1,0:T(8,128)(2,1)} %copy.110), calls=%async_computation | async-start | bytes 1277952 | tf_op jit(solution)/shard_map/all_to_all | solution.py:720
  16.2 147.0 %all-gather.2.cloned.1.call-start = ((), (), s32[]{:S(2)}) async-start(), calls=%async_computation.3 | async-start | bytes 5308416 | tf_op jit(solution)/shard_map/all_gather | solution.py:739
  16.3 11.4 %collective-permute-start.2 = (bf16[96,1536]{1,0:T(8,128)(2,1)S(1)}, bf16[96,1536]{1,0:T(8,128)(2,1)S(1)}, u32[]{:S(2)}, u32[]{:S(2)}) collective-permute-start(bf16[96,1536]{1,0:T(8,128)(2,1)S(1)} %convert_element_type.199), channel_id=1, source_target_pairs={{0,0},{1,4},{2,8},{3,12},{4,16},{5,20},{6,24},{7,28},{8,1},{9,5},{... | collective-permute-start | bytes 884744 | tf_op jit(solution)/shard_map/ppermute | solution.py:728
  21.3 1.2 collective-permute-start.1
  27.6 26.9 %collective-permute-start.3 = (bf16[1,256,1536]{2,1,0:T(8,128)(2,1)S(1)}, bf16[1,256,1536]{2,1,0:T(8,128)(2,1)S(1)}, u32[]{:S(2)}, u32[]{:S(2)}) collective-permute-start(bf16[1,256,1536]{2,1,0:T(8,128)(2,1)S(1)} %bitcast.199), channel_id=1, source_target_pairs={{0,2},{1,3},{2,0},{3,1},{4,6},{5,7},{6,4},{7,5},{8,10},{9,11},{10,... | collective-permute-start | bytes 2359304 | tf_op jit(solution)/shard_map/ppermute | solution.py:511
  40.9 10.2 %collective-permute-start.7 = (bf16[192,896]{1,0:T(8,128)(2,1)}, bf16[192,896]{1,0:T(8,128)(2,1)}, u32[]{:S(2)}, u32[]{:S(2)}) collective-permute-start(bf16[192,896]{1,0:T(8,128)(2,1)} %get-tuple-element.128), channel_id=1, source_target_pairs={{0,4},{4,0},{8,12},{12,8},{16,20},{20,16},{24,28},{28,24},{1,5},{5... | collective-permute-start | bytes 1032200 | tf_op jit(solution)/shard_map/ppermute | solution.py:569
  41.1 30.3 %collective-permute-start.5 = (bf16[1,256,1536]{2,1,0:T(8,128)(2,1)S(1)}, bf16[1,256,1536]{2,1,0:T(8,128)(2,1)S(1)}, u32[]{:S(2)}, u32[]{:S(2)}) collective-permute-start(bf16[1,256,1536]{2,1,0:T(8,128)(2,1)S(1)} %copy-done.8), channel_id=1, source_target_pairs={{0,2},{1,3},{2,0},{3,1},{4,6},{5,7},{6,4},{7,5},{8,10},{9,11},{10,... | collective-permute-start | bytes 2359304 | tf_op jit(solution)/shard_map/ppermute | solution.py:511
  42.8 13.1 %collective-permute-start.8 = (bf16[192,896]{1,0:T(8,128)(2,1)}, bf16[192,896]{1,0:T(8,128)(2,1)}, u32[]{:S(2)}, u32[]{:S(2)}) collective-permute-start(bf16[192,896]{1,0:T(8,128)(2,1)} %get-tuple-element.128), channel_id=1, source_target_pairs={{0,8},{4,12},{8,16},{12,20},{16,24},{20,28},{1,9},{5,13},{9,17},{1... | collective-permute-start | bytes 1032200 | tf_op jit(solution)/shard_map/ppermute | solution.py:565
  48.8 11.5 %collective-permute-start.9 = (bf16[192,896]{1,0:T(8,128)(2,1)}, bf16[192,896]{1,0:T(8,128)(2,1)}, u32[]{:S(2)}, u32[]{:S(2)}) collective-permute-start(bf16[192,896]{1,0:T(8,128)(2,1)} %get-tuple-element.128), channel_id=1, source_target_pairs={{8,0},{12,4},{16,8},{20,12},{24,16},{28,20},{9,1},{13,5},{17,9},{2... | collective-permute-start | bytes 1032200 | tf_op jit(solution)/shard_map/ppermute | solution.py:565
  60.3 16.1 %collective-permute-start.11 = (bf16[192,896]{1,0:T(8,128)(2,1)}, bf16[192,896]{1,0:T(8,128)(2,1)S(1)}, u32[]{:S(2)}, u32[]{:S(2)}) collective-permute-start(bf16[192,896]{1,0:T(8,128)(2,1)} %collective-permute-done.8), channel_id=1, source_target_pairs={{0,8},{4,12},{8,16},{12,20},{16,24},{20,28},{1,9},{5,13},{9,17},{1... | collective-permute-start | bytes 1032200 | tf_op jit(solution)/shard_map/ppermute | solution.py:565
  64.0 12.5 %collective-permute-start.12 = (bf16[192,896]{1,0:T(8,128)(2,1)}, bf16[192,896]{1,0:T(8,128)(2,1)}, u32[]{:S(2)}, u32[]{:S(2)}) collective-permute-start(bf16[192,896]{1,0:T(8,128)(2,1)} %collective-permute-done.9), channel_id=1, source_target_pairs={{8,0},{12,4},{16,8},{20,12},{24,16},{28,20},{9,1},{13,5},{17,9},{2... | collective-permute-start | bytes 1032200 | tf_op jit(solution)/shard_map/ppermute | solution.py:565
  67.2 9.2 %collective-permute-start.10 = (bf16[192,896]{1,0:T(8,128)(2,1)}, bf16[192,896]{1,0:T(8,128)(2,1)}, u32[]{:S(2)}, u32[]{:S(2)}) collective-permute-start(bf16[192,896]{1,0:T(8,128)(2,1)} %get-tuple-element.116), channel_id=1, source_target_pairs={{0,4},{4,0},{8,12},{12,8},{16,20},{20,16},{24,28},{28,24},{1,5},{5... | collective-permute-start | bytes 1032200 | tf_op jit(solution)/shard_map/ppermute | solution.py:569
  76.5 230.9 %reduce-scatter.3.cloned.1.call-start = ((), (), s32[]{:S(2)}) async-start(), calls=%async_computation.4 | async-start | bytes 5308416 | tf_op jit(solution)/shard_map/reduce_scatter | solution.py:807
  77.8 39.8 %collective-permute-start.4 = (bf16[2,256,1536]{2,1,0:T(8,128)(2,1)}, bf16[2,256,1536]{2,1,0:T(8,128)(2,1)}, u32[]{:S(2)}, u32[]{:S(2)}) collective-permute-start(bf16[2,256,1536]{2,1,0:T(8,128)(2,1)} %maximum_select_fusion.2), channel_id=1, source_target_pairs={{0,1},{1,0},{2,3},{3,2},{4,5},{5,4},{6,7},{7,6},{8,9},{9,8},{10,11... | collective-permute-start | bytes 4718600 | tf_op jit(solution)/shard_map/ppermute | solution.py:511
  77.8 25.5 %collective-permute-start.14 = (bf16[192,896]{1,0:T(8,128)(2,1)S(1)}, bf16[192,896]{1,0:T(8,128)(2,1)}, u32[]{:S(2)}, u32[]{:S(2)}) collective-permute-start(bf16[192,896]{1,0:T(8,128)(2,1)S(1)} %collective-permute-done.11), channel_id=1, source_target_pairs={{0,8},{4,12},{8,16},{12,20},{16,24},{20,28},{1,9},{5,13},{9,17},{1... | collective-permute-start | bytes 1032200 | tf_op jit(solution)/shard_map/ppermute | solution.py:565
  82.8 22.5 %collective-permute-start.15 = (bf16[192,896]{1,0:T(8,128)(2,1)}, bf16[192,896]{1,0:T(8,128)(2,1)}, u32[]{:S(2)}, u32[]{:S(2)}) collective-permute-start(bf16[192,896]{1,0:T(8,128)(2,1)} %collective-permute-done.12), channel_id=1, source_target_pairs={{8,0},{12,4},{16,8},{20,12},{24,16},{28,20},{9,1},{13,5},{17,9},{2... | collective-permute-start | bytes 1032200 | tf_op jit(solution)/shard_map/ppermute | solution.py:565
  88.1 15.2 %collective-permute-start.13 = (bf16[192,896]{1,0:T(8,128)(2,1)}, bf16[192,896]{1,0:T(8,128)(2,1)}, u32[]{:S(2)}, u32[]{:S(2)}) collective-permute-start(bf16[192,896]{1,0:T(8,128)(2,1)} %get-tuple-element.114), channel_id=1, source_target_pairs={{0,4},{4,0},{8,12},{12,8},{16,20},{20,16},{24,28},{28,24},{1,5},{5... | collective-permute-start | bytes 1032200 | tf_op jit(solution)/shard_map/ppermute | solution.py:569
  100.5 23.3 %copy-start.27 = (f32[1024]{0:T(1024)}, f32[1024]{0:T(1024)S(1)}, u32[]{:S(2)}) copy-start(f32[1024]{0:T(1024)S(1)} %get-tuple-element.147) | copy-start | bytes 12292
  100.5 23.3 %copy-start.29 = (f32[1024]{0:T(1024)}, f32[1024]{0:T(1024)S(1)}, u32[]{:S(2)}) copy-start(f32[1024]{0:T(1024)S(1)} %get-tuple-element.148) | copy-start | bytes 12292
  100.5 31.4 %collective-permute-start.6 = (bf16[2,256,1536]{2,1,0:T(8,128)(2,1)}, bf16[2,256,1536]{2,1,0:T(8,128)(2,1)S(1)}, u32[]{:S(2)}, u32[]{:S(2)}) collective-permute-start(bf16[2,256,1536]{2,1,0:T(8,128)(2,1)} %maximum_select_fusion.4), channel_id=1, source_target_pairs={{0,1},{1,0},{2,3},{3,2},{4,5},{5,4},{6,7},{7,6},{8,9},{9,8},{10,11... | collective-permute-start | bytes 4718600 | tf_op jit(solution)/shard_map/ppermute | solution.py:511
  108.9 7.9 %collective-permute-start.16 = (bf16[192,896]{1,0:T(8,128)(2,1)S(1)}, bf16[192,896]{1,0:T(8,128)(2,1)S(1)}, u32[]{:S(2)}, u32[]{:S(2)}) collective-permute-start(bf16[192,896]{1,0:T(8,128)(2,1)S(1)} %get-tuple-element.112), channel_id=1, source_target_pairs={{0,4},{4,0},{8,12},{12,8},{16,20},{20,16},{24,28},{28,24},{1,5},{5... | collective-permute-start | bytes 1032200 | tf_op jit(solution)/shard_map/ppermute | solution.py:569
  125.0 9.1 %collective-permute-start.17 = (bf16[1,64,1024]{2,1,0:T(8,128)(2,1)S(1)}, bf16[1,64,1024]{2,1,0:T(8,128)(2,1)S(1)}, u32[]{:S(2)}, u32[]{:S(2)}) collective-permute-start(bf16[1,64,1024]{2,1,0:T(8,128)(2,1)S(1)} %bitcast.219), channel_id=1, source_target_pairs={{0,2},{1,3},{2,0},{3,1},{4,6},{5,7},{6,4},{7,5},{8,10},{9,11},{10,... | collective-permute-start | bytes 393224 | tf_op jit(solution)/shard_map/ppermute | solution.py:511
  134.1 1.6 collective-permute-start.18
  201.3 177.1 %reduce-scatter.5.cloned.1.call-start = ((), (), s32[]{:S(2)}) async-start(), calls=%async_computation.5 | async-start | bytes 3932160 | tf_op jit(solution)/shard_map/reduce_scatter | solution.py:849
  201.6 30.8 %copy-start.1 = (bf16[2,2,256,1536]{3,2,1,0:T(8,128)(2,1)S(1)}, bf16[2,2,256,1536]{3,2,1,0:T(8,128)(2,1)}, u32[]{:S(2)}) copy-start(bf16[2,2,256,1536]{3,2,1,0:T(8,128)(2,1)} %copy-done) | copy-start | bytes 9437188
  239.7 14.6 %collective-permute-start.20 = (bf16[64,1024]{1,0:T(8,128)(2,1)}, bf16[64,1024]{1,0:T(8,128)(2,1)}, u32[]{:S(2)}, u32[]{:S(2)}) collective-permute-start(bf16[64,1024]{1,0:T(8,128)(2,1)} %get-tuple-element.125), channel_id=1, source_target_pairs={{0,1},{1,0},{2,3},{3,2},{4,5},{5,4},{6,7},{7,6},{8,9},{9,8},{10,11... | collective-permute-start | bytes 393224 | tf_op jit(solution)/shard_map/ppermute | solution.py:678
  239.7 14.6 %collective-permute-start.21 = (bf16[64,1024]{1,0:T(8,128)(2,1)}, bf16[64,1024]{1,0:T(8,128)(2,1)}, u32[]{:S(2)}, u32[]{:S(2)}) collective-permute-start(bf16[64,1024]{1,0:T(8,128)(2,1)} %get-tuple-element.127), channel_id=1, source_target_pairs={{0,2},{1,3},{2,0},{3,1},{4,6},{5,7},{6,4},{7,5},{8,10},{9,11},{10,... | collective-permute-start | bytes 393224 | tf_op jit(solution)/shard_map/ppermute | solution.py:678
  241.5 12.8 %collective-permute-start.22 = (bf16[64,1024]{1,0:T(8,128)(2,1)}, bf16[64,1024]{1,0:T(8,128)(2,1)}, u32[]{:S(2)}, u32[]{:S(2)}) collective-permute-start(bf16[64,1024]{1,0:T(8,128)(2,1)} %get-tuple-element.126), channel_id=1, source_target_pairs={{0,3},{1,2},{2,1},{3,0},{4,7},{5,6},{6,5},{7,4},{8,11},{9,10},{10,... | collective-permute-start | bytes 393224 | tf_op jit(solution)/shard_map/ppermute | solution.py:678
  252.9 46.3 %collective-permute-start.19 = (bf16[4,192,768]{2,1,0:T(8,128)(2,1)}, bf16[4,192,768]{2,1,0:T(8,128)(2,1)}, u32[]{:S(2)}, u32[]{:S(2)}) collective-permute-start(bf16[4,192,768]{2,1,0:T(8,128)(2,1)} %dynamic-slice_bitcast_fusion), channel_id=1, source_target_pairs={{0,4},{4,0},{8,12},{12,8},{16,20},{20,16},{24,28},{28,24},{1,5},{5... | collective-permute-start | bytes 3538952 | tf_op jit(solution)/shard_map/ppermute | solution.py:569
  261.8 10.7 %collective-permute-start.26 = (bf16[2,256,1536]{2,1,0:T(8,128)(2,1)}, bf16[2,256,1536]{2,1,0:T(8,128)(2,1)}, u32[]{:S(2)}, u32[]{:S(2)}) collective-permute-start(bf16[2,256,1536]{2,1,0:T(8,128)(2,1)} %select_bitcast_fusion), channel_id=1, source_target_pairs={{0,1},{1,0},{2,3},{3,2},{4,5},{5,4},{6,7},{7,6},{8,9},{9,8},{10,11... | collective-permute-start | bytes 4718600 | tf_op jit(solution)/shard_map/ppermute | solution.py:511
  271.8 26.3 %collective-permute-start.23 = (bf16[4,192,128]{2,1,0:T(8,128)(2,1)S(1)}, bf16[4,192,128]{2,1,0:T(8,128)(2,1)}, u32[]{:S(2)}, u32[]{:S(2)}) collective-permute-start(bf16[4,192,128]{2,1,0:T(8,128)(2,1)S(1)} %dynamic-slice_bitcast_fusion.5), channel_id=1, source_target_pairs={{0,4},{4,0},{8,12},{12,8},{16,20},{20,16},{24,28},{28,24},{1,5},{5... | collective-permute-start | bytes 589832 | tf_op jit(solution)/shard_map/ppermute | solution.py:569
  277.5 23.9 %collective-permute-start.27 = (bf16[1,256,1536]{2,1,0:T(8,128)(2,1)}, bf16[1,256,1536]{2,1,0:T(8,128)(2,1)}, u32[]{:S(2)}, u32[]{:S(2)}) collective-permute-start(bf16[1,256,1536]{2,1,0:T(8,128)(2,1)} %fusion.27), channel_id=1, source_target_pairs={{0,2},{1,3},{2,0},{3,1},{4,6},{5,7},{6,4},{7,5},{8,10},{9,11},{10,... | collective-permute-start | bytes 2359304 | tf_op jit(solution)/shard_map/ppermute | solution.py:511
  286.7 6.8 %collective-permute-start.24 = (f32[6500]{0:T(1024)S(1)}, f32[6500]{0:T(1024)S(1)}, u32[]{:S(2)}, u32[]{:S(2)}) collective-permute-start(f32[6500]{0:T(1024)S(1)} %concatenate.170), channel_id=1, source_target_pairs={{0,16},{4,20},{8,24},{12,28},{16,0},{20,4},{24,8},{28,12},{1,17},{... | collective-permute-start | bytes 78008 | tf_op jit(solution)/shard_map/ppermute | solution.py:569
  293.5 4.0 %collective-permute-start.25 = (f32[6500]{0:T(1024)S(1)}, f32[6500]{0:T(1024)S(1)}, u32[]{:S(2)}, u32[]{:S(2)}) collective-permute-start(f32[6500]{0:T(1024)S(1)} %add.287), channel_id=1, source_target_pairs={{0,8},{4,12},{8,0},{12,4},{16,24},{20,28},{24,16},{28,20},{1,9},{5... | collective-permute-start | bytes 78008 | tf_op jit(solution)/shard_map/ppermute | solution.py:569
  309.8 6.7 %collective-permute-start.31 = (bf16[1,48,768]{2,0,1:T(2,128)(2,1)S(1)}, bf16[1,48,768]{2,0,1:T(2,128)(2,1)S(1)}, u32[]{:S(2)}, u32[]{:S(2)}) collective-permute-start(bf16[1,48,768]{2,0,1:T(2,128)(2,1)S(1)} %get-tuple-element.139), channel_id=1, source_target_pairs={{0,1},{1,0},{2,3},{3,2},{4,5},{5,4},{6,7},{7,6},{8,9},{9,8},{10,11... | collective-permute-start | bytes 221192 | tf_op jit(solution)/shard_map/ppermute | solution.py:652
  309.8 7.1 %collective-permute-start.32 = (bf16[1,48,768]{2,0,1:T(2,128)(2,1)S(1)}, bf16[1,48,768]{2,0,1:T(2,128)(2,1)S(1)}, u32[]{:S(2)}, u32[]{:S(2)}) collective-permute-start(bf16[1,48,768]{2,0,1:T(2,128)(2,1)S(1)} %get-tuple-element.138), channel_id=1, source_target_pairs={{0,2},{1,3},{2,0},{3,1},{4,6},{5,7},{6,4},{7,5},{8,10},{9,11},{10,... | collective-permute-start | bytes 221192 | tf_op jit(solution)/shard_map/ppermute | solution.py:652
  312.2 48.8 %collective-permute-start.28 = (bf16[192,896]{1,0:T(8,128)(2,1)}, bf16[192,896]{1,0:T(8,128)(2,1)S(1)}, u32[]{:S(2)}, u32[]{:S(2)}) collective-permute-start(bf16[192,896]{1,0:T(8,128)(2,1)} %get-tuple-element.123), channel_id=1, source_target_pairs={{0,8},{4,12},{8,0},{12,4},{16,24},{20,28},{24,16},{28,20},{1,9},{5... | collective-permute-start | bytes 1032200 | tf_op jit(solution)/shard_map/ppermute | solution.py:569
  313.5 47.5 %collective-permute-start.29 = (bf16[192,896]{1,0:T(8,128)(2,1)S(1)}, bf16[192,896]{1,0:T(8,128)(2,1)S(1)}, u32[]{:S(2)}, u32[]{:S(2)}) collective-permute-start(bf16[192,896]{1,0:T(8,128)(2,1)S(1)} %get-tuple-element.122), channel_id=1, source_target_pairs={{0,16},{4,20},{8,24},{12,28},{16,0},{20,4},{24,8},{28,12},{1,17},{... | collective-permute-start | bytes 1032200 | tf_op jit(solution)/shard_map/ppermute | solution.py:569
  314.5 46.5 %collective-permute-start.30 = (bf16[192,896]{1,0:T(8,128)(2,1)S(1)}, bf16[192,896]{1,0:T(8,128)(2,1)}, u32[]{:S(2)}, u32[]{:S(2)}) collective-permute-start(bf16[192,896]{1,0:T(8,128)(2,1)S(1)} %get-tuple-element.121), channel_id=1, source_target_pairs={{0,24},{4,28},{8,16},{12,20},{16,8},{20,12},{24,0},{28,4},{1,25},{... | collective-permute-start | bytes 1032200 | tf_op jit(solution)/shard_map/ppermute | solution.py:569
  316.5 11.5 %collective-permute-start.33 = (bf16[1,48,768]{2,0,1:T(2,128)(2,1)}, bf16[1,48,768]{2,0,1:T(2,128)(2,1)}, u32[]{:S(2)}, u32[]{:S(2)}) collective-permute-start(bf16[1,48,768]{2,0,1:T(2,128)(2,1)} %get-tuple-element.137), channel_id=1, source_target_pairs={{0,3},{1,2},{2,1},{3,0},{4,7},{5,6},{6,5},{7,4},{8,11},{9,10},{10,... | collective-permute-start | bytes 221192 | tf_op jit(solution)/shard_map/ppermute | solution.py:652
  317.6 42.5 %collective-permute-start.34 = (bf16[96,1536]{1,0:T(8,128)(2,1)S(1)}, bf16[96,1536]{1,0:T(8,128)(2,1)S(1)}, u32[]{:S(2)}, u32[]{:S(2)}) collective-permute-start(bf16[96,1536]{1,0:T(8,128)(2,1)S(1)} %bitcast.234), channel_id=1, source_target_pairs={{0,0},{4,1},{8,2},{12,3},{16,4},{20,5},{24,6},{28,7},{1,8},{5,9},{... | collective-permute-start | bytes 884744 | tf_op jit(solution)/shard_map/ppermute | solution.py:856
  361.7 3.9 collective-permute-start.35
  365.6 3.9 %collective-permute-start.36 = (f32[1,1,6500]{2,1,0:T(1,128)S(1)}, f32[1,1,6500]{2,1,0:T(1,128)S(1)}, u32[]{:S(2)}, u32[]{:S(2)}) collective-permute-start(f32[1,1,6500]{2,1,0:T(1,128)S(1)} %broadcast_in_dim_broadcast_in_dim.3), channel_id=1, source_target_pairs={{0,2},{1,3},{2,0},{3,1},{4,6},{5,7},{6,4},{7,5},{8,10},{9,11},{10,... | collective-permute-start | bytes 78008 | tf_op jit(solution)/shard_map/ppermute | solution.py:511
  365.7 4.0 %collective-permute-start.38 = (bf16[1,48,896]{2,1,0:T(8,128)(2,1)S(1)}, bf16[1,48,896]{2,1,0:T(8,128)(2,1)S(1)}, u32[]{:S(2)}, u32[]{:S(2)}) collective-permute-start(bf16[1,48,896]{2,1,0:T(8,128)(2,1)S(1)} %constant_dynamic-slice_fusion.2), channel_id=1, source_target_pairs={{0,1},{1,0},{2,3},{3,2},{4,5},{5,4},{6,7},{7,6},{8,9},{9,8},{10,11... | collective-permute-start | bytes 258056 | tf_op jit(solution)/shard_map/ppermute | solution.py:652
  369.6 2.1 collective-permute-start.37
  369.8 6.9 %collective-permute-start.39 = (bf16[1,48,896]{2,1,0:T(8,128)(2,1)S(1)}, bf16[1,48,896]{2,1,0:T(8,128)(2,1)S(1)}, u32[]{:S(2)}, u32[]{:S(2)}) collective-permute-start(bf16[1,48,896]{2,1,0:T(8,128)(2,1)S(1)} %get-tuple-element.135), channel_id=1, source_target_pairs={{0,2},{1,3},{2,0},{3,1},{4,6},{5,7},{6,4},{7,5},{8,10},{9,11},{10,... | collective-permute-start | bytes 258056 | tf_op jit(solution)/shard_map/ppermute | solution.py:652
  369.8 6.9 %collective-permute-start.40 = (bf16[1,48,896]{2,1,0:T(8,128)(2,1)S(1)}, bf16[1,48,896]{2,1,0:T(8,128)(2,1)S(1)}, u32[]{:S(2)}, u32[]{:S(2)}) collective-permute-start(bf16[1,48,896]{2,1,0:T(8,128)(2,1)S(1)} %get-tuple-element.134), channel_id=1, source_target_pairs={{0,3},{1,2},{2,1},{3,0},{4,7},{5,6},{6,5},{7,4},{8,11},{9,10},{10,... | collective-permute-start | bytes 258056 | tf_op jit(solution)/shard_map/ppermute | solution.py:652
  (56 other events, 285.7 us)
Sparse Core Ops, SparseCore 0:
  76.6 86.5 all-gather.1
  201.5 105.9 reduce-scatter.2
  310.0 40.4 reduce-scatter.4

commit v3 on v2

--- a/solution.py
+++ b/solution.py
@@ -711,10 +711,27 @@
     in_rows = in_weight.shape[0]
 
     in_low = in_weight.astype(bf16)
-    z_cols = in_low[:, :n_inner].reshape(in_rows, size, own_inner)
-    x_cols = in_low[:, n_inner : 2 * n_inner].reshape(in_rows, size, own_inner)
+    runs = 2 if groups % 2 == 0 else 1
+
+    def dealt(columns):
+        cut = columns.reshape(columns.shape[0], runs, size, -1)
+        return cut.transpose(0, 2, 1, 3).reshape(columns.shape[0], size, -1)
+
+    def undealt(columns):
+        cut = columns.reshape(columns.shape[0], size, runs, -1)
+        return cut.transpose(0, 2, 1, 3).reshape(columns.shape[0], -1)
+
+    def own_columns(columns):
+        wide = columns.shape[1] // runs
+        narrow = wide // size
+        starts = [run * wide + index * narrow for run in range(runs)]
+        cut = [lax.dynamic_slice_in_dim(columns, start, narrow, 1) for start in starts]
+        return jnp.concatenate(cut, axis=1)
+
+    z_cols = dealt(in_low[:, :n_inner])
+    x_cols = dealt(in_low[:, n_inner : 2 * n_inner])
     bc_cols = in_low[:, 2 * n_inner : n_inner + n_mixed].reshape(in_rows, size, own_bc)
-    dt_cols = in_low[:, n_inner + n_mixed :].reshape(in_rows, size, own_heads)
+    dt_cols = dealt(in_low[:, n_inner + n_mixed :])
     gap = jnp.zeros((in_rows, size, LANES - own_heads - own_bc), bf16)
     laid = jnp.concatenate([x_cols, dt_cols, gap, bc_cols, z_cols], axis=2).transpose(1, 0, 2)
     mine = lax.all_to_all(laid, "seq", 0, 0, tiled=True)
@@ -723,10 +740,23 @@
     unit = flat * inv
     normed_own = (unit * norm_gain).astype(bf16)
     docs = gathered(segments).reshape(tokens).astype(f32)
-    order = [(f, (f % groups) * size + f // groups) for f in range(groups * size)]
+    half = groups // runs
+    order = []
+    for f in range(groups * size):
+        run, owner, spot = f // (half * size), f // half % size, f % half
+        order.append((f, (run * half + spot) * size + owner))
     back = [(b, a) for a, b in order]
     out_moved = lax.ppermute(out_weight.astype(bf16), ("dp", "seq"), order)
-    mine, normed_own = lax.optimization_barrier((after(mine, (docs, out_moved)), normed_own))
+    channels = [conv_weight[:, :n_inner], conv_bias[None, :n_inner], gate_gain[None]]
+    channels = own_columns(jnp.concatenate(channels, axis=0))
+    conv_x, bias_x, gain = channels[:n_taps], channels[n_taps : n_taps + 1], channels[n_taps + 1 :]
+    heads = own_columns(jnp.stack([step_bias, jnp.exp(log_rate), skip_gain]))
+    sb, rate = padded(heads[0:1], LANES), padded(heads[1:2], LANES)
+    skip = jnp.repeat(heads[2:3], head, axis=1)
+    dcol = jnp.broadcast_to(docs[:, None], (tokens, LANES))
+    drow = jnp.broadcast_to(docs[None, :], (8, tokens))
+    early = (docs, out_moved, conv_x, bias_x, gain, sb, rate, skip, dcol, drow)
+    mine, normed_own = lax.optimization_barrier((after(mine, early), normed_own))
     mine = mine.reshape(size * in_rows, -1)
     n_first = own_inner + LANES
     cot_own = cotangent.reshape(block, n_width)
@@ -739,8 +769,6 @@
     joined = lax.all_gather(after(z_block, hopped), "dp", axis=0, tiled=True).reshape(groups, -1, own_inner)
     z_rows = size * in_rows
     cot = gathered(cot_own, cot_held)
-    dcol = jnp.broadcast_to(docs[:, None], (tokens, LANES))
-    drow = jnp.broadcast_to(docs[None, :], (8, tokens))
 
     def own_part(vector, parts):
         return lax.dynamic_slice_in_dim(vector, index * parts, parts, vector.ndim - 1)
@@ -748,14 +776,8 @@
     w_x, w_small = w_first[:, :own_inner], w_first[:, own_inner:]
     small = mm(normed, w_small, NN)
     x_in = mm(normed, w_x, NN).astype(bf16)
-    conv_x = own_part(conv_weight[:, :n_inner], own_inner)
-    bias_x = own_part(conv_bias[None, :n_inner], own_inner)
     conv_bc = own_part(conv_weight[:, n_inner:], own_bc)
     bias_bc = own_part(conv_bias[None, n_inner:], own_bc)
-    sb = padded(own_part(step_bias[None], own_heads), LANES)
-    rate = padded(jnp.exp(own_part(log_rate[None], own_heads)), LANES)
-    skip = jnp.repeat(own_part(skip_gain[None], own_heads), head, axis=1)
-    gain = own_part(gate_gain[None], own_inner)
 
     head_lanes = jnp.arange(LANES) < own_heads
     bc_in = small[:, LANES - own_bc :].astype(bf16).astype(f32)
@@ -844,6 +866,7 @@
     packed = added_over(packed, reversed(bits_of(groups)[1:]))
     lines, packed = lax.optimization_barrier((lines, packed))
     shares = shared_rows(lines)
+    packed = gathered(added_over(packed, bits_of(groups)[:1])[None])
     parts, result = lax.optimization_barrier((after(parts, lines), result))
     d_norm = after(d_normed.astype(bf16), parts)
     d_norm = lax.psum_scatter(d_norm, "seq", scatter_dimension=0, tiled=True).astype(f32)
@@ -856,15 +879,14 @@
     d_out_weight = lax.ppermute(out_part, ("dp", "seq"), back).astype(f32)
     in_z = own_rows(parts[:z_rows])
     shares, in_z, d_out_weight = lax.optimization_barrier((shares, in_z, d_out_weight))
-    packed = gathered(added_over(after(packed, shares), bits_of(groups)[:1])[None])
     first_part = sum(share.astype(f32) for share in shares)
     in_first = own_rows(first_part.astype(bf16))
     d_in_weight = jnp.concatenate(
         [
-            in_z.reshape(in_rows, n_inner),
-            in_first[:, :, :own_inner].reshape(in_rows, n_inner),
+            undealt(in_z),
+            undealt(in_first[:, :, :own_inner]),
             in_first[:, :, n_first - own_bc :].reshape(in_rows, 2 * n_state),
-            in_first[:, :, own_inner : own_inner + own_heads].reshape(in_rows, n_heads),
+            undealt(in_first[:, :, own_inner : own_inner + own_heads]),
         ],
         axis=1,
     )
@@ -884,13 +906,13 @@
 
     got_x = take((n_taps + 1) * own_inner).reshape(size, n_taps + 1, own_inner)
     got_bc = take((n_taps + 1) * own_bc).reshape(size, n_taps + 1, own_bc)
-    got_x = got_x.transpose(1, 0, 2).reshape(n_taps + 1, n_inner)
+    got_x = undealt(got_x.transpose(1, 0, 2))
     got_bc = got_bc.transpose(1, 0, 2).reshape(n_taps + 1, 2 * n_state)
     conv_all = jnp.concatenate([got_x, got_bc], axis=1)
-    d_gate_gain = take(own_inner).reshape(n_inner)
-    d_step_bias = take(own_heads).reshape(n_heads)
-    d_log_rate = take(own_heads).reshape(n_heads)
-    d_skip_gain = take(own_heads).reshape(n_heads)
+    d_gate_gain = undealt(take(own_inner)[None])[0]
+    d_step_bias = undealt(take(own_heads)[None])[0]
+    d_log_rate = undealt(take(own_heads)[None])[0]
+    d_skip_gain = undealt(take(own_heads)[None])[0]
     d_norm_all = jnp.sum(take(n_width), axis=0)
     return (
         result,

time: 392 us -> 374 us (0.954)
  local copies, waits for them, and re-layouts: 67.5 us -> 56.2 us
  waiting for transfers between devices: 88.8 us -> 79 us
    ppermute x1, waiting for transfers between devices: 28.6 us -> 0.01 us  [shards(): d_out_weight = lax.ppermute(out_part, ('dp', 'seq'), back).astype(f32)]
    ppermute x6, waiting for transfers between devices: 0.02 us -> 12 us  [turned(): piece = lax.ppermute(piece, 'seq', [(i, i ^ bits) for i in range(size)])]
    dynamic_update_slice x5 -> x4, local copies, waits for them, and re-layouts: 10.2 us -> 0.05 us  [turned(): out = lax.dynamic_update_slice_in_dim(out, piece, index ^ bits, 0)]
    ppermute x12, waiting for transfers between devices: 26.1 us -> 34.5 us  [crossed(): lax.ppermute(block, 'dp', [(i, i ^ bits) for i in range(lax.axis_size('dp...]
    ppermute x12, starting transfers between devices: 16.7 us -> 9.06 us  [swapped(): return lax.ppermute(block, 'seq', [(i, i ^ bit) for i in range(size)])]
    all_to_all x1, waiting for transfers between devices: 0.01 us -> 5.28 us  [shards(): mine = lax.all_to_all(laid, 'seq', 0, 0, tiled=True)]
    ppermute x6, starting transfers between devices: 3.47 us -> 7.69 us  [turned(): piece = lax.ppermute(piece, 'seq', [(i, i ^ bits) for i in range(size)])]
    unnamed x119 -> x104, local copies, waits for them, and re-layouts: 8.2 us -> 5.62 us
  transfers between devices with their start and end apart: 45 -> 45, of which waited for: 18 -> 21; matrix products, arithmetic and copies ran while one was open for 33% -> 33% of each run, Pallas kernels for 11% -> 12%
where the time goes in v3:
time: 374 us; the launch traced here: 367 us
  waiting for transfers between devices  79 us (21%)
  Pallas kernels  75.3 us (20%)
  starting transfers between devices  60.3 us (16%)
  local copies, waits for them, and re-layouts  56.2 us (15%)
  other arithmetic  46.2 us (12%)
  matrix products  29.2 us (8%)
  between operations  15.5 us (4%)
  blocking collectives  5.73 us (2%)
    ppermute x12, waiting for transfers between devices, crossed(): lax.ppermute(block, 'dp', [(i, i ^ bits) for i in range(lax.axis_size('dp...  34.5 us
    pallas_call x1, Pallas kernels, run_backward(): pl.pallas_call(functools.partial(scan_backward, q, taps, pairs, head, chu...  30.8 us
    dot_general x7, matrix products, mm(): return lax.dot_general(a, b, (dims, ((), ())), preferred_element_type=out)  29.2 us
    ppermute x6, starting transfers between devices, moved_by(): return lax.ppermute(block, 'dp', route)  19.3 us
    pallas_call x1, Pallas kernels, run_gate_backward(): pl.pallas_call(functools.partial(gate_backward, blocks, tile, z_rows, tal...  18.8 us
    pallas_call x1, Pallas kernels, run_forward(): pl.pallas_call(functools.partial(scan_forward, q, taps, pairs, head), gri...  13.4 us
    ppermute x12, starting transfers between devices, crossed(): lax.ppermute(block, 'dp', [(i, i ^ bits) for i in range(lax.axis_size('dp...  13 us
    pallas_call x1, Pallas kernels, run_gate_forward(): pl.pallas_call(functools.partial(gate_forward, groups, z_rows, tall), gri...  12.3 us
  transfers between devices with their start and end apart: 45, of which 21 were waited for; matrix products, arithmetic and copies ran while one was open for 33% of the time, Pallas kernels for 12%

profile of v3, /device:TPU:2, one launch (start us, length us, event | category | flops | bytes accessed | tf_op | source)
XLA Modules:
  0.0 367.3 jit_solution(14913720909550906881)
XLA Ops:
  12.9 3.6 all-to-all-start
  16.7 2.5 collective-permute-start.2
  25.6 5.3 %all-to-all-done = bf16[4,48,1664]{2,1,0:T(8,128)(2,1)S(1)} async-done(((bf16[4,48,1664]{2,1,0:T(8,128)(2,1)}), bf16[4,48,1664]{2,1,0:T(8,128)(2,1)S(1)}, u32[]{:S(2)}, u32[]{:S(2)}) %all-to-all-start) | async-done | bytes 639008 | tf_op jit(solution)/shard_map/all_to_all | solution.py:737
  32.5 2.4 collective-permute-start.3
  39.1 5.9 %collective-permute-start.8 = (bf16[192,896]{1,0:T(8,128)(2,1)}, bf16[192,896]{1,0:T(8,128)(2,1)}, u32[]{:S(2)}, u32[]{:S(2)}) collective-permute-start(bf16[192,896]{1,0:T(8,128)(2,1)} %get-tuple-element.126), channel_id=1, source_target_pairs={{0,8},{4,12},{8,16},{12,20},{16,24},{20,28},{1,9},{5,13},{9,17},{1... | collective-permute-start | bytes 1032200 | tf_op jit(solution)/shard_map/ppermute | solution.py:565
  49.2 4.1 %collective-permute-done.3 = bf16[1,256,1536]{2,1,0:T(8,128)(2,1)S(1)} collective-permute-done((bf16[1,256,1536]{2,1,0:T(8,128)(2,1)S(1)}, bf16[1,256,1536]{2,1,0:T(8,128)(2,1)S(1)}, u32[]{:S(2)}, u32[]{:S(2)}) %collective-permute-start.3) | collective-permute-done | bytes 786464 | tf_op jit(solution)/shard_map/ppermute | solution.py:511
  55.6 4.2 %collective-permute-start.11 = (bf16[192,896]{1,0:T(8,128)(2,1)}, bf16[192,896]{1,0:T(8,128)(2,1)S(1)}, u32[]{:S(2)}, u32[]{:S(2)}) collective-permute-start(bf16[192,896]{1,0:T(8,128)(2,1)} %collective-permute-done.8), channel_id=1, source_target_pairs={{0,8},{4,12},{8,16},{12,20},{16,24},{20,28},{1,9},{5,13},{9,17},{1... | collective-permute-start | bytes 1032200 | tf_op jit(solution)/shard_map/ppermute | solution.py:565
  61.1 1.9 constant_dynamic-update-slice_fusion.11
  64.4 4.9 %collective-permute-done.5 = bf16[1,256,1536]{2,1,0:T(8,128)(2,1)S(1)} collective-permute-done((bf16[1,256,1536]{2,1,0:T(8,128)(2,1)S(1)}, bf16[1,256,1536]{2,1,0:T(8,128)(2,1)S(1)}, u32[]{:S(2)}, u32[]{:S(2)}) %collective-permute-start.5) | collective-permute-done | bytes 786464 | tf_op jit(solution)/shard_map/ppermute | solution.py:511
  71.0 5.2 %collective-permute-start.14 = (bf16[192,896]{1,0:T(8,128)(2,1)S(1)}, bf16[192,896]{1,0:T(8,128)(2,1)}, u32[]{:S(2)}, u32[]{:S(2)}) collective-permute-start(bf16[192,896]{1,0:T(8,128)(2,1)S(1)} %collective-permute-done.11), channel_id=1, source_target_pairs={{0,8},{4,12},{8,16},{12,20},{16,24},{20,28},{1,9},{5,13},{9,17},{1... | collective-permute-start | bytes 1032200 | tf_op jit(solution)/shard_map/ppermute | solution.py:565
  79.4 2.1 constant_dynamic-update-slice_fusion.9
  83.8 12.4 %collective-permute-done.13 = bf16[192,896]{1,0:T(8,128)(2,1)} collective-permute-done((bf16[192,896]{1,0:T(8,128)(2,1)}, bf16[192,896]{1,0:T(8,128)(2,1)}, u32[]{:S(2)}, u32[]{:S(2)}) %collective-permute-start.13) | collective-permute-done | bytes 344096 | tf_op jit(solution)/shard_map/ppermute | solution.py:569
  96.3 2.8 collective-permute-done.15
  100.8 1.9 constant_dynamic-update-slice_fusion.7
  103.7 6.2 %collective-permute-done.16 = bf16[192,896]{1,0:T(8,128)(2,1)S(1)} collective-permute-done((bf16[192,896]{1,0:T(8,128)(2,1)S(1)}, bf16[192,896]{1,0:T(8,128)(2,1)S(1)}, u32[]{:S(2)}, u32[]{:S(2)}) %collective-permute-start.16) | collective-permute-done | bytes 344096 | tf_op jit(solution)/shard_map/ppermute | solution.py:569
  110.7 2.5 maximum_select_fusion
  113.5 2.6 fusion.28
  119.4 5.3 %fusion.16.x_ref.xp_ref = bf16[1024,768]{1,0:T(8,128)(2,1)} fusion(bf16[1024,1536]{1,0:T(8,128)(2,1)S(1)} %bitcast.221, bf16[1536,896]{1,0:T(8,128)(2,1)} %constant_dynamic-update-slice_fusion.6), kind=kOutput, calls=%fused_computation.28 | convolution fusion | flops 2416705536 | bytes 7077888 | tf_op jit(solution)/shard_map/dot_general | solution.py:21
  124.7 1.9 maximum_select_fusion.1
  130.7 13.4 %scan_forward.1 = (f32[1024,768]{1,0:T(8,128)}, f32[8,128,768]{2,1,0:T(8,128)}) custom-call(bf16[1024,768]{1,0:T(8,128)(2,1)} %fusion.16.x_ref.xp_ref, f32[1024,128]{1,0:T(8,128)} %broadcast_select_fusion.1.small_ref, bf16[256,1024]{1,0:T(8,128)(2,1)} %bitcast.234, f32[1024,128]{1,0:T(8,128)} %broadcast_in_dim.75.dcol_ref.dcolp_ref, ...), custom_call_target="tpu_custom_call" | custom-call | tf_op jit(solution)/shard_map/scan_forward/pallas_call | solution.py:271
  144.1 10.8 %all-gather.2.cloned.1.call-done = bf16[3072,768]{1,0:T(8,128)(2,1)} async-done(((bf16[384,768]{1,0:T(8,128)(2,1)}), bf16[3072,768]{1,0:T(8,128)(2,1)}) %all-gather.2.cloned.1.call-update) | async-done | bytes 4718608 | tf_op jit(solution)/shard_map/all_gather | solution.py:769
  154.9 12.3 %gate_forward.1 = (f32[1024,768]{1,0:T(8,128)}, f32[1024,768]{1,0:T(8,128)}, f32[8,1024]{1,0:T(8,128)}, bf16[1536,768]{1,0:T(8,128)(2,1)}, bf16[2,768,768]{2,1,0:T(8,128)(2,1)}) custom-call(bf16[1024,1536]{1,0:T(8,128)(2,1)} %bitcast.222, bf16[1024,1536]{1,0:T(8,128)(2,1)} %bitcast.226, bf16[8,384,768]{2,1,0:T(8,128)(2,1)} %bitcast.237, ...), custom_call_target="tpu_custom_call" | custom-call | tf_op jit(solution)/shard_map/gate_forward/pallas_call | solution.py:452
  168.0 5.7 %psum.7 = f32[2,1024]{1,0:T(2,128)S(1)} all-reduce(f32[2,1024]{1,0:T(2,128)S(1)} %slice.216), channel_id=1, replica_groups=mesh['dp'=8,'seq'=4] {'seq'}, use_global_device_ids=true, to_apply=%region_1.2 | all-reduce | flops 2048 | bytes 16384 | tf_op jit(solution)/shard_map/psum | solution.py:817
  174.3 18.8 %gate_backward.1 = (bf16[1024,768]{1,0:T(8,128)(2,1)}, bf16[1024,768]{1,0:T(8,128)(2,1)}, f32[1024,768]{1,0:T(8,128)}, f32[8,768]{1,0:T(8,128)}, bf16[8,384,768]{2,1,0:T(8,128)(2,1)}) custom-call(bf16[1024,1536]{1,0:T(8,128)(2,1)} %bitcast.223, bf16[1024,1536]{1,0:T(8,128)(2,1)} %bitcast.227, f32[1024,768]{1,0:T(8,128)} %get-tuple-element.64.y_ref, ...), custom_call_target="tpu_custom_call" | custom-call | tf_op jit(solution)/shard_map/gate_backward/pallas_call | solution.py:484
  193.4 30.8 %scan_backward.1 = (bf16[1024,768]{1,0:T(8,128)(2,1)}, f32[1024,128]{1,0:T(8,128)}, f32[256,1024]{1,0:T(8,128)}, f32[8,768]{1,0:T(8,128)}, f32[8,128]{1,0:T(8,128)}) custom-call(bf16[1024,768]{1,0:T(8,128)(2,1)} %fusion.16.x_ref.xp_ref, bf16[1024,768]{1,0:T(8,128)(2,1)} %fusion.16.x_ref.xp_ref, f32[1024,128]{1,0:T(8,128)} %broadcast_select_fusion.1.small_ref, ...), custom_call_target="tpu_custom_call" | custom-call | tf_op jit(solution)/shard_map/scan_backward/pallas_call | solution.py:316
  224.2 5.4 %convolution_convert_fusion.1 = bf16[1536,768]{1,0:T(8,128)(2,1)} fusion(bf16[1024,1536]{1,0:T(8,128)(2,1)S(1)} %bitcast.224, bf16[1024,768]{1,0:T(8,128)(2,1)} %get-tuple-element.72), kind=kOutput, calls=%fused_computation.3 | convolution fusion | flops 2417098752 | bytes 7077888 | tf_op jit(solution)/shard_map/dot_general | solution.py:21
  229.6 1.9 fusion.45
  233.4 1.9 copy.75
  242.4 2.5 dynamic-slice_bitcast_fusion
  247.4 2.1 multiply_reduce_fusion.1
  249.5 2.9 convolution_convert_fusion
  254.9 1.8 slice_reduce_fusion.3
  258.1 4.6 %fusion.70 = f32[1024,1536]{1,0:T(8,128)} fusion(bf16[1024,768]{1,0:T(8,128)(2,1)S(1)} %copy-done.46, bf16[1536,768]{1,0:T(8,128)(2,1)S(1)} %copy-done.45), kind=kOutput, calls=%fused_computation.194 | convolution fusion | flops 2415919104 | bytes 10223616 | tf_op jit(solution)/shard_map/dot_general | solution.py:21
  262.7 1.9 fusion.62
  267.9 2.1 fusion
  274.5 7.3 %fusion.65 = (bf16[1024,1536]{1,0:T(8,128)(2,1)}, f32[1536]{0:T(1024)S(1)}) fusion(bf16[2,2,256,1536]{3,2,1,0:T(8,128)(2,1)S(1)} %copy-done.1, f32[1024,1536]{1,0:T(8,128)S(1)} %copy-done.50, bf16[1536,896]{1,0:T(8,128)(2,1)} %constant_dynamic-update-slice_fusion.6, bf16[1024,64]{1,0:T(8,128)(2,1)S(1)} %copy-done.23, bf16[1024,64]{1,0:T(8,128)(2,1)S(1)} %copy-done.22, ...), kind=kOutput, calls=%fused_computation.189 | convolution fusion | flops 2831940096 | bytes 17176576 | tf_op jit(solution)/shard_map/dot_general | solution.py:21
  285.0 3.1 collective-permute-done.24
  289.4 4.9 %collective-permute-done.25 = f32[6500]{0:T(1024)S(1)} collective-permute-done((f32[6500]{0:T(1024)S(1)}, f32[6500]{0:T(1024)S(1)}, u32[]{:S(2)}, u32[]{:S(2)}) %collective-permute-start.25) | collective-permute-done | bytes 26032 | tf_op jit(solution)/shard_map/ppermute | solution.py:569
  295.4 2.1 fusion.6
  298.7 2.5 fusion.26
  302.8 2.4 collective-permute-done.28
  307.8 2.8 collective-permute-start.32
  319.6 2.9 collective-permute-start.37
  322.7 5.8 %collective-permute-done.36 = bf16[1,48,768]{2,1,0:T(8,128)(2,1)S(1)} collective-permute-done((bf16[1,48,768]{2,1,0:T(8,128)(2,1)S(1)}, bf16[1,48,768]{2,1,0:T(8,128)(2,1)S(1)}, u32[]{:S(2)}, u32[]{:S(2)}) %collective-permute-start.36) | collective-permute-done | bytes 73760 | tf_op jit(solution)/shard_map/ppermute | solution.py:652
  329.4 5.3 %collective-permute-done.32 = bf16[192,896]{1,0:T(8,128)(2,1)} collective-permute-done((bf16[192,896]{1,0:T(8,128)(2,1)}, bf16[192,896]{1,0:T(8,128)(2,1)}, u32[]{:S(2)}, u32[]{:S(2)}) %collective-permute-start.32) | collective-permute-done | bytes 344096 | tf_op jit(solution)/shard_map/ppermute | solution.py:569
  337.5 6.6 %collective-permute-start.39 = (bf16[1,48,896]{2,1,0:T(8,128)(2,1)S(1)}, bf16[1,48,896]{2,1,0:T(8,128)(2,1)S(1)}, u32[]{:S(2)}, u32[]{:S(2)}) collective-permute-start(bf16[1,48,896]{2,1,0:T(8,128)(2,1)S(1)} %get-tuple-element.133), channel_id=1, source_target_pairs={{0,2},{1,3},{2,0},{3,1},{4,6},{5,7},{6,4},{7,5},{8,10},{9,11},{10,... | collective-permute-start | bytes 258056 | tf_op jit(solution)/shard_map/ppermute | solution.py:652
  347.0 3.6 collective-permute-done.40
  352.0 2.3 copy.103
  (339 shorter events, 103.5 us)
Async XLA Ops:
  7.2 15.8 %collective-permute-start = (s32[1,1,256]{2,1,0:T(1,128)}, s32[1,1,256]{2,1,0:T(1,128)S(1)}, u32[]{:S(2)}, u32[]{:S(2)}) collective-permute-start(s32[1,1,256]{2,1,0:T(1,128)} %bitcast.284), channel_id=1, source_target_pairs={{0,2},{1,3},{2,0},{3,1},{4,6},{5,7},{6,4},{7,5},{8,10},{9,11},{10,... | collective-permute-start | bytes 3080 | tf_op jit(solution)/shard_map/ppermute | solution.py:511
  12.9 18.0 %all-to-all-start = ((bf16[4,48,1664]{2,1,0:T(8,128)(2,1)}), bf16[4,48,1664]{2,1,0:T(8,128)(2,1)S(1)}, u32[]{:S(2)}, u32[]{:S(2)}) async-start(bf16[4,48,1664]{2,1,0:T(8,128)(2,1)} %bitcast.4), calls=%async_computation | async-start | bytes 1277952 | tf_op jit(solution)/shard_map/all_to_all | solution.py:737
  16.6 138.3 %all-gather.2.cloned.1.call-start = ((), (), s32[]{:S(2)}) async-start(), calls=%async_computation.3 | async-start | bytes 5308416 | tf_op jit(solution)/shard_map/all_gather | solution.py:769
  16.7 8.9 %collective-permute-start.2 = (bf16[96,1536]{1,0:T(8,128)(2,1)S(1)}, bf16[96,1536]{1,0:T(8,128)(2,1)S(1)}, u32[]{:S(2)}, u32[]{:S(2)}) collective-permute-start(bf16[96,1536]{1,0:T(8,128)(2,1)S(1)} %convert_element_type.199), channel_id=1, source_target_pairs={{0,0},{1,4},{2,8},{3,12},{4,1},{5,5},{6,9},{7,13},{8,2},{9,6},{10,... | collective-permute-start | bytes 884744 | tf_op jit(solution)/shard_map/ppermute | solution.py:749
  23.0 1.2 collective-permute-start.1
  32.5 20.8 %collective-permute-start.3 = (bf16[1,256,1536]{2,1,0:T(8,128)(2,1)S(1)}, bf16[1,256,1536]{2,1,0:T(8,128)(2,1)S(1)}, u32[]{:S(2)}, u32[]{:S(2)}) collective-permute-start(bf16[1,256,1536]{2,1,0:T(8,128)(2,1)S(1)} %bitcast.231), channel_id=1, source_target_pairs={{0,2},{1,3},{2,0},{3,1},{4,6},{5,7},{6,4},{7,5},{8,10},{9,11},{10,... | collective-permute-start | bytes 2359304 | tf_op jit(solution)/shard_map/ppermute | solution.py:511
  37.5 9.9 %collective-permute-start.7 = (bf16[192,896]{1,0:T(8,128)(2,1)}, bf16[192,896]{1,0:T(8,128)(2,1)}, u32[]{:S(2)}, u32[]{:S(2)}) collective-permute-start(bf16[192,896]{1,0:T(8,128)(2,1)} %get-tuple-element.126), channel_id=1, source_target_pairs={{0,4},{4,0},{8,12},{12,8},{16,20},{20,16},{24,28},{28,24},{1,5},{5... | collective-permute-start | bytes 1032200 | tf_op jit(solution)/shard_map/ppermute | solution.py:569
  38.1 31.3 %collective-permute-start.5 = (bf16[1,256,1536]{2,1,0:T(8,128)(2,1)S(1)}, bf16[1,256,1536]{2,1,0:T(8,128)(2,1)S(1)}, u32[]{:S(2)}, u32[]{:S(2)}) collective-permute-start(bf16[1,256,1536]{2,1,0:T(8,128)(2,1)S(1)} %copy-done.8), channel_id=1, source_target_pairs={{0,2},{1,3},{2,0},{3,1},{4,6},{5,7},{6,4},{7,5},{8,10},{9,11},{10,... | collective-permute-start | bytes 2359304 | tf_op jit(solution)/shard_map/ppermute | solution.py:511
  39.1 15.5 %collective-permute-start.8 = (bf16[192,896]{1,0:T(8,128)(2,1)}, bf16[192,896]{1,0:T(8,128)(2,1)}, u32[]{:S(2)}, u32[]{:S(2)}) collective-permute-start(bf16[192,896]{1,0:T(8,128)(2,1)} %get-tuple-element.126), channel_id=1, source_target_pairs={{0,8},{4,12},{8,16},{12,20},{16,24},{20,28},{1,9},{5,13},{9,17},{1... | collective-permute-start | bytes 1032200 | tf_op jit(solution)/shard_map/ppermute | solution.py:565
  45.0 10.6 %collective-permute-start.9 = (bf16[192,896]{1,0:T(8,128)(2,1)}, bf16[192,896]{1,0:T(8,128)(2,1)}, u32[]{:S(2)}, u32[]{:S(2)}) collective-permute-start(bf16[192,896]{1,0:T(8,128)(2,1)} %get-tuple-element.126), channel_id=1, source_target_pairs={{8,0},{12,4},{16,8},{20,12},{24,16},{28,20},{9,1},{13,5},{17,9},{2... | collective-permute-start | bytes 1032200 | tf_op jit(solution)/shard_map/ppermute | solution.py:565
  55.6 15.1 %collective-permute-start.11 = (bf16[192,896]{1,0:T(8,128)(2,1)}, bf16[192,896]{1,0:T(8,128)(2,1)S(1)}, u32[]{:S(2)}, u32[]{:S(2)}) collective-permute-start(bf16[192,896]{1,0:T(8,128)(2,1)} %collective-permute-done.8), channel_id=1, source_target_pairs={{0,8},{4,12},{8,16},{12,20},{16,24},{20,28},{1,9},{5,13},{9,17},{1... | collective-permute-start | bytes 1032200 | tf_op jit(solution)/shard_map/ppermute | solution.py:565
  59.8 11.0 %collective-permute-start.12 = (bf16[192,896]{1,0:T(8,128)(2,1)}, bf16[192,896]{1,0:T(8,128)(2,1)}, u32[]{:S(2)}, u32[]{:S(2)}) collective-permute-start(bf16[192,896]{1,0:T(8,128)(2,1)} %collective-permute-done.9), channel_id=1, source_target_pairs={{8,0},{12,4},{16,8},{20,12},{24,16},{28,20},{9,1},{13,5},{17,9},{2... | collective-permute-start | bytes 1032200 | tf_op jit(solution)/shard_map/ppermute | solution.py:565
  63.0 7.7 %collective-permute-start.10 = (bf16[192,896]{1,0:T(8,128)(2,1)}, bf16[192,896]{1,0:T(8,128)(2,1)}, u32[]{:S(2)}, u32[]{:S(2)}) collective-permute-start(bf16[192,896]{1,0:T(8,128)(2,1)} %get-tuple-element.114), channel_id=1, source_target_pairs={{0,4},{4,0},{8,12},{12,8},{16,20},{20,16},{24,28},{28,24},{1,5},{5... | collective-permute-start | bytes 1032200 | tf_op jit(solution)/shard_map/ppermute | solution.py:569
  70.8 230.4 %reduce-scatter.3.cloned.1.call-start = ((), (), s32[]{:S(2)}) async-start(), calls=%async_computation.4 | async-start | bytes 5308416 | tf_op jit(solution)/shard_map/reduce_scatter | solution.py:829
  71.0 39.8 %collective-permute-start.4 = (bf16[2,256,1536]{2,1,0:T(8,128)(2,1)}, bf16[2,256,1536]{2,1,0:T(8,128)(2,1)}, u32[]{:S(2)}, u32[]{:S(2)}) collective-permute-start(bf16[2,256,1536]{2,1,0:T(8,128)(2,1)} %maximum_select_fusion.2), channel_id=1, source_target_pairs={{0,1},{1,0},{2,3},{3,2},{4,5},{5,4},{6,7},{7,6},{8,9},{9,8},{10,11... | collective-permute-start | bytes 4718600 | tf_op jit(solution)/shard_map/ppermute | solution.py:511
  71.0 25.3 %collective-permute-start.14 = (bf16[192,896]{1,0:T(8,128)(2,1)S(1)}, bf16[192,896]{1,0:T(8,128)(2,1)}, u32[]{:S(2)}, u32[]{:S(2)}) collective-permute-start(bf16[192,896]{1,0:T(8,128)(2,1)S(1)} %collective-permute-done.11), channel_id=1, source_target_pairs={{0,8},{4,12},{8,16},{12,20},{16,24},{20,28},{1,9},{5,13},{9,17},{1... | collective-permute-start | bytes 1032200 | tf_op jit(solution)/shard_map/ppermute | solution.py:565
  76.2 22.8 %collective-permute-start.15 = (bf16[192,896]{1,0:T(8,128)(2,1)}, bf16[192,896]{1,0:T(8,128)(2,1)}, u32[]{:S(2)}, u32[]{:S(2)}) collective-permute-start(bf16[192,896]{1,0:T(8,128)(2,1)} %collective-permute-done.12), channel_id=1, source_target_pairs={{8,0},{12,4},{16,8},{20,12},{24,16},{28,20},{9,1},{13,5},{17,9},{2... | collective-permute-start | bytes 1032200 | tf_op jit(solution)/shard_map/ppermute | solution.py:565
  81.5 14.7 %collective-permute-start.13 = (bf16[192,896]{1,0:T(8,128)(2,1)}, bf16[192,896]{1,0:T(8,128)(2,1)}, u32[]{:S(2)}, u32[]{:S(2)}) collective-permute-start(bf16[192,896]{1,0:T(8,128)(2,1)} %get-tuple-element.112), channel_id=1, source_target_pairs={{0,4},{4,0},{8,12},{12,8},{16,20},{20,16},{24,28},{28,24},{1,5},{5... | collective-permute-start | bytes 1032200 | tf_op jit(solution)/shard_map/ppermute | solution.py:569
  83.8 33.1 %copy-start.25 = (f32[1024]{0:T(1024)}, f32[1024]{0:T(1024)S(1)}, u32[]{:S(2)}) copy-start(f32[1024]{0:T(1024)S(1)} %get-tuple-element.150) | copy-start | bytes 12292
  83.8 40.9 %collective-permute-start.6 = (bf16[2,256,1536]{2,1,0:T(8,128)(2,1)}, bf16[2,256,1536]{2,1,0:T(8,128)(2,1)S(1)}, u32[]{:S(2)}, u32[]{:S(2)}) collective-permute-start(bf16[2,256,1536]{2,1,0:T(8,128)(2,1)} %maximum_select_fusion.4), channel_id=1, source_target_pairs={{0,1},{1,0},{2,3},{3,2},{4,5},{5,4},{6,7},{7,6},{8,9},{9,8},{10,11... | collective-permute-start | bytes 4718600 | tf_op jit(solution)/shard_map/ppermute | solution.py:511
  102.7 7.2 %collective-permute-start.16 = (bf16[192,896]{1,0:T(8,128)(2,1)S(1)}, bf16[192,896]{1,0:T(8,128)(2,1)S(1)}, u32[]{:S(2)}, u32[]{:S(2)}) collective-permute-start(bf16[192,896]{1,0:T(8,128)(2,1)S(1)} %get-tuple-element.110), channel_id=1, source_target_pairs={{0,4},{4,0},{8,12},{12,8},{16,20},{20,16},{24,28},{28,24},{1,5},{5... | collective-permute-start | bytes 1032200 | tf_op jit(solution)/shard_map/ppermute | solution.py:569
  118.0 8.9 %collective-permute-start.17 = (bf16[1,64,1024]{2,1,0:T(8,128)(2,1)S(1)}, bf16[1,64,1024]{2,1,0:T(8,128)(2,1)}, u32[]{:S(2)}, u32[]{:S(2)}) collective-permute-start(bf16[1,64,1024]{2,1,0:T(8,128)(2,1)S(1)} %bitcast.251), channel_id=1, source_target_pairs={{0,2},{1,3},{2,0},{3,1},{4,6},{5,7},{6,4},{7,5},{8,10},{9,11},{10,... | collective-permute-start | bytes 393224 | tf_op jit(solution)/shard_map/ppermute | solution.py:511
  127.9 1.9 collective-permute-start.18
  193.1 164.0 %reduce-scatter.5.cloned.1.call-start = ((), (), s32[]{:S(2)}) async-start(), calls=%async_computation.5 | async-start | bytes 3932160 | tf_op jit(solution)/shard_map/reduce_scatter | solution.py:872
  193.4 30.8 %copy-start.1 = (bf16[2,2,256,1536]{3,2,1,0:T(8,128)(2,1)S(1)}, bf16[2,2,256,1536]{3,2,1,0:T(8,128)(2,1)}, u32[]{:S(2)}) copy-start(bf16[2,2,256,1536]{3,2,1,0:T(8,128)(2,1)} %copy-done) | copy-start | bytes 9437188
  231.5 15.1 %collective-permute-start.20 = (bf16[64,1024]{1,0:T(8,128)(2,1)}, bf16[64,1024]{1,0:T(8,128)(2,1)}, u32[]{:S(2)}, u32[]{:S(2)}) collective-permute-start(bf16[64,1024]{1,0:T(8,128)(2,1)} %get-tuple-element.123), channel_id=1, source_target_pairs={{0,1},{1,0},{2,3},{3,2},{4,5},{5,4},{6,7},{7,6},{8,9},{9,8},{10,11... | collective-permute-start | bytes 393224 | tf_op jit(solution)/shard_map/ppermute | solution.py:678
  231.5 15.1 %collective-permute-start.21 = (bf16[64,1024]{1,0:T(8,128)(2,1)}, bf16[64,1024]{1,0:T(8,128)(2,1)}, u32[]{:S(2)}, u32[]{:S(2)}) collective-permute-start(bf16[64,1024]{1,0:T(8,128)(2,1)} %get-tuple-element.125), channel_id=1, source_target_pairs={{0,2},{1,3},{2,0},{3,1},{4,6},{5,7},{6,4},{7,5},{8,10},{9,11},{10,... | collective-permute-start | bytes 393224 | tf_op jit(solution)/shard_map/ppermute | solution.py:678
  233.2 13.4 %collective-permute-start.22 = (bf16[64,1024]{1,0:T(8,128)(2,1)}, bf16[64,1024]{1,0:T(8,128)(2,1)}, u32[]{:S(2)}, u32[]{:S(2)}) collective-permute-start(bf16[64,1024]{1,0:T(8,128)(2,1)} %get-tuple-element.124), channel_id=1, source_target_pairs={{0,3},{1,2},{2,1},{3,0},{4,7},{5,6},{6,5},{7,4},{8,11},{9,10},{10,... | collective-permute-start | bytes 393224 | tf_op jit(solution)/shard_map/ppermute | solution.py:678
  245.0 50.4 %collective-permute-start.19 = (bf16[4,192,768]{2,1,0:T(8,128)(2,1)}, bf16[4,192,768]{2,1,0:T(8,128)(2,1)}, u32[]{:S(2)}, u32[]{:S(2)}) collective-permute-start(bf16[4,192,768]{2,1,0:T(8,128)(2,1)} %dynamic-slice_bitcast_fusion), channel_id=1, source_target_pairs={{0,4},{4,0},{8,12},{12,8},{16,20},{20,16},{24,28},{28,24},{1,5},{5... | collective-permute-start | bytes 3538952 | tf_op jit(solution)/shard_map/ppermute | solution.py:569
  254.9 13.0 %collective-permute-start.26 = (bf16[2,256,1536]{2,1,0:T(8,128)(2,1)}, bf16[2,256,1536]{2,1,0:T(8,128)(2,1)}, u32[]{:S(2)}, u32[]{:S(2)}) collective-permute-start(bf16[2,256,1536]{2,1,0:T(8,128)(2,1)} %select_bitcast_fusion), channel_id=1, source_target_pairs={{0,1},{1,0},{2,3},{3,2},{4,5},{5,4},{6,7},{7,6},{8,9},{9,8},{10,11... | collective-permute-start | bytes 4718600 | tf_op jit(solution)/shard_map/ppermute | solution.py:511
  267.3 27.1 %collective-permute-start.23 = (bf16[4,192,128]{2,1,0:T(8,128)(2,1)}, bf16[4,192,128]{2,1,0:T(8,128)(2,1)}, u32[]{:S(2)}, u32[]{:S(2)}) collective-permute-start(bf16[4,192,128]{2,1,0:T(8,128)(2,1)} %dynamic-slice_bitcast_fusion.5), channel_id=1, source_target_pairs={{0,4},{4,0},{8,12},{12,8},{16,20},{20,16},{24,28},{28,24},{1,5},{5... | collective-permute-start | bytes 589832 | tf_op jit(solution)/shard_map/ppermute | solution.py:569
  272.7 21.7 %copy-start.20 = (bf16[1536,128]{1,0:T(8,128)(2,1)S(1)}, bf16[1536,128]{1,0:T(8,128)(2,1)}, u32[]{:S(2)}) copy-start(bf16[1536,128]{1,0:T(8,128)(2,1)} %copy-done.19) | copy-start | bytes 1179652
  272.7 24.9 %collective-permute-start.27 = (bf16[1,256,1536]{2,1,0:T(8,128)(2,1)}, bf16[1,256,1536]{2,1,0:T(8,128)(2,1)}, u32[]{:S(2)}, u32[]{:S(2)}) collective-permute-start(bf16[1,256,1536]{2,1,0:T(8,128)(2,1)} %fusion.27), channel_id=1, source_target_pairs={{0,2},{1,3},{2,0},{3,1},{4,6},{5,7},{6,4},{7,5},{8,10},{9,11},{10,... | collective-permute-start | bytes 2359304 | tf_op jit(solution)/shard_map/ppermute | solution.py:511
  283.4 4.8 %collective-permute-start.24 = (f32[6500]{0:T(1024)S(1)}, f32[6500]{0:T(1024)S(1)}, u32[]{:S(2)}, u32[]{:S(2)}) collective-permute-start(f32[6500]{0:T(1024)S(1)} %concatenate.182), channel_id=1, source_target_pairs={{0,16},{4,20},{8,24},{12,28},{16,0},{20,4},{24,8},{28,12},{1,17},{... | collective-permute-start | bytes 78008 | tf_op jit(solution)/shard_map/ppermute | solution.py:569
  288.1 6.2 %collective-permute-start.25 = (f32[6500]{0:T(1024)S(1)}, f32[6500]{0:T(1024)S(1)}, u32[]{:S(2)}, u32[]{:S(2)}) collective-permute-start(f32[6500]{0:T(1024)S(1)} %add.299), channel_id=1, source_target_pairs={{0,8},{4,12},{8,0},{12,4},{16,24},{20,28},{24,16},{28,20},{1,9},{5... | collective-permute-start | bytes 78008 | tf_op jit(solution)/shard_map/ppermute | solution.py:569
  301.2 3.9 %collective-permute-start.28 = (f32[6500]{0:T(1024)S(1)}, f32[6500]{0:T(1024)S(1)}, u32[]{:S(2)}, u32[]{:S(2)}) collective-permute-start(f32[6500]{0:T(1024)S(1)} %add.300), channel_id=1, source_target_pairs={{0,4},{4,0},{8,12},{12,8},{16,20},{20,16},{24,28},{28,24},{1,5},{5... | collective-permute-start | bytes 78008 | tf_op jit(solution)/shard_map/ppermute | solution.py:569
  305.2 7.0 %collective-permute-start.29 = (f32[1,1,6500]{2,1,0:T(1,128)S(1)}, f32[1,1,6500]{2,1,0:T(1,128)S(1)}, u32[]{:S(2)}, u32[]{:S(2)}) collective-permute-start(f32[1,1,6500]{2,1,0:T(1,128)S(1)} %broadcast_in_dim_broadcast_in_dim.3), channel_id=1, source_target_pairs={{0,2},{1,3},{2,0},{3,1},{4,6},{5,7},{6,4},{7,5},{8,10},{9,11},{10,... | collective-permute-start | bytes 78008 | tf_op jit(solution)/shard_map/ppermute | solution.py:511
  307.8 21.6 %collective-permute-start.31 = (bf16[192,896]{1,0:T(8,128)(2,1)}, bf16[192,896]{1,0:T(8,128)(2,1)}, u32[]{:S(2)}, u32[]{:S(2)}) collective-permute-start(bf16[192,896]{1,0:T(8,128)(2,1)} %get-tuple-element.121), channel_id=1, source_target_pairs={{0,8},{4,12},{8,0},{12,4},{16,24},{20,28},{24,16},{28,20},{1,9},{5... | collective-permute-start | bytes 1032200 | tf_op jit(solution)/shard_map/ppermute | solution.py:569
  307.8 26.9 %collective-permute-start.32 = (bf16[192,896]{1,0:T(8,128)(2,1)}, bf16[192,896]{1,0:T(8,128)(2,1)}, u32[]{:S(2)}, u32[]{:S(2)}) collective-permute-start(bf16[192,896]{1,0:T(8,128)(2,1)} %get-tuple-element.120), channel_id=1, source_target_pairs={{0,16},{4,20},{8,24},{12,28},{16,0},{20,4},{24,8},{28,12},{1,17},{... | collective-permute-start | bytes 1032200 | tf_op jit(solution)/shard_map/ppermute | solution.py:569
  310.6 24.1 %collective-permute-start.33 = (bf16[192,896]{1,0:T(8,128)(2,1)S(1)}, bf16[192,896]{1,0:T(8,128)(2,1)}, u32[]{:S(2)}, u32[]{:S(2)}) collective-permute-start(bf16[192,896]{1,0:T(8,128)(2,1)S(1)} %get-tuple-element.119), channel_id=1, source_target_pairs={{0,24},{4,28},{8,16},{12,20},{16,8},{20,12},{24,0},{28,4},{1,25},{... | collective-permute-start | bytes 1032200 | tf_op jit(solution)/shard_map/ppermute | solution.py:569
  312.3 1.3 collective-permute-start.30
  314.1 1.3 collective-permute-start.34
  315.5 7.0 %collective-permute-start.35 = (bf16[1,48,768]{2,1,0:T(8,128)(2,1)S(1)}, bf16[1,48,768]{2,1,0:T(8,128)(2,1)S(1)}, u32[]{:S(2)}, u32[]{:S(2)}) collective-permute-start(bf16[1,48,768]{2,1,0:T(8,128)(2,1)S(1)} %get-tuple-element.136), channel_id=1, source_target_pairs={{0,2},{1,3},{2,0},{3,1},{4,6},{5,7},{6,4},{7,5},{8,10},{9,11},{10,... | collective-permute-start | bytes 221192 | tf_op jit(solution)/shard_map/ppermute | solution.py:652
  319.6 9.0 %collective-permute-start.37 = (bf16[96,1536]{1,0:T(8,128)(2,1)S(1)}, bf16[96,1536]{1,0:T(8,128)(2,1)S(1)}, u32[]{:S(2)}, u32[]{:S(2)}) collective-permute-start(bf16[96,1536]{1,0:T(8,128)(2,1)S(1)} %bitcast.265), channel_id=1, source_target_pairs={{0,0},{4,1},{8,2},{12,3},{1,4},{5,5},{9,6},{13,7},{2,8},{6,9},{10,... | collective-permute-start | bytes 884744 | tf_op jit(solution)/shard_map/ppermute | solution.py:879
  322.5 6.0 %collective-permute-start.36 = (bf16[1,48,768]{2,1,0:T(8,128)(2,1)S(1)}, bf16[1,48,768]{2,1,0:T(8,128)(2,1)S(1)}, u32[]{:S(2)}, u32[]{:S(2)}) collective-permute-start(bf16[1,48,768]{2,1,0:T(8,128)(2,1)S(1)} %get-tuple-element.135), channel_id=1, source_target_pairs={{0,3},{1,2},{2,1},{3,0},{4,7},{5,6},{6,5},{7,4},{8,11},{9,10},{10,... | collective-permute-start | bytes 221192 | tf_op jit(solution)/shard_map/ppermute | solution.py:652
  336.1 1.3 collective-permute-start.38
  337.5 9.5 %collective-permute-start.39 = (bf16[1,48,896]{2,1,0:T(8,128)(2,1)S(1)}, bf16[1,48,896]{2,1,0:T(8,128)(2,1)S(1)}, u32[]{:S(2)}, u32[]{:S(2)}) collective-permute-start(bf16[1,48,896]{2,1,0:T(8,128)(2,1)S(1)} %get-tuple-element.133), channel_id=1, source_target_pairs={{0,2},{1,3},{2,0},{3,1},{4,6},{5,7},{6,4},{7,5},{8,10},{9,11},{10,... | collective-permute-start | bytes 258056 | tf_op jit(solution)/shard_map/ppermute | solution.py:652
  345.8 4.8 %collective-permute-start.40 = (bf16[1,48,896]{2,1,0:T(8,128)(2,1)S(1)}, bf16[1,48,896]{2,1,0:T(8,128)(2,1)S(1)}, u32[]{:S(2)}, u32[]{:S(2)}) collective-permute-start(bf16[1,48,896]{2,1,0:T(8,128)(2,1)S(1)} %get-tuple-element.132), channel_id=1, source_target_pairs={{0,3},{1,2},{2,1},{3,0},{4,7},{5,6},{6,5},{7,4},{8,11},{9,10},{10,... | collective-permute-start | bytes 258056 | tf_op jit(solution)/shard_map/ppermute | solution.py:652
  (53 other events, 242.4 us)
Sparse Core Ops, SparseCore 0:
  70.9 83.9 all-gather.1
  193.2 105.9 reduce-scatter.2
  301.7 42.6 reduce-scatter.4

commit v4 on v3

--- a/solution.py
+++ b/solution.py
@@ -569,7 +569,7 @@
     return lax.ppermute(block, "dp", [(i, i ^ bits) for i in range(lax.axis_size("dp"))])
 
 
-def gathered_rows(block, waits):
+def gathered_rows(block, waits, whole_rows):
     count = lax.axis_size("dp")
     length = count // 2
     if not is_small(count):
@@ -577,7 +577,6 @@
     at = lax.axis_index("dp")
     place, side = at // 2, at % 2
     rows = block.shape[0]
-    whole_rows = jnp.zeros((count * rows, block.shape[1]), block.dtype)
 
     def put(into, piece, pair, half):
         return lax.dynamic_update_slice(into, piece, ((pair * 2 + half) * rows, 0))
@@ -756,13 +755,15 @@
     dcol = jnp.broadcast_to(docs[:, None], (tokens, LANES))
     drow = jnp.broadcast_to(docs[None, :], (8, tokens))
     early = (docs, out_moved, conv_x, bias_x, gain, sb, rate, skip, dcol, drow)
-    mine, normed_own = lax.optimization_barrier((after(mine, early), normed_own))
+    n_first = own_inner + LANES
+    cleared = jnp.zeros((groups * size * in_rows, n_first), bf16)
+    mine, normed_own, cleared = lax.optimization_barrier((after(mine, early), normed_own, cleared))
     mine = mine.reshape(size * in_rows, -1)
     n_first = own_inner + LANES
     cot_own = cotangent.reshape(block, n_width)
     normed_held = opened(normed_own)
     cot_held = opened(after(cot_own, mine))
-    w_first, hopped = gathered_rows(mine[:, :n_first], [normed_held, cot_held])
+    w_first, hopped = gathered_rows(mine[:, :n_first], [normed_held, cot_held], cleared)
     z_block = jnp.concatenate([mine[:, n_first:], folded(out_moved, 1, own_inner)], axis=0)
 
     normed = gathered(normed_own, normed_held)
@@ -872,30 +873,35 @@
     d_norm = lax.psum_scatter(d_norm, "seq", scatter_dimension=0, tiled=True).astype(f32)
 
     def own_rows(part):
-        out = turned(part.reshape(size, in_rows, -1))
-        return out.transpose(1, 0, 2).astype(f32)
+        return turned(part.reshape(size, in_rows, -1))
+
+    def placed(rows, cuts=runs):
+        wide = rows.shape[2] // cuts
+        spots = [(run * wide, owner) for run in range(cuts) for owner in range(size)]
+        pieces = [rows[owner, :, at : at + wide] for at, owner in spots]
+        return jnp.concatenate(pieces, axis=1).astype(f32)
 
     out_part = unfolded(parts[None, z_rows:], n_width)
     d_out_weight = lax.ppermute(out_part, ("dp", "seq"), back).astype(f32)
-    in_z = own_rows(parts[:z_rows])
+    in_z = placed(own_rows(parts[:z_rows]))
     shares, in_z, d_out_weight = lax.optimization_barrier((shares, in_z, d_out_weight))
     first_part = sum(share.astype(f32) for share in shares)
     in_first = own_rows(first_part.astype(bf16))
-    d_in_weight = jnp.concatenate(
-        [
-            undealt(in_z),
-            undealt(in_first[:, :, :own_inner]),
-            in_first[:, :, n_first - own_bc :].reshape(in_rows, 2 * n_state),
-            undealt(in_first[:, :, own_inner : own_inner + own_heads]),
-        ],
-        axis=1,
-    )
-
     lifted = d_norm * norm_gain
     d_flat = inv * lifted - flat * (
         inv * inv * inv * jnp.mean(lifted * flat, axis=-1, keepdims=True)
     )
     d_hidden = (cot_own.astype(f32) + d_flat).reshape(n_seqs, block, n_width)
+    in_first, d_hidden = lax.optimization_barrier((in_first, d_hidden))
+    d_in_weight = jnp.concatenate(
+        [
+            in_z,
+            placed(in_first[:, :, :own_inner]),
+            placed(in_first[:, :, n_first - own_bc :], 1),
+            placed(in_first[:, :, own_inner : own_inner + own_heads]),
+        ],
+        axis=1,
+    )
 
     at = 0
 

time: 374 us -> 366 us (0.979)
  waiting for transfers between devices: 79 us -> 91.9 us
  local copies, waits for them, and re-layouts: 56.2 us -> 44.1 us
  starting transfers between devices: 60.3 us -> 55 us
  matrix products: 29.2 us -> 33.4 us
  other arithmetic: 46.2 us -> 42.3 us
    ppermute x12, waiting for transfers between devices: 11.3 us -> 18.9 us  [swapped(): return lax.ppermute(block, 'seq', [(i, i ^ bit) for i in range(size)])]
    ppermute x12, waiting for transfers between devices: 34.5 us -> 27 us  [crossed(): lax.ppermute(block, 'dp', [(i, i ^ bits) for i in range(lax.axis_size('dp...]
    reduce_scatter x1, waiting for transfers between devices: 0.01 us -> 6.63 us  [shards(): lax.psum_scatter(d_norm, 'seq', scatter_dimension=0, tiled=True).astype(f32)]
    ppermute x6, waiting for transfers between devices: 12 us -> 18.5 us  [turned(): piece = lax.ppermute(piece, 'seq', [(i, i ^ bits) for i in range(size)])]
    dot_general x7, matrix products: 29.2 us -> 33.4 us  [mm(): return lax.dot_general(a, b, (dims, ((), ())), preferred_element_type=out)]
  transfers between devices with their start and end apart: 45 -> 45, of which waited for: 21 -> 21; matrix products, arithmetic and copies ran while one was open for 33% -> 30% of each run, Pallas kernels for 12% -> 12%
where the time goes in v4:
time: 366 us; the launch traced here: 363 us
  waiting for transfers between devices  91.9 us (25%)
  Pallas kernels  75.3 us (21%)
  starting transfers between devices  55 us (15%)
  local copies, waits for them, and re-layouts  44.1 us (12%)
  other arithmetic  42.3 us (12%)
  matrix products  33.4 us (9%)
  between operations  15.2 us (4%)
  blocking collectives  5.73 us (2%)
    dot_general x7, matrix products, mm(): return lax.dot_general(a, b, (dims, ((), ())), preferred_element_type=out)  33.4 us
    pallas_call x1, Pallas kernels, run_backward(): pl.pallas_call(functools.partial(scan_backward, q, taps, pairs, head, chu...  30.8 us
    ppermute x12, waiting for transfers between devices, crossed(): lax.ppermute(block, 'dp', [(i, i ^ bits) for i in range(lax.axis_size('dp...  27 us
    ppermute x6, starting transfers between devices, moved_by(): return lax.ppermute(block, 'dp', route)  19.3 us
    ppermute x12, waiting for transfers between devices, swapped(): return lax.ppermute(block, 'seq', [(i, i ^ bit) for i in range(size)])  18.9 us
    pallas_call x1, Pallas kernels, run_gate_backward(): pl.pallas_call(functools.partial(gate_backward, blocks, tile, z_rows, tal...  18.8 us
    ppermute x6, waiting for transfers between devices, turned(): piece = lax.ppermute(piece, 'seq', [(i, i ^ bits) for i in range(size)])  18.5 us
    pallas_call x1, Pallas kernels, run_forward(): pl.pallas_call(functools.partial(scan_forward, q, taps, pairs, head), gri...  13.4 us
  transfers between devices with their start and end apart: 45, of which 21 were waited for; matrix products, arithmetic and copies ran while one was open for 30% of the time, Pallas kernels for 12%

profile of v4, /device:TPU:2, one launch (start us, length us, event | category | flops | bytes accessed | tf_op | source)
XLA Modules:
  0.0 362.9 jit_solution(7861162126394595181)
XLA Ops:
  12.9 3.6 all-to-all-start
  16.7 2.5 collective-permute-start.2
  25.6 5.3 %all-to-all-done = bf16[4,48,1664]{2,1,0:T(8,128)(2,1)S(1)} async-done(((bf16[4,48,1664]{2,1,0:T(8,128)(2,1)}), bf16[4,48,1664]{2,1,0:T(8,128)(2,1)S(1)}, u32[]{:S(2)}, u32[]{:S(2)}) %all-to-all-start) | async-done | bytes 639008 | tf_op jit(solution)/shard_map/all_to_all | solution.py:736
  32.5 2.4 collective-permute-start.3
  39.2 5.8 %collective-permute-start.8 = (bf16[192,896]{1,0:T(8,128)(2,1)}, bf16[192,896]{1,0:T(8,128)(2,1)}, u32[]{:S(2)}, u32[]{:S(2)}) collective-permute-start(bf16[192,896]{1,0:T(8,128)(2,1)} %get-tuple-element.132), channel_id=1, source_target_pairs={{0,8},{4,12},{8,16},{12,20},{16,24},{20,28},{1,9},{5,13},{9,17},{1... | collective-permute-start | bytes 1032200 | tf_op jit(solution)/shard_map/ppermute | solution.py:565
  49.2 4.1 %collective-permute-done.3 = bf16[1,256,1536]{2,1,0:T(8,128)(2,1)S(1)} collective-permute-done((bf16[1,256,1536]{2,1,0:T(8,128)(2,1)S(1)}, bf16[1,256,1536]{2,1,0:T(8,128)(2,1)S(1)}, u32[]{:S(2)}, u32[]{:S(2)}) %collective-permute-start.3) | collective-permute-done | bytes 786464 | tf_op jit(solution)/shard_map/ppermute | solution.py:511
  55.6 4.2 %collective-permute-start.11 = (bf16[192,896]{1,0:T(8,128)(2,1)}, bf16[192,896]{1,0:T(8,128)(2,1)S(1)}, u32[]{:S(2)}, u32[]{:S(2)}) collective-permute-start(bf16[192,896]{1,0:T(8,128)(2,1)} %collective-permute-done.8), channel_id=1, source_target_pairs={{0,8},{4,12},{8,16},{12,20},{16,24},{20,28},{1,9},{5,13},{9,17},{1... | collective-permute-start | bytes 1032200 | tf_op jit(solution)/shard_map/ppermute | solution.py:565
  61.1 2.0 constant_dynamic-update-slice_fusion.29
  64.5 4.9 %collective-permute-done.5 = bf16[1,256,1536]{2,1,0:T(8,128)(2,1)S(1)} collective-permute-done((bf16[1,256,1536]{2,1,0:T(8,128)(2,1)S(1)}, bf16[1,256,1536]{2,1,0:T(8,128)(2,1)S(1)}, u32[]{:S(2)}, u32[]{:S(2)}) %collective-permute-start.5) | collective-permute-done | bytes 786464 | tf_op jit(solution)/shard_map/ppermute | solution.py:511
  71.0 5.2 %collective-permute-start.14 = (bf16[192,896]{1,0:T(8,128)(2,1)S(1)}, bf16[192,896]{1,0:T(8,128)(2,1)}, u32[]{:S(2)}, u32[]{:S(2)}) collective-permute-start(bf16[192,896]{1,0:T(8,128)(2,1)S(1)} %collective-permute-done.11), channel_id=1, source_target_pairs={{0,8},{4,12},{8,16},{12,20},{16,24},{20,28},{1,9},{5,13},{9,17},{1... | collective-permute-start | bytes 1032200 | tf_op jit(solution)/shard_map/ppermute | solution.py:565
  77.7 1.8 constant_dynamic-update-slice_fusion.28
  79.5 2.1 constant_dynamic-update-slice_fusion.27
  83.9 12.4 %collective-permute-done.13 = bf16[192,896]{1,0:T(8,128)(2,1)} collective-permute-done((bf16[192,896]{1,0:T(8,128)(2,1)}, bf16[192,896]{1,0:T(8,128)(2,1)}, u32[]{:S(2)}, u32[]{:S(2)}) %collective-permute-start.13) | collective-permute-done | bytes 344096 | tf_op jit(solution)/shard_map/ppermute | solution.py:569
  96.3 2.8 collective-permute-done.15
  99.1 1.7 constant_dynamic-update-slice_fusion.26
  100.8 1.9 constant_dynamic-update-slice_fusion.25
  103.7 6.2 %collective-permute-done.16 = bf16[192,896]{1,0:T(8,128)(2,1)S(1)} collective-permute-done((bf16[192,896]{1,0:T(8,128)(2,1)S(1)}, bf16[192,896]{1,0:T(8,128)(2,1)S(1)}, u32[]{:S(2)}, u32[]{:S(2)}) %collective-permute-start.16) | collective-permute-done | bytes 344096 | tf_op jit(solution)/shard_map/ppermute | solution.py:569
  110.7 2.5 maximum_select_fusion
  113.5 2.6 fusion.28
  119.4 5.3 %fusion.16.x_ref.xp_ref = bf16[1024,768]{1,0:T(8,128)(2,1)} fusion(bf16[1024,1536]{1,0:T(8,128)(2,1)S(1)} %bitcast.276, bf16[1536,896]{1,0:T(8,128)(2,1)} %constant_dynamic-update-slice_fusion.24), kind=kOutput, calls=%fused_computation.28 | convolution fusion | flops 2416705536 | bytes 7077888 | tf_op jit(solution)/shard_map/dot_general | solution.py:21
  124.8 1.9 maximum_select_fusion.1
  130.7 13.4 %scan_forward.1 = (f32[1024,768]{1,0:T(8,128)}, f32[8,128,768]{2,1,0:T(8,128)}) custom-call(bf16[1024,768]{1,0:T(8,128)(2,1)} %fusion.16.x_ref.xp_ref, f32[1024,128]{1,0:T(8,128)} %broadcast_select_fusion.1.small_ref, bf16[256,1024]{1,0:T(8,128)(2,1)} %bitcast.289, f32[1024,128]{1,0:T(8,128)} %broadcast_in_dim.75.dcol_ref.dcolp_ref, ...), custom_call_target="tpu_custom_call" | custom-call | tf_op jit(solution)/shard_map/scan_forward/pallas_call | solution.py:271
  144.2 10.8 %all-gather.2.cloned.1.call-done = bf16[3072,768]{1,0:T(8,128)(2,1)} async-done(((bf16[384,768]{1,0:T(8,128)(2,1)}), bf16[3072,768]{1,0:T(8,128)(2,1)}) %all-gather.2.cloned.1.call-update) | async-done | bytes 4718608 | tf_op jit(solution)/shard_map/all_gather | solution.py:770
  154.9 12.2 %gate_forward.1 = (f32[1024,768]{1,0:T(8,128)}, f32[1024,768]{1,0:T(8,128)}, f32[8,1024]{1,0:T(8,128)}, bf16[1536,768]{1,0:T(8,128)(2,1)}, bf16[2,768,768]{2,1,0:T(8,128)(2,1)}) custom-call(bf16[1024,1536]{1,0:T(8,128)(2,1)} %bitcast.277, bf16[1024,1536]{1,0:T(8,128)(2,1)} %bitcast.281, bf16[8,384,768]{2,1,0:T(8,128)(2,1)} %bitcast.292, ...), custom_call_target="tpu_custom_call" | custom-call | tf_op jit(solution)/shard_map/gate_forward/pallas_call | solution.py:452
  167.9 5.7 %psum.7 = f32[2,1024]{1,0:T(2,128)S(1)} all-reduce(f32[2,1024]{1,0:T(2,128)S(1)} %slice.314), channel_id=1, replica_groups=mesh['dp'=8,'seq'=4] {'seq'}, use_global_device_ids=true, to_apply=%region_1.2 | all-reduce | flops 2048 | bytes 16384 | tf_op jit(solution)/shard_map/psum | solution.py:818
  174.3 18.8 %gate_backward.1 = (bf16[1024,768]{1,0:T(8,128)(2,1)}, bf16[1024,768]{1,0:T(8,128)(2,1)}, f32[1024,768]{1,0:T(8,128)}, f32[8,768]{1,0:T(8,128)}, bf16[8,384,768]{2,1,0:T(8,128)(2,1)}) custom-call(bf16[1024,1536]{1,0:T(8,128)(2,1)} %bitcast.278, bf16[1024,1536]{1,0:T(8,128)(2,1)} %bitcast.282, f32[1024,768]{1,0:T(8,128)} %get-tuple-element.68.y_ref, ...), custom_call_target="tpu_custom_call" | custom-call | tf_op jit(solution)/shard_map/gate_backward/pallas_call | solution.py:484
  193.5 30.8 %scan_backward.1 = (bf16[1024,768]{1,0:T(8,128)(2,1)}, f32[1024,128]{1,0:T(8,128)}, f32[256,1024]{1,0:T(8,128)}, f32[8,768]{1,0:T(8,128)}, f32[8,128]{1,0:T(8,128)}) custom-call(bf16[1024,768]{1,0:T(8,128)(2,1)} %fusion.16.x_ref.xp_ref, bf16[1024,768]{1,0:T(8,128)(2,1)} %fusion.16.x_ref.xp_ref, f32[1024,128]{1,0:T(8,128)} %broadcast_select_fusion.1.small_ref, ...), custom_call_target="tpu_custom_call" | custom-call | tf_op jit(solution)/shard_map/scan_backward/pallas_call | solution.py:316
  224.3 5.4 %convolution_convert_fusion.1 = bf16[1536,768]{1,0:T(8,128)(2,1)} fusion(bf16[1024,1536]{1,0:T(8,128)(2,1)S(1)} %bitcast.279, bf16[1024,768]{1,0:T(8,128)(2,1)} %get-tuple-element.76), kind=kOutput, calls=%fused_computation.3 | convolution fusion | flops 2417098752 | bytes 7077888 | tf_op jit(solution)/shard_map/dot_general | solution.py:21
  229.7 1.9 fusion.45
  231.6 1.8 collective-permute-start.21
  233.5 1.9 copy.70
  242.5 2.5 dynamic-slice_bitcast_fusion
  247.7 6.2 %fusion.70 = f32[1024,1536]{1,0:T(8,128)} fusion(bf16[1024,768]{1,0:T(8,128)(2,1)} %get-tuple-element.84, bf16[1536,768]{1,0:T(8,128)(2,1)S(1)} %copy-done.47), kind=kOutput, calls=%fused_computation.228 | convolution fusion | flops 2415919104 | bytes 10223616 | tf_op jit(solution)/shard_map/dot_general | solution.py:21
  255.6 2.1 multiply_reduce_fusion.1
  257.8 3.2 convolution_convert_fusion
  265.4 9.6 %fusion.65 = (bf16[1024,1536]{1,0:T(8,128)(2,1)}, f32[1536]{0:T(1024)S(1)}) fusion(bf16[2,2,256,1536]{3,2,1,0:T(8,128)(2,1)S(1)} %copy-done.1, f32[1024,1536]{1,0:T(8,128)} %fusion.70, bf16[1536,896]{1,0:T(8,128)(2,1)} %constant_dynamic-update-slice_fusion.24, bf16[1024,64]{1,0:T(8,128)(2,1)} %copy.73, bf16[1024,64]{1,0:T(8,128)(2,1)} %copy.72, ...), kind=kOutput, calls=%fused_computation.223 | convolution fusion | flops 2831940096 | bytes 17176576 | tf_op jit(solution)/shard_map/dot_general | solution.py:21
  278.0 4.7 %collective-permute-done.24 = f32[6500]{0:T(1024)S(1)} collective-permute-done((f32[6500]{0:T(1024)S(1)}, f32[6500]{0:T(1024)S(1)}, u32[]{:S(2)}, u32[]{:S(2)}) %collective-permute-start.24) | collective-permute-done | bytes 26032 | tf_op jit(solution)/shard_map/ppermute | solution.py:569
  283.4 3.5 collective-permute-done.25
  287.0 2.0 fusion
  295.3 2.1 collective-permute-start.29
  300.5 7.5 %collective-permute-done.27 = bf16[1,256,1536]{2,1,0:T(8,128)(2,1)S(1)} collective-permute-done((bf16[1,256,1536]{2,1,0:T(8,128)(2,1)S(1)}, bf16[1,256,1536]{2,1,0:T(8,128)(2,1)S(1)}, u32[]{:S(2)}, u32[]{:S(2)}) %collective-permute-start.27) | collective-permute-done | bytes 786464 | tf_op jit(solution)/shard_map/ppermute | solution.py:511
  312.7 1.8 collective-permute-start.32
  318.2 2.0 collective-permute-start.34
  320.7 9.3 %collective-permute-done.33 = bf16[1,48,768]{2,1,0:T(8,128)(2,1)S(1)} collective-permute-done((bf16[1,48,768]{2,1,0:T(8,128)(2,1)S(1)}, bf16[1,48,768]{2,1,0:T(8,128)(2,1)S(1)}, u32[]{:S(2)}, u32[]{:S(2)}) %collective-permute-start.33) | collective-permute-done | bytes 73760 | tf_op jit(solution)/shard_map/ppermute | solution.py:651
  333.9 2.5 collective-permute-start.36
  337.1 4.5 %collective-permute-done.36 = bf16[1,48,896]{2,1,0:T(8,128)(2,1)S(1)} collective-permute-done((bf16[1,48,896]{2,1,0:T(8,128)(2,1)S(1)}, bf16[1,48,896]{2,1,0:T(8,128)(2,1)S(1)}, u32[]{:S(2)}, u32[]{:S(2)}) %collective-permute-start.36) | collective-permute-done | bytes 86048 | tf_op jit(solution)/shard_map/ppermute | solution.py:651
  341.6 3.2 collective-permute-done.37
  344.9 6.6 %reduce-scatter.5.cloned.1.call-done = bf16[256,1536]{1,0:T(8,128)(2,1)} async-done(((bf16[1024,1536]{1,0:T(8,128)(2,1)}), bf16[256,1536]{1,0:T(8,128)(2,1)}) %reduce-scatter.5.cloned.1.call-update) | async-done | bytes 786448 | tf_op jit(solution)/shard_map/reduce_scatter | solution.py:873
  (342 shorter events, 90.1 us)
Async XLA Ops:
  7.2 16.2 %collective-permute-start = (s32[1,1,256]{2,1,0:T(1,128)}, s32[1,1,256]{2,1,0:T(1,128)S(1)}, u32[]{:S(2)}, u32[]{:S(2)}) collective-permute-start(s32[1,1,256]{2,1,0:T(1,128)} %bitcast.336), channel_id=1, source_target_pairs={{0,2},{1,3},{2,0},{3,1},{4,6},{5,7},{6,4},{7,5},{8,10},{9,11},{10,... | collective-permute-start | bytes 3080 | tf_op jit(solution)/shard_map/ppermute | solution.py:511
  12.9 18.0 %all-to-all-start = ((bf16[4,48,1664]{2,1,0:T(8,128)(2,1)}), bf16[4,48,1664]{2,1,0:T(8,128)(2,1)S(1)}, u32[]{:S(2)}, u32[]{:S(2)}) async-start(bf16[4,48,1664]{2,1,0:T(8,128)(2,1)} %bitcast.4), calls=%async_computation | async-start | bytes 1277952 | tf_op jit(solution)/shard_map/all_to_all | solution.py:736
  16.6 138.3 %all-gather.2.cloned.1.call-start = ((), (), s32[]{:S(2)}) async-start(), calls=%async_computation.3 | async-start | bytes 5308416 | tf_op jit(solution)/shard_map/all_gather | solution.py:770
  16.7 8.9 %collective-permute-start.2 = (bf16[96,1536]{1,0:T(8,128)(2,1)S(1)}, bf16[96,1536]{1,0:T(8,128)(2,1)S(1)}, u32[]{:S(2)}, u32[]{:S(2)}) collective-permute-start(bf16[96,1536]{1,0:T(8,128)(2,1)S(1)} %convert_element_type.199), channel_id=1, source_target_pairs={{0,0},{1,4},{2,8},{3,12},{4,1},{5,5},{6,9},{7,13},{8,2},{9,6},{10,... | collective-permute-start | bytes 884744 | tf_op jit(solution)/shard_map/ppermute | solution.py:748
  23.3 1.2 collective-permute-start.1
  32.5 20.8 %collective-permute-start.3 = (bf16[1,256,1536]{2,1,0:T(8,128)(2,1)S(1)}, bf16[1,256,1536]{2,1,0:T(8,128)(2,1)S(1)}, u32[]{:S(2)}, u32[]{:S(2)}) collective-permute-start(bf16[1,256,1536]{2,1,0:T(8,128)(2,1)S(1)} %bitcast.286), channel_id=1, source_target_pairs={{0,2},{1,3},{2,0},{3,1},{4,6},{5,7},{6,4},{7,5},{8,10},{9,11},{10,... | collective-permute-start | bytes 2359304 | tf_op jit(solution)/shard_map/ppermute | solution.py:511
  37.5 9.9 %collective-permute-start.7 = (bf16[192,896]{1,0:T(8,128)(2,1)}, bf16[192,896]{1,0:T(8,128)(2,1)}, u32[]{:S(2)}, u32[]{:S(2)}) collective-permute-start(bf16[192,896]{1,0:T(8,128)(2,1)} %get-tuple-element.132), channel_id=1, source_target_pairs={{0,4},{4,0},{8,12},{12,8},{16,20},{20,16},{24,28},{28,24},{1,5},{5... | collective-permute-start | bytes 1032200 | tf_op jit(solution)/shard_map/ppermute | solution.py:569
  38.1 31.3 %collective-permute-start.5 = (bf16[1,256,1536]{2,1,0:T(8,128)(2,1)S(1)}, bf16[1,256,1536]{2,1,0:T(8,128)(2,1)S(1)}, u32[]{:S(2)}, u32[]{:S(2)}) collective-permute-start(bf16[1,256,1536]{2,1,0:T(8,128)(2,1)S(1)} %copy-done.6), channel_id=1, source_target_pairs={{0,2},{1,3},{2,0},{3,1},{4,6},{5,7},{6,4},{7,5},{8,10},{9,11},{10,... | collective-permute-start | bytes 2359304 | tf_op jit(solution)/shard_map/ppermute | solution.py:511
  39.2 15.5 %collective-permute-start.8 = (bf16[192,896]{1,0:T(8,128)(2,1)}, bf16[192,896]{1,0:T(8,128)(2,1)}, u32[]{:S(2)}, u32[]{:S(2)}) collective-permute-start(bf16[192,896]{1,0:T(8,128)(2,1)} %get-tuple-element.132), channel_id=1, source_target_pairs={{0,8},{4,12},{8,16},{12,20},{16,24},{20,28},{1,9},{5,13},{9,17},{1... | collective-permute-start | bytes 1032200 | tf_op jit(solution)/shard_map/ppermute | solution.py:565
  45.0 10.6 %collective-permute-start.9 = (bf16[192,896]{1,0:T(8,128)(2,1)}, bf16[192,896]{1,0:T(8,128)(2,1)}, u32[]{:S(2)}, u32[]{:S(2)}) collective-permute-start(bf16[192,896]{1,0:T(8,128)(2,1)} %get-tuple-element.132), channel_id=1, source_target_pairs={{8,0},{12,4},{16,8},{20,12},{24,16},{28,20},{9,1},{13,5},{17,9},{2... | collective-permute-start | bytes 1032200 | tf_op jit(solution)/shard_map/ppermute | solution.py:565
  55.6 15.1 %collective-permute-start.11 = (bf16[192,896]{1,0:T(8,128)(2,1)}, bf16[192,896]{1,0:T(8,128)(2,1)S(1)}, u32[]{:S(2)}, u32[]{:S(2)}) collective-permute-start(bf16[192,896]{1,0:T(8,128)(2,1)} %collective-permute-done.8), channel_id=1, source_target_pairs={{0,8},{4,12},{8,16},{12,20},{16,24},{20,28},{1,9},{5,13},{9,17},{1... | collective-permute-start | bytes 1032200 | tf_op jit(solution)/shard_map/ppermute | solution.py:565
  59.8 11.0 %collective-permute-start.12 = (bf16[192,896]{1,0:T(8,128)(2,1)}, bf16[192,896]{1,0:T(8,128)(2,1)}, u32[]{:S(2)}, u32[]{:S(2)}) collective-permute-start(bf16[192,896]{1,0:T(8,128)(2,1)} %collective-permute-done.9), channel_id=1, source_target_pairs={{8,0},{12,4},{16,8},{20,12},{24,16},{28,20},{9,1},{13,5},{17,9},{2... | collective-permute-start | bytes 1032200 | tf_op jit(solution)/shard_map/ppermute | solution.py:565
  63.1 7.7 %collective-permute-start.10 = (bf16[192,896]{1,0:T(8,128)(2,1)}, bf16[192,896]{1,0:T(8,128)(2,1)}, u32[]{:S(2)}, u32[]{:S(2)}) collective-permute-start(bf16[192,896]{1,0:T(8,128)(2,1)} %get-tuple-element.120), channel_id=1, source_target_pairs={{0,4},{4,0},{8,12},{12,8},{16,20},{20,16},{24,28},{28,24},{1,5},{5... | collective-permute-start | bytes 1032200 | tf_op jit(solution)/shard_map/ppermute | solution.py:569
  70.8 238.6 %reduce-scatter.3.cloned.1.call-start = ((), (), s32[]{:S(2)}) async-start(), calls=%async_computation.4 | async-start | bytes 5308416 | tf_op jit(solution)/shard_map/reduce_scatter | solution.py:830
  71.0 39.8 %collective-permute-start.4 = (bf16[2,256,1536]{2,1,0:T(8,128)(2,1)}, bf16[2,256,1536]{2,1,0:T(8,128)(2,1)}, u32[]{:S(2)}, u32[]{:S(2)}) collective-permute-start(bf16[2,256,1536]{2,1,0:T(8,128)(2,1)} %maximum_select_fusion.2), channel_id=1, source_target_pairs={{0,1},{1,0},{2,3},{3,2},{4,5},{5,4},{6,7},{7,6},{8,9},{9,8},{10,11... | collective-permute-start | bytes 4718600 | tf_op jit(solution)/shard_map/ppermute | solution.py:511
  71.0 25.3 %collective-permute-start.14 = (bf16[192,896]{1,0:T(8,128)(2,1)S(1)}, bf16[192,896]{1,0:T(8,128)(2,1)}, u32[]{:S(2)}, u32[]{:S(2)}) collective-permute-start(bf16[192,896]{1,0:T(8,128)(2,1)S(1)} %collective-permute-done.11), channel_id=1, source_target_pairs={{0,8},{4,12},{8,16},{12,20},{16,24},{20,28},{1,9},{5,13},{9,17},{1... | collective-permute-start | bytes 1032200 | tf_op jit(solution)/shard_map/ppermute | solution.py:565
  76.2 22.9 %collective-permute-start.15 = (bf16[192,896]{1,0:T(8,128)(2,1)}, bf16[192,896]{1,0:T(8,128)(2,1)}, u32[]{:S(2)}, u32[]{:S(2)}) collective-permute-start(bf16[192,896]{1,0:T(8,128)(2,1)} %collective-permute-done.12), channel_id=1, source_target_pairs={{8,0},{12,4},{16,8},{20,12},{24,16},{28,20},{9,1},{13,5},{17,9},{2... | collective-permute-start | bytes 1032200 | tf_op jit(solution)/shard_map/ppermute | solution.py:565
  81.6 14.7 %collective-permute-start.13 = (bf16[192,896]{1,0:T(8,128)(2,1)}, bf16[192,896]{1,0:T(8,128)(2,1)}, u32[]{:S(2)}, u32[]{:S(2)}) collective-permute-start(bf16[192,896]{1,0:T(8,128)(2,1)} %get-tuple-element.118), channel_id=1, source_target_pairs={{0,4},{4,0},{8,12},{12,8},{16,20},{20,16},{24,28},{28,24},{1,5},{5... | collective-permute-start | bytes 1032200 | tf_op jit(solution)/shard_map/ppermute | solution.py:569
  83.9 33.1 %copy-start.20 = (f32[1024]{0:T(1024)}, f32[1024]{0:T(1024)S(1)}, u32[]{:S(2)}) copy-start(f32[1024]{0:T(1024)S(1)} %get-tuple-element.168) | copy-start | bytes 12292
  83.9 40.9 %collective-permute-start.6 = (bf16[2,256,1536]{2,1,0:T(8,128)(2,1)}, bf16[2,256,1536]{2,1,0:T(8,128)(2,1)S(1)}, u32[]{:S(2)}, u32[]{:S(2)}) collective-permute-start(bf16[2,256,1536]{2,1,0:T(8,128)(2,1)} %maximum_select_fusion.4), channel_id=1, source_target_pairs={{0,1},{1,0},{2,3},{3,2},{4,5},{5,4},{6,7},{7,6},{8,9},{9,8},{10,11... | collective-permute-start | bytes 4718600 | tf_op jit(solution)/shard_map/ppermute | solution.py:511
  102.7 7.2 %collective-permute-start.16 = (bf16[192,896]{1,0:T(8,128)(2,1)S(1)}, bf16[192,896]{1,0:T(8,128)(2,1)S(1)}, u32[]{:S(2)}, u32[]{:S(2)}) collective-permute-start(bf16[192,896]{1,0:T(8,128)(2,1)S(1)} %get-tuple-element.116), channel_id=1, source_target_pairs={{0,4},{4,0},{8,12},{12,8},{16,20},{20,16},{24,28},{28,24},{1,5},{5... | collective-permute-start | bytes 1032200 | tf_op jit(solution)/shard_map/ppermute | solution.py:569
  118.0 8.9 %collective-permute-start.17 = (bf16[1,64,1024]{2,1,0:T(8,128)(2,1)S(1)}, bf16[1,64,1024]{2,1,0:T(8,128)(2,1)}, u32[]{:S(2)}, u32[]{:S(2)}) collective-permute-start(bf16[1,64,1024]{2,1,0:T(8,128)(2,1)S(1)} %bitcast.304), channel_id=1, source_target_pairs={{0,2},{1,3},{2,0},{3,1},{4,6},{5,7},{6,4},{7,5},{8,10},{9,11},{10,... | collective-permute-start | bytes 393224 | tf_op jit(solution)/shard_map/ppermute | solution.py:511
  127.9 1.9 collective-permute-start.18
  193.1 158.4 %reduce-scatter.5.cloned.1.call-start = ((), (), s32[]{:S(2)}) async-start(), calls=%async_computation.5 | async-start | bytes 3932160 | tf_op jit(solution)/shard_map/reduce_scatter | solution.py:873
  193.5 30.8 %copy-start.1 = (bf16[2,2,256,1536]{3,2,1,0:T(8,128)(2,1)S(1)}, bf16[2,2,256,1536]{3,2,1,0:T(8,128)(2,1)}, u32[]{:S(2)}) copy-start(bf16[2,2,256,1536]{3,2,1,0:T(8,128)(2,1)} %copy-done) | copy-start | bytes 9437188
  231.6 24.0 %collective-permute-start.20 = (bf16[64,1024]{1,0:T(8,128)(2,1)}, bf16[64,1024]{1,0:T(8,128)(2,1)}, u32[]{:S(2)}, u32[]{:S(2)}) collective-permute-start(bf16[64,1024]{1,0:T(8,128)(2,1)} %get-tuple-element.129), channel_id=1, source_target_pairs={{0,1},{1,0},{2,3},{3,2},{4,5},{5,4},{6,7},{7,6},{8,9},{9,8},{10,11... | collective-permute-start | bytes 393224 | tf_op jit(solution)/shard_map/ppermute | solution.py:677
  231.6 24.0 %collective-permute-start.21 = (bf16[64,1024]{1,0:T(8,128)(2,1)}, bf16[64,1024]{1,0:T(8,128)(2,1)}, u32[]{:S(2)}, u32[]{:S(2)}) collective-permute-start(bf16[64,1024]{1,0:T(8,128)(2,1)} %get-tuple-element.131), channel_id=1, source_target_pairs={{0,2},{1,3},{2,0},{3,1},{4,6},{5,7},{6,4},{7,5},{8,10},{9,11},{10,... | collective-permute-start | bytes 393224 | tf_op jit(solution)/shard_map/ppermute | solution.py:677
  233.3 22.3 %collective-permute-start.22 = (bf16[64,1024]{1,0:T(8,128)(2,1)}, bf16[64,1024]{1,0:T(8,128)(2,1)}, u32[]{:S(2)}, u32[]{:S(2)}) collective-permute-start(bf16[64,1024]{1,0:T(8,128)(2,1)} %get-tuple-element.130), channel_id=1, source_target_pairs={{0,3},{1,2},{2,1},{3,0},{4,7},{5,6},{6,5},{7,4},{8,11},{9,10},{10,... | collective-permute-start | bytes 393224 | tf_op jit(solution)/shard_map/ppermute | solution.py:677
  245.0 45.9 %collective-permute-start.19 = (bf16[4,192,768]{2,1,0:T(8,128)(2,1)}, bf16[4,192,768]{2,1,0:T(8,128)(2,1)}, u32[]{:S(2)}, u32[]{:S(2)}) collective-permute-start(bf16[4,192,768]{2,1,0:T(8,128)(2,1)} %dynamic-slice_bitcast_fusion), channel_id=1, source_target_pairs={{0,4},{4,0},{8,12},{12,8},{16,20},{20,16},{24,28},{28,24},{1,5},{5... | collective-permute-start | bytes 3538952 | tf_op jit(solution)/shard_map/ppermute | solution.py:569
  263.1 23.9 %collective-permute-start.26 = (bf16[2,256,1536]{2,1,0:T(8,128)(2,1)}, bf16[2,256,1536]{2,1,0:T(8,128)(2,1)}, u32[]{:S(2)}, u32[]{:S(2)}) collective-permute-start(bf16[2,256,1536]{2,1,0:T(8,128)(2,1)} %select_bitcast_fusion), channel_id=1, source_target_pairs={{0,1},{1,0},{2,3},{3,2},{4,5},{5,4},{6,7},{7,6},{8,9},{9,8},{10,11... | collective-permute-start | bytes 4718600 | tf_op jit(solution)/shard_map/ppermute | solution.py:511
  275.2 7.5 %collective-permute-start.24 = (f32[6500]{0:T(1024)S(1)}, f32[6500]{0:T(1024)S(1)}, u32[]{:S(2)}, u32[]{:S(2)}) collective-permute-start(f32[6500]{0:T(1024)S(1)} %concatenate.194), channel_id=1, source_target_pairs={{0,16},{4,20},{8,24},{12,28},{16,0},{20,4},{24,8},{28,12},{1,17},{... | collective-permute-start | bytes 78008 | tf_op jit(solution)/shard_map/ppermute | solution.py:569
  282.7 4.2 %collective-permute-start.25 = (f32[6500]{0:T(1024)S(1)}, f32[6500]{0:T(1024)S(1)}, u32[]{:S(2)}, u32[]{:S(2)}) collective-permute-start(f32[6500]{0:T(1024)S(1)} %add.299), channel_id=1, source_target_pairs={{0,8},{4,12},{8,0},{12,4},{16,24},{20,28},{24,16},{28,20},{1,9},{5... | collective-permute-start | bytes 78008 | tf_op jit(solution)/shard_map/ppermute | solution.py:569
  282.8 8.0 %collective-permute-start.23 = (bf16[4,192,128]{2,1,0:T(8,128)(2,1)S(1)}, bf16[4,192,128]{2,1,0:T(8,128)(2,1)S(1)}, u32[]{:S(2)}, u32[]{:S(2)}) collective-permute-start(bf16[4,192,128]{2,1,0:T(8,128)(2,1)S(1)} %dynamic-slice_bitcast_fusion.5), channel_id=1, source_target_pairs={{0,4},{4,0},{8,12},{12,8},{16,20},{20,16},{24,28},{28,24},{1,5},{5... | collective-permute-start | bytes 589832 | tf_op jit(solution)/shard_map/ppermute | solution.py:569
  289.1 18.9 %collective-permute-start.27 = (bf16[1,256,1536]{2,1,0:T(8,128)(2,1)S(1)}, bf16[1,256,1536]{2,1,0:T(8,128)(2,1)S(1)}, u32[]{:S(2)}, u32[]{:S(2)}) collective-permute-start(bf16[1,256,1536]{2,1,0:T(8,128)(2,1)S(1)} %fusion.27), channel_id=1, source_target_pairs={{0,2},{1,3},{2,0},{3,1},{4,6},{5,7},{6,4},{7,5},{8,10},{9,11},{10,... | collective-permute-start | bytes 2359304 | tf_op jit(solution)/shard_map/ppermute | solution.py:511
  292.6 6.2 %collective-permute-start.38 = (f32[6500]{0:T(1024)S(1)}, f32[6500]{0:T(1024)S(1)}, u32[]{:S(2)}, u32[]{:S(2)}) collective-permute-start(f32[6500]{0:T(1024)S(1)} %add.300), channel_id=1, source_target_pairs={{0,4},{4,0},{8,12},{12,8},{16,20},{20,16},{24,28},{28,24},{1,5},{5... | collective-permute-start | bytes 78008 | tf_op jit(solution)/shard_map/ppermute | solution.py:569
  294.4 36.7 %collective-permute-start.28 = (bf16[192,896]{1,0:T(8,128)(2,1)}, bf16[192,896]{1,0:T(8,128)(2,1)}, u32[]{:S(2)}, u32[]{:S(2)}) collective-permute-start(bf16[192,896]{1,0:T(8,128)(2,1)} %get-tuple-element.127), channel_id=1, source_target_pairs={{0,8},{4,12},{8,0},{12,4},{16,24},{20,28},{24,16},{28,20},{1,9},{5... | collective-permute-start | bytes 1032200 | tf_op jit(solution)/shard_map/ppermute | solution.py:569
  295.3 35.7 %collective-permute-start.29 = (bf16[192,896]{1,0:T(8,128)(2,1)S(1)}, bf16[192,896]{1,0:T(8,128)(2,1)}, u32[]{:S(2)}, u32[]{:S(2)}) collective-permute-start(bf16[192,896]{1,0:T(8,128)(2,1)S(1)} %get-tuple-element.126), channel_id=1, source_target_pairs={{0,16},{4,20},{8,24},{12,28},{16,0},{20,4},{24,8},{28,12},{1,17},{... | collective-permute-start | bytes 1032200 | tf_op jit(solution)/shard_map/ppermute | solution.py:569
  297.4 33.6 %collective-permute-start.30 = (bf16[192,896]{1,0:T(8,128)(2,1)S(1)}, bf16[192,896]{1,0:T(8,128)(2,1)}, u32[]{:S(2)}, u32[]{:S(2)}) collective-permute-start(bf16[192,896]{1,0:T(8,128)(2,1)S(1)} %get-tuple-element.125), channel_id=1, source_target_pairs={{0,24},{4,28},{8,16},{12,20},{16,8},{20,12},{24,0},{28,4},{1,25},{... | collective-permute-start | bytes 1032200 | tf_op jit(solution)/shard_map/ppermute | solution.py:569
  298.9 10.6 %collective-permute-start.39 = (f32[1,1,6500]{2,1,0:T(1,128)S(1)}, f32[1,1,6500]{2,1,0:T(1,128)S(1)}, u32[]{:S(2)}, u32[]{:S(2)}) collective-permute-start(f32[1,1,6500]{2,1,0:T(1,128)S(1)} %broadcast_in_dim_broadcast_in_dim.3), channel_id=1, source_target_pairs={{0,2},{1,3},{2,0},{3,1},{4,6},{5,7},{6,4},{7,5},{8,10},{9,11},{10,... | collective-permute-start | bytes 78008 | tf_op jit(solution)/shard_map/ppermute | solution.py:511
  309.5 1.3 collective-permute-start.40
  311.4 1.3 collective-permute-start.31
  312.7 7.5 %collective-permute-start.32 = (bf16[1,48,768]{2,1,0:T(8,128)(2,1)S(1)}, bf16[1,48,768]{2,1,0:T(8,128)(2,1)S(1)}, u32[]{:S(2)}, u32[]{:S(2)}) collective-permute-start(bf16[1,48,768]{2,1,0:T(8,128)(2,1)S(1)} %get-tuple-element.154), channel_id=1, source_target_pairs={{0,2},{1,3},{2,0},{3,1},{4,6},{5,7},{6,4},{7,5},{8,10},{9,11},{10,... | collective-permute-start | bytes 221192 | tf_op jit(solution)/shard_map/ppermute | solution.py:651
  318.2 12.0 %collective-permute-start.34 = (bf16[96,1536]{1,0:T(8,128)(2,1)S(1)}, bf16[96,1536]{1,0:T(8,128)(2,1)S(1)}, u32[]{:S(2)}, u32[]{:S(2)}) collective-permute-start(bf16[96,1536]{1,0:T(8,128)(2,1)S(1)} %bitcast.318), channel_id=1, source_target_pairs={{0,0},{4,1},{8,2},{12,3},{1,4},{5,5},{9,6},{13,7},{2,8},{6,9},{10,... | collective-permute-start | bytes 884744 | tf_op jit(solution)/shard_map/ppermute | solution.py:885
  320.2 9.8 %collective-permute-start.33 = (bf16[1,48,768]{2,1,0:T(8,128)(2,1)S(1)}, bf16[1,48,768]{2,1,0:T(8,128)(2,1)S(1)}, u32[]{:S(2)}, u32[]{:S(2)}) collective-permute-start(bf16[1,48,768]{2,1,0:T(8,128)(2,1)S(1)} %get-tuple-element.153), channel_id=1, source_target_pairs={{0,3},{1,2},{2,1},{3,0},{4,7},{5,6},{6,5},{7,4},{8,11},{9,10},{10,... | collective-permute-start | bytes 221192 | tf_op jit(solution)/shard_map/ppermute | solution.py:651
  332.4 20.6 %copy-start.7 = (bf16[1,256,1536]{2,1,0:T(8,128)(2,1)S(1)}, bf16[1,256,1536]{2,1,0:T(8,128)(2,1)}, u32[]{:S(2)}) copy-start(bf16[1,256,1536]{2,1,0:T(8,128)(2,1)} %param.14) | copy-start | bytes 2359300
  332.5 1.3 collective-permute-start.35
  333.9 7.7 %collective-permute-start.36 = (bf16[1,48,896]{2,1,0:T(8,128)(2,1)S(1)}, bf16[1,48,896]{2,1,0:T(8,128)(2,1)S(1)}, u32[]{:S(2)}, u32[]{:S(2)}) collective-permute-start(bf16[1,48,896]{2,1,0:T(8,128)(2,1)S(1)} %get-tuple-element.151), channel_id=1, source_target_pairs={{0,2},{1,3},{2,0},{3,1},{4,6},{5,7},{6,4},{7,5},{8,10},{9,11},{10,... | collective-permute-start | bytes 258056 | tf_op jit(solution)/shard_map/ppermute | solution.py:651
  337.1 7.8 %collective-permute-start.37 = (bf16[1,48,896]{2,1,0:T(8,128)(2,1)S(1)}, bf16[1,48,896]{2,1,0:T(8,128)(2,1)S(1)}, u32[]{:S(2)}, u32[]{:S(2)}) collective-permute-start(bf16[1,48,896]{2,1,0:T(8,128)(2,1)S(1)} %get-tuple-element.150), channel_id=1, source_target_pairs={{0,3},{1,2},{2,1},{3,0},{4,7},{5,6},{6,5},{7,4},{8,11},{9,10},{10,... | collective-permute-start | bytes 258056 | tf_op jit(solution)/shard_map/ppermute | solution.py:651
  (51 other events, 314.2 us)
Sparse Core Ops, SparseCore 0:
  70.9 83.9 all-gather.1
  193.2 104.1 reduce-scatter.2
  309.6 41.8 reduce-scatter.4

commit v5 on v4

--- a/solution.py
+++ b/solution.py
@@ -865,10 +865,11 @@
     )
     lines = jnp.concatenate([x_lines, small_lines], axis=-1)
     packed = added_over(packed, reversed(bits_of(groups)[1:]))
+    packed, result = lax.optimization_barrier((packed, result))
     lines, packed = lax.optimization_barrier((lines, packed))
     shares = shared_rows(lines)
     packed = gathered(added_over(packed, bits_of(groups)[:1])[None])
-    parts, result = lax.optimization_barrier((after(parts, lines), result))
+    parts = after(parts, lines)
     d_norm = after(d_normed.astype(bf16), parts)
     d_norm = lax.psum_scatter(d_norm, "seq", scatter_dimension=0, tiled=True).astype(f32)
 

time: 366 us -> 374 us (1.022)
  local copies, waits for them, and re-layouts: 44.1 us -> 50.5 us
  waiting for transfers between devices: 91.9 us -> 86.7 us
  other arithmetic: 42.3 us -> 46.2 us
  matrix products: 33.4 us -> 29.6 us
    ppermute x12, waiting for transfers between devices: 27 us -> 38.6 us  [crossed(): lax.ppermute(block, 'dp', [(i, i ^ bits) for i in range(lax.axis_size('dp...]
    ppermute x12, waiting for transfers between devices: 18.9 us -> 9.33 us  [swapped(): return lax.ppermute(block, 'seq', [(i, i ^ bit) for i in range(size)])]
    ppermute x6, waiting for transfers between devices: 18.5 us -> 12.7 us  [turned(): piece = lax.ppermute(piece, 'seq', [(i, i ^ bits) for i in range(size)])]
    reduce_scatter x1, waiting for transfers between devices: 6.63 us -> 1.96 us  [shards(): lax.psum_scatter(d_norm, 'seq', scatter_dimension=0, tiled=True).astype(f32)]
    unnamed x116, local copies, waits for them, and re-layouts: 2.1 us -> 6.69 us
    ppermute x6, starting transfers between devices: 5.08 us -> 8.99 us  [turned(): piece = lax.ppermute(piece, 'seq', [(i, i ^ bits) for i in range(size)])]
    dot_general x7, matrix products: 33.4 us -> 29.6 us  [mm(): return lax.dot_general(a, b, (dims, ((), ())), preferred_element_type=out)]
  transfers between devices with their start and end apart: 45 -> 45, of which waited for: 21 -> 24; matrix products, arithmetic and copies ran while one was open for 30% -> 31% of each run, Pallas kernels for 12% -> 12%
where the time goes in v5:
time: 374 us; the launch traced here: 367 us
  waiting for transfers between devices  86.7 us (23%)
  Pallas kernels  75.3 us (20%)
  starting transfers between devices  58 us (16%)
  local copies, waits for them, and re-layouts  50.5 us (14%)
  other arithmetic  46.2 us (12%)
  matrix products  29.6 us (8%)
  between operations  15.1 us (4%)
  blocking collectives  5.73 us (2%)
    ppermute x12, waiting for transfers between devices, crossed(): lax.ppermute(block, 'dp', [(i, i ^ bits) for i in range(lax.axis_size('dp...  38.6 us
    pallas_call x1, Pallas kernels, run_backward(): pl.pallas_call(functools.partial(scan_backward, q, taps, pairs, head, chu...  30.8 us
    dot_general x7, matrix products, mm(): return lax.dot_general(a, b, (dims, ((), ())), preferred_element_type=out)  29.6 us
    ppermute x6, starting transfers between devices, moved_by(): return lax.ppermute(block, 'dp', route)  19.4 us
    pallas_call x1, Pallas kernels, run_gate_backward(): pl.pallas_call(functools.partial(gate_backward, blocks, tile, z_rows, tal...  18.8 us
    pallas_call x1, Pallas kernels, run_forward(): pl.pallas_call(functools.partial(scan_forward, q, taps, pairs, head), gri...  13.4 us
    ppermute x6, waiting for transfers between devices, turned(): piece = lax.ppermute(piece, 'seq', [(i, i ^ bits) for i in range(size)])  12.7 us
    pallas_call x1, Pallas kernels, run_gate_forward(): pl.pallas_call(functools.partial(gate_forward, groups, z_rows, tall), gri...  12.3 us
  transfers between devices with their start and end apart: 45, of which 24 were waited for; matrix products, arithmetic and copies ran while one was open for 31% of the time, Pallas kernels for 12%

profile of v5, /device:TPU:2, one launch (start us, length us, event | category | flops | bytes accessed | tf_op | source)
XLA Modules:
  0.0 367.2 jit_solution(9086478334644130047)
XLA Ops:
  12.9 3.6 all-to-all-start
  16.7 2.5 collective-permute-start.2
  25.6 5.3 %all-to-all-done = bf16[4,48,1664]{2,1,0:T(8,128)(2,1)S(1)} async-done(((bf16[4,48,1664]{2,1,0:T(8,128)(2,1)}), bf16[4,48,1664]{2,1,0:T(8,128)(2,1)S(1)}, u32[]{:S(2)}, u32[]{:S(2)}) %all-to-all-start) | async-done | bytes 639008 | tf_op jit(solution)/shard_map/all_to_all | solution.py:736
  32.5 2.4 collective-permute-start.3
  39.2 5.8 %collective-permute-start.6 = (bf16[192,896]{1,0:T(8,128)(2,1)}, bf16[192,896]{1,0:T(8,128)(2,1)}, u32[]{:S(2)}, u32[]{:S(2)}) collective-permute-start(bf16[192,896]{1,0:T(8,128)(2,1)} %get-tuple-element.132), channel_id=1, source_target_pairs={{0,8},{4,12},{8,16},{12,20},{16,24},{20,28},{1,9},{5,13},{9,17},{1... | collective-permute-start | bytes 1032200 | tf_op jit(solution)/shard_map/ppermute | solution.py:565
  49.2 4.1 %collective-permute-done.3 = bf16[1,256,1536]{2,1,0:T(8,128)(2,1)S(1)} collective-permute-done((bf16[1,256,1536]{2,1,0:T(8,128)(2,1)S(1)}, bf16[1,256,1536]{2,1,0:T(8,128)(2,1)S(1)}, u32[]{:S(2)}, u32[]{:S(2)}) %collective-permute-start.3) | collective-permute-done | bytes 786464 | tf_op jit(solution)/shard_map/ppermute | solution.py:511
  56.9 5.5 %collective-permute-start.9 = (bf16[192,896]{1,0:T(8,128)(2,1)}, bf16[192,896]{1,0:T(8,128)(2,1)}, u32[]{:S(2)}, u32[]{:S(2)}) collective-permute-start(bf16[192,896]{1,0:T(8,128)(2,1)} %collective-permute-done.6), channel_id=1, source_target_pairs={{0,8},{4,12},{8,16},{12,20},{16,24},{20,28},{1,9},{5,13},{9,17},{1... | collective-permute-start | bytes 1032200 | tf_op jit(solution)/shard_map/ppermute | solution.py:565
  62.4 1.9 constant_dynamic-update-slice_fusion.29
  66.5 2.9 collective-permute-done.11
  72.2 4.0 %collective-permute-start.13 = (bf16[192,896]{1,0:T(8,128)(2,1)}, bf16[192,896]{1,0:T(8,128)(2,1)}, u32[]{:S(2)}, u32[]{:S(2)}) collective-permute-start(bf16[192,896]{1,0:T(8,128)(2,1)} %collective-permute-done.9), channel_id=1, source_target_pairs={{0,8},{4,12},{8,16},{12,20},{16,24},{20,28},{1,9},{5,13},{9,17},{1... | collective-permute-start | bytes 1032200 | tf_op jit(solution)/shard_map/ppermute | solution.py:565
  79.4 2.0 constant_dynamic-update-slice_fusion.27
  83.8 11.9 %collective-permute-done.12 = bf16[192,896]{1,0:T(8,128)(2,1)} collective-permute-done((bf16[192,896]{1,0:T(8,128)(2,1)}, bf16[192,896]{1,0:T(8,128)(2,1)}, u32[]{:S(2)}, u32[]{:S(2)}) %collective-permute-start.12) | collective-permute-done | bytes 344096 | tf_op jit(solution)/shard_map/ppermute | solution.py:569
  95.7 4.4 %collective-permute-done.14 = bf16[192,896]{1,0:T(8,128)(2,1)} collective-permute-done((bf16[192,896]{1,0:T(8,128)(2,1)S(1)}, bf16[192,896]{1,0:T(8,128)(2,1)}, u32[]{:S(2)}, u32[]{:S(2)}) %collective-permute-start.14) | collective-permute-done | bytes 344096 | tf_op jit(solution)/shard_map/ppermute | solution.py:565
  101.8 1.9 constant_dynamic-update-slice_fusion.25
  104.7 6.2 %collective-permute-done.15 = bf16[192,896]{1,0:T(8,128)(2,1)S(1)} collective-permute-done((bf16[192,896]{1,0:T(8,128)(2,1)S(1)}, bf16[192,896]{1,0:T(8,128)(2,1)S(1)}, u32[]{:S(2)}, u32[]{:S(2)}) %collective-permute-start.15) | collective-permute-done | bytes 344096 | tf_op jit(solution)/shard_map/ppermute | solution.py:569
  111.7 2.5 maximum_select_fusion
  114.4 2.6 fusion.28
  119.0 5.3 %fusion.16.x_ref.xp_ref = bf16[1024,768]{1,0:T(8,128)(2,1)} fusion(bf16[1024,1536]{1,0:T(8,128)(2,1)S(1)} %bitcast.276, bf16[1536,896]{1,0:T(8,128)(2,1)} %constant_dynamic-update-slice_fusion.24), kind=kOutput, calls=%fused_computation.28 | convolution fusion | flops 2416705536 | bytes 7077888 | tf_op jit(solution)/shard_map/dot_general | solution.py:21
  124.3 1.9 maximum_select_fusion.1
  130.3 13.4 %scan_forward.1 = (f32[1024,768]{1,0:T(8,128)}, f32[8,128,768]{2,1,0:T(8,128)}) custom-call(bf16[1024,768]{1,0:T(8,128)(2,1)} %fusion.16.x_ref.xp_ref, f32[1024,128]{1,0:T(8,128)} %broadcast_select_fusion.1.small_ref, bf16[256,1024]{1,0:T(8,128)(2,1)} %bitcast.289, f32[1024,128]{1,0:T(8,128)} %broadcast_in_dim.75.dcol_ref.dcolp_ref, ...), custom_call_target="tpu_custom_call" | custom-call | tf_op jit(solution)/shard_map/scan_forward/pallas_call | solution.py:271
  143.7 10.4 %all-gather.2.cloned.1.call-done = bf16[3072,768]{1,0:T(8,128)(2,1)} async-done(((bf16[384,768]{1,0:T(8,128)(2,1)}), bf16[3072,768]{1,0:T(8,128)(2,1)}) %all-gather.2.cloned.1.call-update) | async-done | bytes 4718608 | tf_op jit(solution)/shard_map/all_gather | solution.py:770
  154.1 12.3 %gate_forward.1 = (f32[1024,768]{1,0:T(8,128)}, f32[1024,768]{1,0:T(8,128)}, f32[8,1024]{1,0:T(8,128)}, bf16[1536,768]{1,0:T(8,128)(2,1)}, bf16[2,768,768]{2,1,0:T(8,128)(2,1)}) custom-call(bf16[1024,1536]{1,0:T(8,128)(2,1)} %bitcast.277, bf16[1024,1536]{1,0:T(8,128)(2,1)} %bitcast.281, bf16[8,384,768]{2,1,0:T(8,128)(2,1)} %bitcast.292, ...), custom_call_target="tpu_custom_call" | custom-call | tf_op jit(solution)/shard_map/gate_forward/pallas_call | solution.py:452
  167.1 5.7 %psum.7 = f32[2,1024]{1,0:T(2,128)S(1)} all-reduce(f32[2,1024]{1,0:T(2,128)S(1)} %slice.314), channel_id=1, replica_groups=mesh['dp'=8,'seq'=4] {'seq'}, use_global_device_ids=true, to_apply=%region_1.2 | all-reduce | flops 2048 | bytes 16384 | tf_op jit(solution)/shard_map/psum | solution.py:818
  173.5 18.8 %gate_backward.1 = (bf16[1024,768]{1,0:T(8,128)(2,1)}, bf16[1024,768]{1,0:T(8,128)(2,1)}, f32[1024,768]{1,0:T(8,128)}, f32[8,768]{1,0:T(8,128)}, bf16[8,384,768]{2,1,0:T(8,128)(2,1)}) custom-call(bf16[1024,1536]{1,0:T(8,128)(2,1)} %bitcast.278, bf16[1024,1536]{1,0:T(8,128)(2,1)} %bitcast.282, f32[1024,768]{1,0:T(8,128)} %get-tuple-element.68.y_ref, ...), custom_call_target="tpu_custom_call" | custom-call | tf_op jit(solution)/shard_map/gate_backward/pallas_call | solution.py:484
  192.6 30.8 %scan_backward.1 = (bf16[1024,768]{1,0:T(8,128)(2,1)}, f32[1024,128]{1,0:T(8,128)}, f32[256,1024]{1,0:T(8,128)}, f32[8,768]{1,0:T(8,128)}, f32[8,128]{1,0:T(8,128)}) custom-call(bf16[1024,768]{1,0:T(8,128)(2,1)} %fusion.16.x_ref.xp_ref, bf16[1024,768]{1,0:T(8,128)(2,1)} %fusion.16.x_ref.xp_ref, f32[1024,128]{1,0:T(8,128)} %broadcast_select_fusion.1.small_ref, ...), custom_call_target="tpu_custom_call" | custom-call | tf_op jit(solution)/shard_map/scan_backward/pallas_call | solution.py:316
  223.4 4.4 %convolution_convert_fusion.1 = bf16[1536,768]{1,0:T(8,128)(2,1)S(1)} fusion(bf16[1024,1536]{1,0:T(8,128)(2,1)S(1)} %bitcast.279, bf16[1024,768]{1,0:T(8,128)(2,1)} %get-tuple-element.76), kind=kOutput, calls=%fused_computation.3 | convolution fusion | flops 2417098752 | bytes 7077888 | tf_op jit(solution)/shard_map/dot_general | solution.py:21
  231.7 1.9 fusion.45
  237.1 1.9 copy.70
  246.2 2.3 multiply_reduce_fusion.1
  248.4 4.3 %convolution_convert_fusion = bf16[1024,1536]{1,0:T(8,128)(2,1)S(1)} fusion(bf16[1024,768]{1,0:T(8,128)(2,1)} %get-tuple-element.85, bf16[768,768]{1,0:T(8,128)(2,1)} %get-tuple-element.124, bf16[768,768]{1,0:T(8,128)(2,1)S(1)} %copy-done.16), kind=kOutput, calls=%fused_computation.2 | convolution fusion | flops 2422210560 | bytes 7077888 | tf_op jit(solution)/shard_map/dot_general | solution.py:21
  257.8 4.7 %fusion.70 = f32[1024,1536]{1,0:T(8,128)} fusion(bf16[1024,768]{1,0:T(8,128)(2,1)S(1)} %copy-done.46, bf16[1536,768]{1,0:T(8,128)(2,1)S(1)} %copy-done.45), kind=kOutput, calls=%fused_computation.228 | convolution fusion | flops 2415919104 | bytes 10223616 | tf_op jit(solution)/shard_map/dot_general | solution.py:21
  262.5 1.9 fusion.62
  267.7 2.1 fusion
  274.3 7.3 %fusion.65 = (bf16[1024,1536]{1,0:T(8,128)(2,1)}, f32[1536]{0:T(1024)S(1)}) fusion(bf16[2,2,256,1536]{3,2,1,0:T(8,128)(2,1)S(1)} %copy-done.1, f32[1024,1536]{1,0:T(8,128)S(1)} %copy-done.49, bf16[1536,896]{1,0:T(8,128)(2,1)} %constant_dynamic-update-slice_fusion.24, bf16[1024,64]{1,0:T(8,128)(2,1)S(1)} %copy-done.23, bf16[1024,64]{1,0:T(8,128)(2,1)S(1)} %copy-done.22, ...), kind=kOutput, calls=%fused_computation.223 | convolution fusion | flops 2831940096 | bytes 17176576 | tf_op jit(solution)/shard_map/dot_general | solution.py:21
  284.8 5.4 %collective-permute-done.22 = f32[6500]{0:T(1024)S(1)} collective-permute-done((f32[6500]{0:T(1024)S(1)}, f32[6500]{0:T(1024)S(1)}, u32[]{:S(2)}, u32[]{:S(2)}) %collective-permute-start.22) | collective-permute-done | bytes 26032 | tf_op jit(solution)/shard_map/ppermute | solution.py:569
  290.3 6.1 %collective-permute-done.23 = f32[6500]{0:T(1024)S(1)} collective-permute-done((f32[6500]{0:T(1024)S(1)}, f32[6500]{0:T(1024)S(1)}, u32[]{:S(2)}, u32[]{:S(2)}) %collective-permute-start.23) | collective-permute-done | bytes 26032 | tf_op jit(solution)/shard_map/ppermute | solution.py:569
  297.4 2.1 fusion.6
  300.7 2.5 fusion.26
  304.3 2.8 collective-permute-done.38
  308.6 3.2 collective-permute-start.29
  321.6 2.5 collective-permute-start.34
  324.2 3.7 %collective-permute-done.33 = bf16[1,48,768]{2,1,0:T(8,128)(2,1)S(1)} collective-permute-done((bf16[1,48,768]{2,1,0:T(8,128)(2,1)S(1)}, bf16[1,48,768]{2,1,0:T(8,128)(2,1)S(1)}, u32[]{:S(2)}, u32[]{:S(2)}) %collective-permute-start.33) | collective-permute-done | bytes 73760 | tf_op jit(solution)/shard_map/ppermute | solution.py:651
  328.1 2.0 collective-permute-done.34
  330.9 4.9 %collective-permute-done.29 = bf16[192,896]{1,0:T(8,128)(2,1)} collective-permute-done((bf16[192,896]{1,0:T(8,128)(2,1)}, bf16[192,896]{1,0:T(8,128)(2,1)}, u32[]{:S(2)}, u32[]{:S(2)}) %collective-permute-start.29) | collective-permute-done | bytes 344096 | tf_op jit(solution)/shard_map/ppermute | solution.py:569
  338.6 7.0 %collective-permute-start.36 = (bf16[1,48,896]{2,1,0:T(8,128)(2,1)S(1)}, bf16[1,48,896]{2,1,0:T(8,128)(2,1)S(1)}, u32[]{:S(2)}, u32[]{:S(2)}) collective-permute-start(bf16[1,48,896]{2,1,0:T(8,128)(2,1)S(1)} %get-tuple-element.151), channel_id=1, source_target_pairs={{0,2},{1,3},{2,0},{3,1},{4,6},{5,7},{6,4},{7,5},{8,10},{9,11},{10,... | collective-permute-start | bytes 258056 | tf_op jit(solution)/shard_map/ppermute | solution.py:651
  346.3 4.5 %collective-permute-done.36 = bf16[1,48,896]{2,1,0:T(8,128)(2,1)S(1)} collective-permute-done((bf16[1,48,896]{2,1,0:T(8,128)(2,1)S(1)}, bf16[1,48,896]{2,1,0:T(8,128)(2,1)S(1)}, u32[]{:S(2)}, u32[]{:S(2)}) %collective-permute-start.36) | collective-permute-done | bytes 86048 | tf_op jit(solution)/shard_map/ppermute | solution.py:651
  350.9 3.0 collective-permute-done.37
  353.9 2.0 reduce-scatter.5.cloned.1.call-done
  (342 shorter events, 101.6 us)
Async XLA Ops:
  7.2 16.1 %collective-permute-start = (s32[1,1,256]{2,1,0:T(1,128)}, s32[1,1,256]{2,1,0:T(1,128)S(1)}, u32[]{:S(2)}, u32[]{:S(2)}) collective-permute-start(s32[1,1,256]{2,1,0:T(1,128)} %bitcast.336), channel_id=1, source_target_pairs={{0,2},{1,3},{2,0},{3,1},{4,6},{5,7},{6,4},{7,5},{8,10},{9,11},{10,... | collective-permute-start | bytes 3080 | tf_op jit(solution)/shard_map/ppermute | solution.py:511
  12.9 18.0 %all-to-all-start = ((bf16[4,48,1664]{2,1,0:T(8,128)(2,1)}), bf16[4,48,1664]{2,1,0:T(8,128)(2,1)S(1)}, u32[]{:S(2)}, u32[]{:S(2)}) async-start(bf16[4,48,1664]{2,1,0:T(8,128)(2,1)} %bitcast.4), calls=%async_computation | async-start | bytes 1277952 | tf_op jit(solution)/shard_map/all_to_all | solution.py:736
  16.6 137.5 %all-gather.2.cloned.1.call-start = ((), (), s32[]{:S(2)}) async-start(), calls=%async_computation.3 | async-start | bytes 5308416 | tf_op jit(solution)/shard_map/all_gather | solution.py:770
  16.7 8.9 %collective-permute-start.2 = (bf16[96,1536]{1,0:T(8,128)(2,1)S(1)}, bf16[96,1536]{1,0:T(8,128)(2,1)S(1)}, u32[]{:S(2)}, u32[]{:S(2)}) collective-permute-start(bf16[96,1536]{1,0:T(8,128)(2,1)S(1)} %convert_element_type.199), channel_id=1, source_target_pairs={{0,0},{1,4},{2,8},{3,12},{4,1},{5,5},{6,9},{7,13},{8,2},{9,6},{10,... | collective-permute-start | bytes 884744 | tf_op jit(solution)/shard_map/ppermute | solution.py:748
  23.3 1.2 collective-permute-start.1
  32.5 20.8 %collective-permute-start.3 = (bf16[1,256,1536]{2,1,0:T(8,128)(2,1)S(1)}, bf16[1,256,1536]{2,1,0:T(8,128)(2,1)S(1)}, u32[]{:S(2)}, u32[]{:S(2)}) collective-permute-start(bf16[1,256,1536]{2,1,0:T(8,128)(2,1)S(1)} %bitcast.286), channel_id=1, source_target_pairs={{0,2},{1,3},{2,0},{3,1},{4,6},{5,7},{6,4},{7,5},{8,10},{9,11},{10,... | collective-permute-start | bytes 2359304 | tf_op jit(solution)/shard_map/ppermute | solution.py:511
  37.5 9.9 %collective-permute-start.5 = (bf16[192,896]{1,0:T(8,128)(2,1)}, bf16[192,896]{1,0:T(8,128)(2,1)}, u32[]{:S(2)}, u32[]{:S(2)}) collective-permute-start(bf16[192,896]{1,0:T(8,128)(2,1)} %get-tuple-element.132), channel_id=1, source_target_pairs={{0,4},{4,0},{8,12},{12,8},{16,20},{20,16},{24,28},{28,24},{1,5},{5... | collective-permute-start | bytes 1032200 | tf_op jit(solution)/shard_map/ppermute | solution.py:569
  38.0 31.3 %collective-permute-start.11 = (bf16[1,256,1536]{2,1,0:T(8,128)(2,1)S(1)}, bf16[1,256,1536]{2,1,0:T(8,128)(2,1)S(1)}, u32[]{:S(2)}, u32[]{:S(2)}) collective-permute-start(bf16[1,256,1536]{2,1,0:T(8,128)(2,1)S(1)} %copy-done.8), channel_id=1, source_target_pairs={{0,2},{1,3},{2,0},{3,1},{4,6},{5,7},{6,4},{7,5},{8,10},{9,11},{10,... | collective-permute-start | bytes 2359304 | tf_op jit(solution)/shard_map/ppermute | solution.py:511
  39.2 15.5 %collective-permute-start.6 = (bf16[192,896]{1,0:T(8,128)(2,1)}, bf16[192,896]{1,0:T(8,128)(2,1)}, u32[]{:S(2)}, u32[]{:S(2)}) collective-permute-start(bf16[192,896]{1,0:T(8,128)(2,1)} %get-tuple-element.132), channel_id=1, source_target_pairs={{0,8},{4,12},{8,16},{12,20},{16,24},{20,28},{1,9},{5,13},{9,17},{1... | collective-permute-start | bytes 1032200 | tf_op jit(solution)/shard_map/ppermute | solution.py:565
  45.0 10.6 %collective-permute-start.7 = (bf16[192,896]{1,0:T(8,128)(2,1)}, bf16[192,896]{1,0:T(8,128)(2,1)}, u32[]{:S(2)}, u32[]{:S(2)}) collective-permute-start(bf16[192,896]{1,0:T(8,128)(2,1)} %get-tuple-element.132), channel_id=1, source_target_pairs={{8,0},{12,4},{16,8},{20,12},{24,16},{28,20},{9,1},{13,5},{17,9},{2... | collective-permute-start | bytes 1032200 | tf_op jit(solution)/shard_map/ppermute | solution.py:565
  55.6 16.3 %collective-permute-start.10 = (bf16[192,896]{1,0:T(8,128)(2,1)}, bf16[192,896]{1,0:T(8,128)(2,1)S(1)}, u32[]{:S(2)}, u32[]{:S(2)}) collective-permute-start(bf16[192,896]{1,0:T(8,128)(2,1)} %collective-permute-done.7), channel_id=1, source_target_pairs={{8,0},{12,4},{16,8},{20,12},{24,16},{28,20},{9,1},{13,5},{17,9},{2... | collective-permute-start | bytes 1032200 | tf_op jit(solution)/shard_map/ppermute | solution.py:565
  56.9 15.1 %collective-permute-start.9 = (bf16[192,896]{1,0:T(8,128)(2,1)}, bf16[192,896]{1,0:T(8,128)(2,1)}, u32[]{:S(2)}, u32[]{:S(2)}) collective-permute-start(bf16[192,896]{1,0:T(8,128)(2,1)} %collective-permute-done.6), channel_id=1, source_target_pairs={{0,8},{4,12},{8,16},{12,20},{16,24},{20,28},{1,9},{5,13},{9,17},{1... | collective-permute-start | bytes 1032200 | tf_op jit(solution)/shard_map/ppermute | solution.py:565
  64.4 7.6 %collective-permute-start.8 = (bf16[192,896]{1,0:T(8,128)(2,1)}, bf16[192,896]{1,0:T(8,128)(2,1)}, u32[]{:S(2)}, u32[]{:S(2)}) collective-permute-start(bf16[192,896]{1,0:T(8,128)(2,1)} %get-tuple-element.120), channel_id=1, source_target_pairs={{0,4},{4,0},{8,12},{12,8},{16,20},{20,16},{24,28},{28,24},{1,5},{5... | collective-permute-start | bytes 1032200 | tf_op jit(solution)/shard_map/ppermute | solution.py:569
  72.0 241.0 %reduce-scatter.3.cloned.1.call-start = ((), (), s32[]{:S(2)}) async-start(), calls=%async_computation.4 | async-start | bytes 5308416 | tf_op jit(solution)/shard_map/reduce_scatter | solution.py:830
  72.1 39.6 %collective-permute-start.4 = (bf16[2,256,1536]{2,1,0:T(8,128)(2,1)}, bf16[2,256,1536]{2,1,0:T(8,128)(2,1)}, u32[]{:S(2)}, u32[]{:S(2)}) collective-permute-start(bf16[2,256,1536]{2,1,0:T(8,128)(2,1)} %maximum_select_fusion.2), channel_id=1, source_target_pairs={{0,1},{1,0},{2,3},{3,2},{4,5},{5,4},{6,7},{7,6},{8,9},{9,8},{10,11... | collective-permute-start | bytes 4718600 | tf_op jit(solution)/shard_map/ppermute | solution.py:511
  72.2 23.5 %collective-permute-start.13 = (bf16[192,896]{1,0:T(8,128)(2,1)}, bf16[192,896]{1,0:T(8,128)(2,1)}, u32[]{:S(2)}, u32[]{:S(2)}) collective-permute-start(bf16[192,896]{1,0:T(8,128)(2,1)} %collective-permute-done.9), channel_id=1, source_target_pairs={{0,8},{4,12},{8,16},{12,20},{16,24},{20,28},{1,9},{5,13},{9,17},{1... | collective-permute-start | bytes 1032200 | tf_op jit(solution)/shard_map/ppermute | solution.py:565
  76.2 23.8 %collective-permute-start.14 = (bf16[192,896]{1,0:T(8,128)(2,1)S(1)}, bf16[192,896]{1,0:T(8,128)(2,1)}, u32[]{:S(2)}, u32[]{:S(2)}) collective-permute-start(bf16[192,896]{1,0:T(8,128)(2,1)S(1)} %collective-permute-done.10), channel_id=1, source_target_pairs={{8,0},{12,4},{16,8},{20,12},{24,16},{28,20},{9,1},{13,5},{17,9},{2... | collective-permute-start | bytes 1032200 | tf_op jit(solution)/shard_map/ppermute | solution.py:565
  81.4 14.2 %collective-permute-start.12 = (bf16[192,896]{1,0:T(8,128)(2,1)}, bf16[192,896]{1,0:T(8,128)(2,1)}, u32[]{:S(2)}, u32[]{:S(2)}) collective-permute-start(bf16[192,896]{1,0:T(8,128)(2,1)} %get-tuple-element.118), channel_id=1, source_target_pairs={{0,4},{4,0},{8,12},{12,8},{16,20},{20,16},{24,28},{28,24},{1,5},{5... | collective-permute-start | bytes 1032200 | tf_op jit(solution)/shard_map/ppermute | solution.py:569
  83.7 34.1 %copy-start.25 = (f32[1024]{0:T(1024)}, f32[1024]{0:T(1024)S(1)}, u32[]{:S(2)}) copy-start(f32[1024]{0:T(1024)S(1)} %get-tuple-element.168) | copy-start | bytes 12292
  83.7 40.5 %collective-permute-start.18 = (bf16[2,256,1536]{2,1,0:T(8,128)(2,1)}, bf16[2,256,1536]{2,1,0:T(8,128)(2,1)S(1)}, u32[]{:S(2)}, u32[]{:S(2)}) collective-permute-start(bf16[2,256,1536]{2,1,0:T(8,128)(2,1)} %maximum_select_fusion.4), channel_id=1, source_target_pairs={{0,1},{1,0},{2,3},{3,2},{4,5},{5,4},{6,7},{7,6},{8,9},{9,8},{10,11... | collective-permute-start | bytes 4718600 | tf_op jit(solution)/shard_map/ppermute | solution.py:511
  103.7 7.2 %collective-permute-start.15 = (bf16[192,896]{1,0:T(8,128)(2,1)S(1)}, bf16[192,896]{1,0:T(8,128)(2,1)S(1)}, u32[]{:S(2)}, u32[]{:S(2)}) collective-permute-start(bf16[192,896]{1,0:T(8,128)(2,1)S(1)} %get-tuple-element.116), channel_id=1, source_target_pairs={{0,4},{4,0},{8,12},{12,8},{16,20},{20,16},{24,28},{28,24},{1,5},{5... | collective-permute-start | bytes 1032200 | tf_op jit(solution)/shard_map/ppermute | solution.py:569
  119.0 7.5 %collective-permute-start.16 = (bf16[1,64,1024]{2,1,0:T(8,128)(2,1)S(1)}, bf16[1,64,1024]{2,1,0:T(8,128)(2,1)}, u32[]{:S(2)}, u32[]{:S(2)}) collective-permute-start(bf16[1,64,1024]{2,1,0:T(8,128)(2,1)S(1)} %bitcast.304), channel_id=1, source_target_pairs={{0,2},{1,3},{2,0},{3,1},{4,6},{5,7},{6,4},{7,5},{8,10},{9,11},{10,... | collective-permute-start | bytes 393224 | tf_op jit(solution)/shard_map/ppermute | solution.py:511
  127.5 1.9 collective-permute-start.17
  192.3 163.5 %reduce-scatter.5.cloned.1.call-start = ((), (), s32[]{:S(2)}) async-start(), calls=%async_computation.5 | async-start | bytes 3932160 | tf_op jit(solution)/shard_map/reduce_scatter | solution.py:874
  192.6 30.8 %copy-start.1 = (bf16[2,2,256,1536]{3,2,1,0:T(8,128)(2,1)S(1)}, bf16[2,2,256,1536]{3,2,1,0:T(8,128)(2,1)}, u32[]{:S(2)}) copy-start(bf16[2,2,256,1536]{3,2,1,0:T(8,128)(2,1)} %copy-done) | copy-start | bytes 9437188
  230.3 67.1 %collective-permute-start.26 = (bf16[4,192,768]{2,1,0:T(8,128)(2,1)}, bf16[4,192,768]{2,1,0:T(8,128)(2,1)}, u32[]{:S(2)}, u32[]{:S(2)}) collective-permute-start(bf16[4,192,768]{2,1,0:T(8,128)(2,1)} %dynamic-slice_bitcast_fusion), channel_id=1, source_target_pairs={{0,4},{4,0},{8,12},{12,8},{16,20},{20,16},{24,28},{28,24},{1,5},{5... | collective-permute-start | bytes 3538952 | tf_op jit(solution)/shard_map/ppermute | solution.py:569
  233.6 12.5 %collective-permute-start.19 = (bf16[64,1024]{1,0:T(8,128)(2,1)}, bf16[64,1024]{1,0:T(8,128)(2,1)}, u32[]{:S(2)}, u32[]{:S(2)}) collective-permute-start(bf16[64,1024]{1,0:T(8,128)(2,1)} %get-tuple-element.129), channel_id=1, source_target_pairs={{0,1},{1,0},{2,3},{3,2},{4,5},{5,4},{6,7},{7,6},{8,9},{9,8},{10,11... | collective-permute-start | bytes 393224 | tf_op jit(solution)/shard_map/ppermute | solution.py:677
  233.6 12.5 %collective-permute-start.20 = (bf16[64,1024]{1,0:T(8,128)(2,1)}, bf16[64,1024]{1,0:T(8,128)(2,1)}, u32[]{:S(2)}, u32[]{:S(2)}) collective-permute-start(bf16[64,1024]{1,0:T(8,128)(2,1)} %get-tuple-element.131), channel_id=1, source_target_pairs={{0,2},{1,3},{2,0},{3,1},{4,6},{5,7},{6,4},{7,5},{8,10},{9,11},{10,... | collective-permute-start | bytes 393224 | tf_op jit(solution)/shard_map/ppermute | solution.py:677
  235.4 10.8 %collective-permute-start.21 = (bf16[64,1024]{1,0:T(8,128)(2,1)}, bf16[64,1024]{1,0:T(8,128)(2,1)}, u32[]{:S(2)}, u32[]{:S(2)}) collective-permute-start(bf16[64,1024]{1,0:T(8,128)(2,1)} %get-tuple-element.130), channel_id=1, source_target_pairs={{0,3},{1,2},{2,1},{3,0},{4,7},{5,6},{6,5},{7,4},{8,11},{9,10},{10,... | collective-permute-start | bytes 393224 | tf_op jit(solution)/shard_map/ppermute | solution.py:677
  255.2 12.4 %collective-permute-start.24 = (bf16[2,256,1536]{2,1,0:T(8,128)(2,1)}, bf16[2,256,1536]{2,1,0:T(8,128)(2,1)}, u32[]{:S(2)}, u32[]{:S(2)}) collective-permute-start(bf16[2,256,1536]{2,1,0:T(8,128)(2,1)} %select_bitcast_fusion), channel_id=1, source_target_pairs={{0,1},{1,0},{2,3},{3,2},{4,5},{5,4},{6,7},{7,6},{8,9},{9,8},{10,11... | collective-permute-start | bytes 4718600 | tf_op jit(solution)/shard_map/ppermute | solution.py:511
  267.1 29.3 %collective-permute-start.27 = (bf16[4,192,128]{2,1,0:T(8,128)(2,1)}, bf16[4,192,128]{2,1,0:T(8,128)(2,1)}, u32[]{:S(2)}, u32[]{:S(2)}) collective-permute-start(bf16[4,192,128]{2,1,0:T(8,128)(2,1)} %dynamic-slice_bitcast_fusion.5), channel_id=1, source_target_pairs={{0,4},{4,0},{8,12},{12,8},{16,20},{20,16},{24,28},{28,24},{1,5},{5... | collective-permute-start | bytes 589832 | tf_op jit(solution)/shard_map/ppermute | solution.py:569
  272.5 23.8 %copy-start.20 = (bf16[1536,128]{1,0:T(8,128)(2,1)S(1)}, bf16[1536,128]{1,0:T(8,128)(2,1)}, u32[]{:S(2)}) copy-start(bf16[1536,128]{1,0:T(8,128)(2,1)} %copy-done.19) | copy-start | bytes 1179652
  272.5 27.1 %collective-permute-start.25 = (bf16[1,256,1536]{2,1,0:T(8,128)(2,1)}, bf16[1,256,1536]{2,1,0:T(8,128)(2,1)}, u32[]{:S(2)}, u32[]{:S(2)}) collective-permute-start(bf16[1,256,1536]{2,1,0:T(8,128)(2,1)} %fusion.27), channel_id=1, source_target_pairs={{0,2},{1,3},{2,0},{3,1},{4,6},{5,7},{6,4},{7,5},{8,10},{9,11},{10,... | collective-permute-start | bytes 2359304 | tf_op jit(solution)/shard_map/ppermute | solution.py:511
  283.1 7.1 %collective-permute-start.22 = (f32[6500]{0:T(1024)S(1)}, f32[6500]{0:T(1024)S(1)}, u32[]{:S(2)}, u32[]{:S(2)}) collective-permute-start(f32[6500]{0:T(1024)S(1)} %concatenate.192), channel_id=1, source_target_pairs={{0,16},{4,20},{8,24},{12,28},{16,0},{20,4},{24,8},{28,12},{1,17},{... | collective-permute-start | bytes 78008 | tf_op jit(solution)/shard_map/ppermute | solution.py:569
  290.2 6.1 %collective-permute-start.23 = (f32[6500]{0:T(1024)S(1)}, f32[6500]{0:T(1024)S(1)}, u32[]{:S(2)}, u32[]{:S(2)}) collective-permute-start(f32[6500]{0:T(1024)S(1)} %add.295), channel_id=1, source_target_pairs={{0,8},{4,12},{8,0},{12,4},{16,24},{20,28},{24,16},{28,20},{1,9},{5... | collective-permute-start | bytes 78008 | tf_op jit(solution)/shard_map/ppermute | solution.py:569
  303.2 3.9 %collective-permute-start.38 = (f32[6500]{0:T(1024)S(1)}, f32[6500]{0:T(1024)S(1)}, u32[]{:S(2)}, u32[]{:S(2)}) collective-permute-start(f32[6500]{0:T(1024)S(1)} %add.296), channel_id=1, source_target_pairs={{0,4},{4,0},{8,12},{12,8},{16,20},{20,16},{24,28},{28,24},{1,5},{5... | collective-permute-start | bytes 78008 | tf_op jit(solution)/shard_map/ppermute | solution.py:569
  307.1 6.0 %collective-permute-start.39 = (f32[1,1,6500]{2,1,0:T(1,128)S(1)}, f32[1,1,6500]{2,1,0:T(1,128)S(1)}, u32[]{:S(2)}, u32[]{:S(2)}) collective-permute-start(f32[1,1,6500]{2,1,0:T(1,128)S(1)} %broadcast_in_dim_broadcast_in_dim.3), channel_id=1, source_target_pairs={{0,2},{1,3},{2,0},{3,1},{4,6},{5,7},{6,4},{7,5},{8,10},{9,11},{10,... | collective-permute-start | bytes 78008 | tf_op jit(solution)/shard_map/ppermute | solution.py:511
  308.6 22.4 %collective-permute-start.28 = (bf16[192,896]{1,0:T(8,128)(2,1)}, bf16[192,896]{1,0:T(8,128)(2,1)}, u32[]{:S(2)}, u32[]{:S(2)}) collective-permute-start(bf16[192,896]{1,0:T(8,128)(2,1)} %get-tuple-element.127), channel_id=1, source_target_pairs={{0,8},{4,12},{8,0},{12,4},{16,24},{20,28},{24,16},{28,20},{1,9},{5... | collective-permute-start | bytes 1032200 | tf_op jit(solution)/shard_map/ppermute | solution.py:569
  308.6 27.3 %collective-permute-start.29 = (bf16[192,896]{1,0:T(8,128)(2,1)}, bf16[192,896]{1,0:T(8,128)(2,1)}, u32[]{:S(2)}, u32[]{:S(2)}) collective-permute-start(bf16[192,896]{1,0:T(8,128)(2,1)} %get-tuple-element.126), channel_id=1, source_target_pairs={{0,16},{4,20},{8,24},{12,28},{16,0},{20,4},{24,8},{28,12},{1,17},{... | collective-permute-start | bytes 1032200 | tf_op jit(solution)/shard_map/ppermute | solution.py:569
  311.8 24.0 %collective-permute-start.30 = (bf16[192,896]{1,0:T(8,128)(2,1)S(1)}, bf16[192,896]{1,0:T(8,128)(2,1)}, u32[]{:S(2)}, u32[]{:S(2)}) collective-permute-start(bf16[192,896]{1,0:T(8,128)(2,1)S(1)} %get-tuple-element.125), channel_id=1, source_target_pairs={{0,24},{4,28},{8,16},{12,20},{16,8},{20,12},{24,0},{28,4},{1,25},{... | collective-permute-start | bytes 1032200 | tf_op jit(solution)/shard_map/ppermute | solution.py:569
  313.1 1.3 collective-permute-start.40
  314.9 1.3 collective-permute-start.31
  316.3 7.8 %collective-permute-start.32 = (bf16[1,48,768]{2,1,0:T(8,128)(2,1)S(1)}, bf16[1,48,768]{2,1,0:T(8,128)(2,1)S(1)}, u32[]{:S(2)}, u32[]{:S(2)}) collective-permute-start(bf16[1,48,768]{2,1,0:T(8,128)(2,1)S(1)} %get-tuple-element.154), channel_id=1, source_target_pairs={{0,2},{1,3},{2,0},{3,1},{4,6},{5,7},{6,4},{7,5},{8,10},{9,11},{10,... | collective-permute-start | bytes 221192 | tf_op jit(solution)/shard_map/ppermute | solution.py:651
  321.6 8.5 %collective-permute-start.34 = (bf16[96,1536]{1,0:T(8,128)(2,1)S(1)}, bf16[96,1536]{1,0:T(8,128)(2,1)S(1)}, u32[]{:S(2)}, u32[]{:S(2)}) collective-permute-start(bf16[96,1536]{1,0:T(8,128)(2,1)S(1)} %bitcast.318), channel_id=1, source_target_pairs={{0,0},{4,1},{8,2},{12,3},{1,4},{5,5},{9,6},{13,7},{2,8},{6,9},{10,... | collective-permute-start | bytes 884744 | tf_op jit(solution)/shard_map/ppermute | solution.py:886
  324.1 3.8 %collective-permute-start.33 = (bf16[1,48,768]{2,1,0:T(8,128)(2,1)S(1)}, bf16[1,48,768]{2,1,0:T(8,128)(2,1)S(1)}, u32[]{:S(2)}, u32[]{:S(2)}) collective-permute-start(bf16[1,48,768]{2,1,0:T(8,128)(2,1)S(1)} %get-tuple-element.153), channel_id=1, source_target_pairs={{0,3},{1,2},{2,1},{3,0},{4,7},{5,6},{6,5},{7,4},{8,11},{9,10},{10,... | collective-permute-start | bytes 221192 | tf_op jit(solution)/shard_map/ppermute | solution.py:651
  337.2 1.3 collective-permute-start.35
  338.6 12.2 %collective-permute-start.36 = (bf16[1,48,896]{2,1,0:T(8,128)(2,1)S(1)}, bf16[1,48,896]{2,1,0:T(8,128)(2,1)S(1)}, u32[]{:S(2)}, u32[]{:S(2)}) collective-permute-start(bf16[1,48,896]{2,1,0:T(8,128)(2,1)S(1)} %get-tuple-element.151), channel_id=1, source_target_pairs={{0,2},{1,3},{2,0},{3,1},{4,6},{5,7},{6,4},{7,5},{8,10},{9,11},{10,... | collective-permute-start | bytes 258056 | tf_op jit(solution)/shard_map/ppermute | solution.py:651
  346.3 7.5 %collective-permute-start.37 = (bf16[1,48,896]{2,1,0:T(8,128)(2,1)S(1)}, bf16[1,48,896]{2,1,0:T(8,128)(2,1)S(1)}, u32[]{:S(2)}, u32[]{:S(2)}) collective-permute-start(bf16[1,48,896]{2,1,0:T(8,128)(2,1)S(1)} %get-tuple-element.150), channel_id=1, source_target_pairs={{0,3},{1,2},{2,1},{3,0},{4,7},{5,6},{6,5},{7,4},{8,11},{9,10},{10,... | collective-permute-start | bytes 258056 | tf_op jit(solution)/shard_map/ppermute | solution.py:651
  (51 other events, 272.6 us)
Sparse Core Ops, SparseCore 0:
  72.1 81.9 all-gather.1
  192.4 109.9 reduce-scatter.2
  313.2 42.6 reduce-scatter.4

commit v6 on v4

--- a/solution.py
+++ b/solution.py
@@ -640,15 +640,17 @@
     return lax.optimization_barrier((value, other))[0]
 
 
-def turned(blocks):
+def turned(blocks, together=False):
     size = lax.axis_size("seq")
     index = lax.axis_index("seq")
     if size & (size - 1):
         return lax.all_to_all(blocks, "seq", 0, 0, tiled=True)
-    out = blocks
+    pieces = []
     for bits in range(1, size):
         piece = lax.dynamic_slice_in_dim(blocks, index ^ bits, 1, 0)
-        piece = lax.ppermute(piece, "seq", [(i, i ^ bits) for i in range(size)])
+        pieces.append(lax.ppermute(piece, "seq", [(i, i ^ bits) for i in range(size)]))
+    out = blocks
+    for bits, piece in enumerate(lax.optimization_barrier(pieces) if together else pieces, 1):
         out = lax.dynamic_update_slice_in_dim(out, piece, index ^ bits, 0)
     return out
 
@@ -872,8 +874,8 @@
     d_norm = after(d_normed.astype(bf16), parts)
     d_norm = lax.psum_scatter(d_norm, "seq", scatter_dimension=0, tiled=True).astype(f32)
 
-    def own_rows(part):
-        return turned(part.reshape(size, in_rows, -1))
+    def own_rows(part, together=False):
+        return turned(part.reshape(size, in_rows, -1), together)
 
     def placed(rows, cuts=runs):
         wide = rows.shape[2] // cuts
@@ -886,7 +888,7 @@
     in_z = placed(own_rows(parts[:z_rows]))
     shares, in_z, d_out_weight = lax.optimization_barrier((shares, in_z, d_out_weight))
     first_part = sum(share.astype(f32) for share in shares)
-    in_first = own_rows(first_part.astype(bf16))
+    in_first = own_rows(first_part.astype(bf16), True)
     lifted = d_norm * norm_gain
     d_flat = inv * lifted - flat * (
         inv * inv * inv * jnp.mean(lifted * flat, axis=-1, keepdims=True)

time: 366 us -> 366 us (level)
  transfers between devices with their start and end apart: 45 -> 45, of which waited for: 21 -> 19; matrix products, arithmetic and copies ran while one was open for 30% -> 30% of each run, Pallas kernels for 12% -> 12%
where the time goes in v6:
time: 366 us; the launch traced here: 363 us
  waiting for transfers between devices  91.5 us (25%)
  Pallas kernels  75.3 us (21%)
  starting transfers between devices  55.4 us (15%)
  local copies, waits for them, and re-layouts  44.1 us (12%)
  other arithmetic  42.3 us (12%)
  matrix products  33.4 us (9%)
  between operations  15.2 us (4%)
  blocking collectives  5.73 us (2%)
    dot_general x7, matrix products, mm(): return lax.dot_general(a, b, (dims, ((), ())), preferred_element_type=out)  33.4 us
    pallas_call x1, Pallas kernels, run_backward(): pl.pallas_call(functools.partial(scan_backward, q, taps, pairs, head, chu...  30.8 us
    ppermute x12, waiting for transfers between devices, crossed(): lax.ppermute(block, 'dp', [(i, i ^ bits) for i in range(lax.axis_size('dp...  27 us
    ppermute x6, starting transfers between devices, moved_by(): return lax.ppermute(block, 'dp', route)  19.3 us
    ppermute x12, waiting for transfers between devices, swapped(): return lax.ppermute(block, 'seq', [(i, i ^ bit) for i in range(size)])  18.9 us
    pallas_call x1, Pallas kernels, run_gate_backward(): pl.pallas_call(functools.partial(gate_backward, blocks, tile, z_rows, tal...  18.8 us
    ppermute x6, waiting for transfers between devices, turned(): lax.ppermute(piece, 'seq', [(i, i ^ bits) for i in range(size)])  17.2 us
    pallas_call x1, Pallas kernels, run_forward(): pl.pallas_call(functools.partial(scan_forward, q, taps, pairs, head), gri...  13.4 us
  transfers between devices with their start and end apart: 45, of which 19 were waited for; matrix products, arithmetic and copies ran while one was open for 30% of the time, Pallas kernels for 12%

profile of v6, /device:TPU:2, one launch (start us, length us, event | category | flops | bytes accessed | tf_op | source)
XLA Modules:
  0.0 363.0 jit_solution(665510606312019773)
XLA Ops:
  12.9 3.6 all-to-all-start
  16.7 2.5 collective-permute-start.2
  25.6 5.3 %all-to-all-done = bf16[4,48,1664]{2,1,0:T(8,128)(2,1)S(1)} async-done(((bf16[4,48,1664]{2,1,0:T(8,128)(2,1)}), bf16[4,48,1664]{2,1,0:T(8,128)(2,1)S(1)}, u32[]{:S(2)}, u32[]{:S(2)}) %all-to-all-start) | async-done | bytes 639008 | tf_op jit(solution)/shard_map/all_to_all | solution.py:738
  32.5 2.4 collective-permute-start.3
  39.2 5.8 %collective-permute-start.8 = (bf16[192,896]{1,0:T(8,128)(2,1)}, bf16[192,896]{1,0:T(8,128)(2,1)}, u32[]{:S(2)}, u32[]{:S(2)}) collective-permute-start(bf16[192,896]{1,0:T(8,128)(2,1)} %get-tuple-element.138), channel_id=1, source_target_pairs={{0,8},{4,12},{8,16},{12,20},{16,24},{20,28},{1,9},{5,13},{9,17},{1... | collective-permute-start | bytes 1032200 | tf_op jit(solution)/shard_map/ppermute | solution.py:565
  49.2 4.1 %collective-permute-done.3 = bf16[1,256,1536]{2,1,0:T(8,128)(2,1)S(1)} collective-permute-done((bf16[1,256,1536]{2,1,0:T(8,128)(2,1)S(1)}, bf16[1,256,1536]{2,1,0:T(8,128)(2,1)S(1)}, u32[]{:S(2)}, u32[]{:S(2)}) %collective-permute-start.3) | collective-permute-done | bytes 786464 | tf_op jit(solution)/shard_map/ppermute | solution.py:511
  55.6 4.2 %collective-permute-start.11 = (bf16[192,896]{1,0:T(8,128)(2,1)}, bf16[192,896]{1,0:T(8,128)(2,1)S(1)}, u32[]{:S(2)}, u32[]{:S(2)}) collective-permute-start(bf16[192,896]{1,0:T(8,128)(2,1)} %collective-permute-done.8), channel_id=1, source_target_pairs={{0,8},{4,12},{8,16},{12,20},{16,24},{20,28},{1,9},{5,13},{9,17},{1... | collective-permute-start | bytes 1032200 | tf_op jit(solution)/shard_map/ppermute | solution.py:565
  61.1 2.0 constant_dynamic-update-slice_fusion.29
  64.5 4.9 %collective-permute-done.5 = bf16[1,256,1536]{2,1,0:T(8,128)(2,1)S(1)} collective-permute-done((bf16[1,256,1536]{2,1,0:T(8,128)(2,1)S(1)}, bf16[1,256,1536]{2,1,0:T(8,128)(2,1)S(1)}, u32[]{:S(2)}, u32[]{:S(2)}) %collective-permute-start.5) | collective-permute-done | bytes 786464 | tf_op jit(solution)/shard_map/ppermute | solution.py:511
  71.0 5.2 %collective-permute-start.14 = (bf16[192,896]{1,0:T(8,128)(2,1)S(1)}, bf16[192,896]{1,0:T(8,128)(2,1)}, u32[]{:S(2)}, u32[]{:S(2)}) collective-permute-start(bf16[192,896]{1,0:T(8,128)(2,1)S(1)} %collective-permute-done.11), channel_id=1, source_target_pairs={{0,8},{4,12},{8,16},{12,20},{16,24},{20,28},{1,9},{5,13},{9,17},{1... | collective-permute-start | bytes 1032200 | tf_op jit(solution)/shard_map/ppermute | solution.py:565
  77.7 1.8 constant_dynamic-update-slice_fusion.28
  79.5 2.1 constant_dynamic-update-slice_fusion.27
  83.9 12.4 %collective-permute-done.13 = bf16[192,896]{1,0:T(8,128)(2,1)} collective-permute-done((bf16[192,896]{1,0:T(8,128)(2,1)}, bf16[192,896]{1,0:T(8,128)(2,1)}, u32[]{:S(2)}, u32[]{:S(2)}) %collective-permute-start.13) | collective-permute-done | bytes 344096 | tf_op jit(solution)/shard_map/ppermute | solution.py:569
  96.3 2.8 collective-permute-done.15
  99.1 1.7 constant_dynamic-update-slice_fusion.26
  100.8 1.9 constant_dynamic-update-slice_fusion.25
  103.7 6.2 %collective-permute-done.16 = bf16[192,896]{1,0:T(8,128)(2,1)S(1)} collective-permute-done((bf16[192,896]{1,0:T(8,128)(2,1)S(1)}, bf16[192,896]{1,0:T(8,128)(2,1)S(1)}, u32[]{:S(2)}, u32[]{:S(2)}) %collective-permute-start.16) | collective-permute-done | bytes 344096 | tf_op jit(solution)/shard_map/ppermute | solution.py:569
  110.7 2.5 maximum_select_fusion
  113.5 2.6 fusion.28
  119.4 5.3 %fusion.16.x_ref.xp_ref = bf16[1024,768]{1,0:T(8,128)(2,1)} fusion(bf16[1024,1536]{1,0:T(8,128)(2,1)S(1)} %bitcast.276, bf16[1536,896]{1,0:T(8,128)(2,1)} %constant_dynamic-update-slice_fusion.24), kind=kOutput, calls=%fused_computation.28 | convolution fusion | flops 2416705536 | bytes 7077888 | tf_op jit(solution)/shard_map/dot_general | solution.py:21
  124.8 1.9 maximum_select_fusion.1
  130.7 13.4 %scan_forward.1 = (f32[1024,768]{1,0:T(8,128)}, f32[8,128,768]{2,1,0:T(8,128)}) custom-call(bf16[1024,768]{1,0:T(8,128)(2,1)} %fusion.16.x_ref.xp_ref, f32[1024,128]{1,0:T(8,128)} %broadcast_select_fusion.1.small_ref, bf16[256,1024]{1,0:T(8,128)(2,1)} %bitcast.289, f32[1024,128]{1,0:T(8,128)} %broadcast_in_dim.75.dcol_ref.dcolp_ref, ...), custom_call_target="tpu_custom_call" | custom-call | tf_op jit(solution)/shard_map/scan_forward/pallas_call | solution.py:271
  144.2 10.8 %all-gather.2.cloned.1.call-done = bf16[3072,768]{1,0:T(8,128)(2,1)} async-done(((bf16[384,768]{1,0:T(8,128)(2,1)}), bf16[3072,768]{1,0:T(8,128)(2,1)}) %all-gather.2.cloned.1.call-update) | async-done | bytes 4718608 | tf_op jit(solution)/shard_map/all_gather | solution.py:772
  154.9 12.2 %gate_forward.1 = (f32[1024,768]{1,0:T(8,128)}, f32[1024,768]{1,0:T(8,128)}, f32[8,1024]{1,0:T(8,128)}, bf16[1536,768]{1,0:T(8,128)(2,1)}, bf16[2,768,768]{2,1,0:T(8,128)(2,1)}) custom-call(bf16[1024,1536]{1,0:T(8,128)(2,1)} %bitcast.277, bf16[1024,1536]{1,0:T(8,128)(2,1)} %bitcast.281, bf16[8,384,768]{2,1,0:T(8,128)(2,1)} %bitcast.292, ...), custom_call_target="tpu_custom_call" | custom-call | tf_op jit(solution)/shard_map/gate_forward/pallas_call | solution.py:452
  167.9 5.7 %psum.7 = f32[2,1024]{1,0:T(2,128)S(1)} all-reduce(f32[2,1024]{1,0:T(2,128)S(1)} %slice.314), channel_id=1, replica_groups=mesh['dp'=8,'seq'=4] {'seq'}, use_global_device_ids=true, to_apply=%region_1.2 | all-reduce | flops 2048 | bytes 16384 | tf_op jit(solution)/shard_map/psum | solution.py:820
  174.3 18.8 %gate_backward.1 = (bf16[1024,768]{1,0:T(8,128)(2,1)}, bf16[1024,768]{1,0:T(8,128)(2,1)}, f32[1024,768]{1,0:T(8,128)}, f32[8,768]{1,0:T(8,128)}, bf16[8,384,768]{2,1,0:T(8,128)(2,1)}) custom-call(bf16[1024,1536]{1,0:T(8,128)(2,1)} %bitcast.278, bf16[1024,1536]{1,0:T(8,128)(2,1)} %bitcast.282, f32[1024,768]{1,0:T(8,128)} %get-tuple-element.71.y_ref, ...), custom_call_target="tpu_custom_call" | custom-call | tf_op jit(solution)/shard_map/gate_backward/pallas_call | solution.py:484
  193.5 30.8 %scan_backward.1 = (bf16[1024,768]{1,0:T(8,128)(2,1)}, f32[1024,128]{1,0:T(8,128)}, f32[256,1024]{1,0:T(8,128)}, f32[8,768]{1,0:T(8,128)}, f32[8,128]{1,0:T(8,128)}) custom-call(bf16[1024,768]{1,0:T(8,128)(2,1)} %fusion.16.x_ref.xp_ref, bf16[1024,768]{1,0:T(8,128)(2,1)} %fusion.16.x_ref.xp_ref, f32[1024,128]{1,0:T(8,128)} %broadcast_select_fusion.1.small_ref, ...), custom_call_target="tpu_custom_call" | custom-call | tf_op jit(solution)/shard_map/scan_backward/pallas_call | solution.py:316
  224.3 5.4 %convolution_convert_fusion.1 = bf16[1536,768]{1,0:T(8,128)(2,1)} fusion(bf16[1024,1536]{1,0:T(8,128)(2,1)S(1)} %bitcast.279, bf16[1024,768]{1,0:T(8,128)(2,1)} %get-tuple-element.79), kind=kOutput, calls=%fused_computation.3 | convolution fusion | flops 2417098752 | bytes 7077888 | tf_op jit(solution)/shard_map/dot_general | solution.py:21
  229.7 1.9 fusion.45
  231.6 1.8 collective-permute-start.21
  233.5 1.9 copy.70
  242.5 2.5 dynamic-slice_bitcast_fusion
  247.7 6.2 %fusion.70 = f32[1024,1536]{1,0:T(8,128)} fusion(bf16[1024,768]{1,0:T(8,128)(2,1)} %get-tuple-element.87, bf16[1536,768]{1,0:T(8,128)(2,1)S(1)} %copy-done.47), kind=kOutput, calls=%fused_computation.228 | convolution fusion | flops 2415919104 | bytes 10223616 | tf_op jit(solution)/shard_map/dot_general | solution.py:21
  255.6 2.1 multiply_reduce_fusion.1
  257.8 3.2 convolution_convert_fusion
  265.4 9.6 %fusion.65 = (bf16[1024,1536]{1,0:T(8,128)(2,1)}, f32[1536]{0:T(1024)S(1)}) fusion(bf16[2,2,256,1536]{3,2,1,0:T(8,128)(2,1)S(1)} %copy-done.1, f32[1024,1536]{1,0:T(8,128)} %fusion.70, bf16[1536,896]{1,0:T(8,128)(2,1)} %constant_dynamic-update-slice_fusion.24, bf16[1024,64]{1,0:T(8,128)(2,1)} %copy.73, bf16[1024,64]{1,0:T(8,128)(2,1)} %copy.72, ...), kind=kOutput, calls=%fused_computation.223 | convolution fusion | flops 2831940096 | bytes 17176576 | tf_op jit(solution)/shard_map/dot_general | solution.py:21
  278.0 4.7 %collective-permute-done.24 = f32[6500]{0:T(1024)S(1)} collective-permute-done((f32[6500]{0:T(1024)S(1)}, f32[6500]{0:T(1024)S(1)}, u32[]{:S(2)}, u32[]{:S(2)}) %collective-permute-start.24) | collective-permute-done | bytes 26032 | tf_op jit(solution)/shard_map/ppermute | solution.py:569
  283.4 3.5 collective-permute-done.25
  287.0 2.0 fusion
  295.3 2.1 collective-permute-start.29
  300.5 7.5 %collective-permute-done.27 = bf16[1,256,1536]{2,1,0:T(8,128)(2,1)S(1)} collective-permute-done((bf16[1,256,1536]{2,1,0:T(8,128)(2,1)S(1)}, bf16[1,256,1536]{2,1,0:T(8,128)(2,1)S(1)}, u32[]{:S(2)}, u32[]{:S(2)}) %collective-permute-start.27) | collective-permute-done | bytes 786464 | tf_op jit(solution)/shard_map/ppermute | solution.py:511
  315.2 1.8 collective-permute-start.32
  318.0 2.2 collective-permute-start.34
  320.8 9.3 %collective-permute-done.33 = bf16[1,48,768]{2,1,0:T(8,128)(2,1)S(1)} collective-permute-done((bf16[1,48,768]{2,1,0:T(8,128)(2,1)S(1)}, bf16[1,48,768]{2,1,0:T(8,128)(2,1)S(1)}, u32[]{:S(2)}, u32[]{:S(2)}) %collective-permute-start.33) | collective-permute-done | bytes 73760 | tf_op jit(solution)/shard_map/ppermute | solution.py:651
  332.9 2.5 collective-permute-start.36
  336.1 4.5 %collective-permute-done.36 = bf16[1,48,896]{2,1,0:T(8,128)(2,1)S(1)} collective-permute-done((bf16[1,48,896]{2,1,0:T(8,128)(2,1)S(1)}, bf16[1,48,896]{2,1,0:T(8,128)(2,1)S(1)}, u32[]{:S(2)}, u32[]{:S(2)}) %collective-permute-start.36) | collective-permute-done | bytes 86048 | tf_op jit(solution)/shard_map/ppermute | solution.py:651
  340.6 3.4 collective-permute-done.37
  344.1 7.5 %reduce-scatter.5.cloned.1.call-done = bf16[256,1536]{1,0:T(8,128)(2,1)} async-done(((bf16[1024,1536]{1,0:T(8,128)(2,1)}), bf16[256,1536]{1,0:T(8,128)(2,1)}) %reduce-scatter.5.cloned.1.call-update) | async-done | bytes 786448 | tf_op jit(solution)/shard_map/reduce_scatter | solution.py:875
  (342 shorter events, 89.0 us)
Async XLA Ops:
  7.2 16.2 %collective-permute-start = (s32[1,1,256]{2,1,0:T(1,128)}, s32[1,1,256]{2,1,0:T(1,128)S(1)}, u32[]{:S(2)}, u32[]{:S(2)}) collective-permute-start(s32[1,1,256]{2,1,0:T(1,128)} %bitcast.336), channel_id=1, source_target_pairs={{0,2},{1,3},{2,0},{3,1},{4,6},{5,7},{6,4},{7,5},{8,10},{9,11},{10,... | collective-permute-start | bytes 3080 | tf_op jit(solution)/shard_map/ppermute | solution.py:511
  12.9 18.0 %all-to-all-start = ((bf16[4,48,1664]{2,1,0:T(8,128)(2,1)}), bf16[4,48,1664]{2,1,0:T(8,128)(2,1)S(1)}, u32[]{:S(2)}, u32[]{:S(2)}) async-start(bf16[4,48,1664]{2,1,0:T(8,128)(2,1)} %bitcast.4), calls=%async_computation | async-start | bytes 1277952 | tf_op jit(solution)/shard_map/all_to_all | solution.py:738
  16.6 138.3 %all-gather.2.cloned.1.call-start = ((), (), s32[]{:S(2)}) async-start(), calls=%async_computation.3 | async-start | bytes 5308416 | tf_op jit(solution)/shard_map/all_gather | solution.py:772
  16.7 8.9 %collective-permute-start.2 = (bf16[96,1536]{1,0:T(8,128)(2,1)S(1)}, bf16[96,1536]{1,0:T(8,128)(2,1)S(1)}, u32[]{:S(2)}, u32[]{:S(2)}) collective-permute-start(bf16[96,1536]{1,0:T(8,128)(2,1)S(1)} %convert_element_type.199), channel_id=1, source_target_pairs={{0,0},{1,4},{2,8},{3,12},{4,1},{5,5},{6,9},{7,13},{8,2},{9,6},{10,... | collective-permute-start | bytes 884744 | tf_op jit(solution)/shard_map/ppermute | solution.py:750
  23.3 1.2 collective-permute-start.1
  32.5 20.8 %collective-permute-start.3 = (bf16[1,256,1536]{2,1,0:T(8,128)(2,1)S(1)}, bf16[1,256,1536]{2,1,0:T(8,128)(2,1)S(1)}, u32[]{:S(2)}, u32[]{:S(2)}) collective-permute-start(bf16[1,256,1536]{2,1,0:T(8,128)(2,1)S(1)} %bitcast.286), channel_id=1, source_target_pairs={{0,2},{1,3},{2,0},{3,1},{4,6},{5,7},{6,4},{7,5},{8,10},{9,11},{10,... | collective-permute-start | bytes 2359304 | tf_op jit(solution)/shard_map/ppermute | solution.py:511
  37.5 9.9 %collective-permute-start.7 = (bf16[192,896]{1,0:T(8,128)(2,1)}, bf16[192,896]{1,0:T(8,128)(2,1)}, u32[]{:S(2)}, u32[]{:S(2)}) collective-permute-start(bf16[192,896]{1,0:T(8,128)(2,1)} %get-tuple-element.138), channel_id=1, source_target_pairs={{0,4},{4,0},{8,12},{12,8},{16,20},{20,16},{24,28},{28,24},{1,5},{5... | collective-permute-start | bytes 1032200 | tf_op jit(solution)/shard_map/ppermute | solution.py:569
  38.1 31.3 %collective-permute-start.5 = (bf16[1,256,1536]{2,1,0:T(8,128)(2,1)S(1)}, bf16[1,256,1536]{2,1,0:T(8,128)(2,1)S(1)}, u32[]{:S(2)}, u32[]{:S(2)}) collective-permute-start(bf16[1,256,1536]{2,1,0:T(8,128)(2,1)S(1)} %copy-done.6), channel_id=1, source_target_pairs={{0,2},{1,3},{2,0},{3,1},{4,6},{5,7},{6,4},{7,5},{8,10},{9,11},{10,... | collective-permute-start | bytes 2359304 | tf_op jit(solution)/shard_map/ppermute | solution.py:511
  39.2 15.5 %collective-permute-start.8 = (bf16[192,896]{1,0:T(8,128)(2,1)}, bf16[192,896]{1,0:T(8,128)(2,1)}, u32[]{:S(2)}, u32[]{:S(2)}) collective-permute-start(bf16[192,896]{1,0:T(8,128)(2,1)} %get-tuple-element.138), channel_id=1, source_target_pairs={{0,8},{4,12},{8,16},{12,20},{16,24},{20,28},{1,9},{5,13},{9,17},{1... | collective-permute-start | bytes 1032200 | tf_op jit(solution)/shard_map/ppermute | solution.py:565
  45.0 10.6 %collective-permute-start.9 = (bf16[192,896]{1,0:T(8,128)(2,1)}, bf16[192,896]{1,0:T(8,128)(2,1)}, u32[]{:S(2)}, u32[]{:S(2)}) collective-permute-start(bf16[192,896]{1,0:T(8,128)(2,1)} %get-tuple-element.138), channel_id=1, source_target_pairs={{8,0},{12,4},{16,8},{20,12},{24,16},{28,20},{9,1},{13,5},{17,9},{2... | collective-permute-start | bytes 1032200 | tf_op jit(solution)/shard_map/ppermute | solution.py:565
  55.6 15.1 %collective-permute-start.11 = (bf16[192,896]{1,0:T(8,128)(2,1)}, bf16[192,896]{1,0:T(8,128)(2,1)S(1)}, u32[]{:S(2)}, u32[]{:S(2)}) collective-permute-start(bf16[192,896]{1,0:T(8,128)(2,1)} %collective-permute-done.8), channel_id=1, source_target_pairs={{0,8},{4,12},{8,16},{12,20},{16,24},{20,28},{1,9},{5,13},{9,17},{1... | collective-permute-start | bytes 1032200 | tf_op jit(solution)/shard_map/ppermute | solution.py:565
  59.8 11.0 %collective-permute-start.12 = (bf16[192,896]{1,0:T(8,128)(2,1)}, bf16[192,896]{1,0:T(8,128)(2,1)}, u32[]{:S(2)}, u32[]{:S(2)}) collective-permute-start(bf16[192,896]{1,0:T(8,128)(2,1)} %collective-permute-done.9), channel_id=1, source_target_pairs={{8,0},{12,4},{16,8},{20,12},{24,16},{28,20},{9,1},{13,5},{17,9},{2... | collective-permute-start | bytes 1032200 | tf_op jit(solution)/shard_map/ppermute | solution.py:565
  63.1 7.7 %collective-permute-start.10 = (bf16[192,896]{1,0:T(8,128)(2,1)}, bf16[192,896]{1,0:T(8,128)(2,1)}, u32[]{:S(2)}, u32[]{:S(2)}) collective-permute-start(bf16[192,896]{1,0:T(8,128)(2,1)} %get-tuple-element.126), channel_id=1, source_target_pairs={{0,4},{4,0},{8,12},{12,8},{16,20},{20,16},{24,28},{28,24},{1,5},{5... | collective-permute-start | bytes 1032200 | tf_op jit(solution)/shard_map/ppermute | solution.py:569
  70.8 238.6 %reduce-scatter.3.cloned.1.call-start = ((), (), s32[]{:S(2)}) async-start(), calls=%async_computation.4 | async-start | bytes 5308416 | tf_op jit(solution)/shard_map/reduce_scatter | solution.py:832
  71.0 39.8 %collective-permute-start.4 = (bf16[2,256,1536]{2,1,0:T(8,128)(2,1)}, bf16[2,256,1536]{2,1,0:T(8,128)(2,1)}, u32[]{:S(2)}, u32[]{:S(2)}) collective-permute-start(bf16[2,256,1536]{2,1,0:T(8,128)(2,1)} %maximum_select_fusion.2), channel_id=1, source_target_pairs={{0,1},{1,0},{2,3},{3,2},{4,5},{5,4},{6,7},{7,6},{8,9},{9,8},{10,11... | collective-permute-start | bytes 4718600 | tf_op jit(solution)/shard_map/ppermute | solution.py:511
  71.0 25.3 %collective-permute-start.14 = (bf16[192,896]{1,0:T(8,128)(2,1)S(1)}, bf16[192,896]{1,0:T(8,128)(2,1)}, u32[]{:S(2)}, u32[]{:S(2)}) collective-permute-start(bf16[192,896]{1,0:T(8,128)(2,1)S(1)} %collective-permute-done.11), channel_id=1, source_target_pairs={{0,8},{4,12},{8,16},{12,20},{16,24},{20,28},{1,9},{5,13},{9,17},{1... | collective-permute-start | bytes 1032200 | tf_op jit(solution)/shard_map/ppermute | solution.py:565
  76.2 22.9 %collective-permute-start.15 = (bf16[192,896]{1,0:T(8,128)(2,1)}, bf16[192,896]{1,0:T(8,128)(2,1)}, u32[]{:S(2)}, u32[]{:S(2)}) collective-permute-start(bf16[192,896]{1,0:T(8,128)(2,1)} %collective-permute-done.12), channel_id=1, source_target_pairs={{8,0},{12,4},{16,8},{20,12},{24,16},{28,20},{9,1},{13,5},{17,9},{2... | collective-permute-start | bytes 1032200 | tf_op jit(solution)/shard_map/ppermute | solution.py:565
  81.6 14.7 %collective-permute-start.13 = (bf16[192,896]{1,0:T(8,128)(2,1)}, bf16[192,896]{1,0:T(8,128)(2,1)}, u32[]{:S(2)}, u32[]{:S(2)}) collective-permute-start(bf16[192,896]{1,0:T(8,128)(2,1)} %get-tuple-element.124), channel_id=1, source_target_pairs={{0,4},{4,0},{8,12},{12,8},{16,20},{20,16},{24,28},{28,24},{1,5},{5... | collective-permute-start | bytes 1032200 | tf_op jit(solution)/shard_map/ppermute | solution.py:569
  83.9 33.1 %copy-start.20 = (f32[1024]{0:T(1024)}, f32[1024]{0:T(1024)S(1)}, u32[]{:S(2)}) copy-start(f32[1024]{0:T(1024)S(1)} %get-tuple-element.174) | copy-start | bytes 12292
  83.9 40.9 %collective-permute-start.6 = (bf16[2,256,1536]{2,1,0:T(8,128)(2,1)}, bf16[2,256,1536]{2,1,0:T(8,128)(2,1)S(1)}, u32[]{:S(2)}, u32[]{:S(2)}) collective-permute-start(bf16[2,256,1536]{2,1,0:T(8,128)(2,1)} %maximum_select_fusion.4), channel_id=1, source_target_pairs={{0,1},{1,0},{2,3},{3,2},{4,5},{5,4},{6,7},{7,6},{8,9},{9,8},{10,11... | collective-permute-start | bytes 4718600 | tf_op jit(solution)/shard_map/ppermute | solution.py:511
  102.7 7.2 %collective-permute-start.16 = (bf16[192,896]{1,0:T(8,128)(2,1)S(1)}, bf16[192,896]{1,0:T(8,128)(2,1)S(1)}, u32[]{:S(2)}, u32[]{:S(2)}) collective-permute-start(bf16[192,896]{1,0:T(8,128)(2,1)S(1)} %get-tuple-element.122), channel_id=1, source_target_pairs={{0,4},{4,0},{8,12},{12,8},{16,20},{20,16},{24,28},{28,24},{1,5},{5... | collective-permute-start | bytes 1032200 | tf_op jit(solution)/shard_map/ppermute | solution.py:569
  118.0 8.9 %collective-permute-start.17 = (bf16[1,64,1024]{2,1,0:T(8,128)(2,1)S(1)}, bf16[1,64,1024]{2,1,0:T(8,128)(2,1)}, u32[]{:S(2)}, u32[]{:S(2)}) collective-permute-start(bf16[1,64,1024]{2,1,0:T(8,128)(2,1)S(1)} %bitcast.304), channel_id=1, source_target_pairs={{0,2},{1,3},{2,0},{3,1},{4,6},{5,7},{6,4},{7,5},{8,10},{9,11},{10,... | collective-permute-start | bytes 393224 | tf_op jit(solution)/shard_map/ppermute | solution.py:511
  127.9 1.9 collective-permute-start.18
  193.1 158.5 %reduce-scatter.5.cloned.1.call-start = ((), (), s32[]{:S(2)}) async-start(), calls=%async_computation.5 | async-start | bytes 3932160 | tf_op jit(solution)/shard_map/reduce_scatter | solution.py:875
  193.5 30.8 %copy-start.1 = (bf16[2,2,256,1536]{3,2,1,0:T(8,128)(2,1)S(1)}, bf16[2,2,256,1536]{3,2,1,0:T(8,128)(2,1)}, u32[]{:S(2)}) copy-start(bf16[2,2,256,1536]{3,2,1,0:T(8,128)(2,1)} %copy-done) | copy-start | bytes 9437188
  231.6 24.0 %collective-permute-start.20 = (bf16[64,1024]{1,0:T(8,128)(2,1)}, bf16[64,1024]{1,0:T(8,128)(2,1)}, u32[]{:S(2)}, u32[]{:S(2)}) collective-permute-start(bf16[64,1024]{1,0:T(8,128)(2,1)} %get-tuple-element.135), channel_id=1, source_target_pairs={{0,1},{1,0},{2,3},{3,2},{4,5},{5,4},{6,7},{7,6},{8,9},{9,8},{10,11... | collective-permute-start | bytes 393224 | tf_op jit(solution)/shard_map/ppermute | solution.py:679
  231.6 24.0 %collective-permute-start.21 = (bf16[64,1024]{1,0:T(8,128)(2,1)}, bf16[64,1024]{1,0:T(8,128)(2,1)}, u32[]{:S(2)}, u32[]{:S(2)}) collective-permute-start(bf16[64,1024]{1,0:T(8,128)(2,1)} %get-tuple-element.137), channel_id=1, source_target_pairs={{0,2},{1,3},{2,0},{3,1},{4,6},{5,7},{6,4},{7,5},{8,10},{9,11},{10,... | collective-permute-start | bytes 393224 | tf_op jit(solution)/shard_map/ppermute | solution.py:679
  233.3 22.3 %collective-permute-start.22 = (bf16[64,1024]{1,0:T(8,128)(2,1)}, bf16[64,1024]{1,0:T(8,128)(2,1)}, u32[]{:S(2)}, u32[]{:S(2)}) collective-permute-start(bf16[64,1024]{1,0:T(8,128)(2,1)} %get-tuple-element.136), channel_id=1, source_target_pairs={{0,3},{1,2},{2,1},{3,0},{4,7},{5,6},{6,5},{7,4},{8,11},{9,10},{10,... | collective-permute-start | bytes 393224 | tf_op jit(solution)/shard_map/ppermute | solution.py:679
  245.0 45.9 %collective-permute-start.19 = (bf16[4,192,768]{2,1,0:T(8,128)(2,1)}, bf16[4,192,768]{2,1,0:T(8,128)(2,1)}, u32[]{:S(2)}, u32[]{:S(2)}) collective-permute-start(bf16[4,192,768]{2,1,0:T(8,128)(2,1)} %dynamic-slice_bitcast_fusion), channel_id=1, source_target_pairs={{0,4},{4,0},{8,12},{12,8},{16,20},{20,16},{24,28},{28,24},{1,5},{5... | collective-permute-start | bytes 3538952 | tf_op jit(solution)/shard_map/ppermute | solution.py:569
  263.1 23.9 %collective-permute-start.26 = (bf16[2,256,1536]{2,1,0:T(8,128)(2,1)}, bf16[2,256,1536]{2,1,0:T(8,128)(2,1)}, u32[]{:S(2)}, u32[]{:S(2)}) collective-permute-start(bf16[2,256,1536]{2,1,0:T(8,128)(2,1)} %select_bitcast_fusion), channel_id=1, source_target_pairs={{0,1},{1,0},{2,3},{3,2},{4,5},{5,4},{6,7},{7,6},{8,9},{9,8},{10,11... | collective-permute-start | bytes 4718600 | tf_op jit(solution)/shard_map/ppermute | solution.py:511
  275.2 7.5 %collective-permute-start.24 = (f32[6500]{0:T(1024)S(1)}, f32[6500]{0:T(1024)S(1)}, u32[]{:S(2)}, u32[]{:S(2)}) collective-permute-start(f32[6500]{0:T(1024)S(1)} %concatenate.194), channel_id=1, source_target_pairs={{0,16},{4,20},{8,24},{12,28},{16,0},{20,4},{24,8},{28,12},{1,17},{... | collective-permute-start | bytes 78008 | tf_op jit(solution)/shard_map/ppermute | solution.py:569
  282.7 4.2 %collective-permute-start.25 = (f32[6500]{0:T(1024)S(1)}, f32[6500]{0:T(1024)S(1)}, u32[]{:S(2)}, u32[]{:S(2)}) collective-permute-start(f32[6500]{0:T(1024)S(1)} %add.299), channel_id=1, source_target_pairs={{0,8},{4,12},{8,0},{12,4},{16,24},{20,28},{24,16},{28,20},{1,9},{5... | collective-permute-start | bytes 78008 | tf_op jit(solution)/shard_map/ppermute | solution.py:569
  282.8 8.0 %collective-permute-start.23 = (bf16[4,192,128]{2,1,0:T(8,128)(2,1)S(1)}, bf16[4,192,128]{2,1,0:T(8,128)(2,1)S(1)}, u32[]{:S(2)}, u32[]{:S(2)}) collective-permute-start(bf16[4,192,128]{2,1,0:T(8,128)(2,1)S(1)} %dynamic-slice_bitcast_fusion.5), channel_id=1, source_target_pairs={{0,4},{4,0},{8,12},{12,8},{16,20},{20,16},{24,28},{28,24},{1,5},{5... | collective-permute-start | bytes 589832 | tf_op jit(solution)/shard_map/ppermute | solution.py:569
  289.1 18.9 %collective-permute-start.27 = (bf16[1,256,1536]{2,1,0:T(8,128)(2,1)S(1)}, bf16[1,256,1536]{2,1,0:T(8,128)(2,1)S(1)}, u32[]{:S(2)}, u32[]{:S(2)}) collective-permute-start(bf16[1,256,1536]{2,1,0:T(8,128)(2,1)S(1)} %fusion.27), channel_id=1, source_target_pairs={{0,2},{1,3},{2,0},{3,1},{4,6},{5,7},{6,4},{7,5},{8,10},{9,11},{10,... | collective-permute-start | bytes 2359304 | tf_op jit(solution)/shard_map/ppermute | solution.py:511
  292.6 6.2 %collective-permute-start.38 = (f32[6500]{0:T(1024)S(1)}, f32[6500]{0:T(1024)S(1)}, u32[]{:S(2)}, u32[]{:S(2)}) collective-permute-start(f32[6500]{0:T(1024)S(1)} %add.300), channel_id=1, source_target_pairs={{0,4},{4,0},{8,12},{12,8},{16,20},{20,16},{24,28},{28,24},{1,5},{5... | collective-permute-start | bytes 78008 | tf_op jit(solution)/shard_map/ppermute | solution.py:569
  294.4 36.8 %collective-permute-start.28 = (bf16[192,896]{1,0:T(8,128)(2,1)}, bf16[192,896]{1,0:T(8,128)(2,1)}, u32[]{:S(2)}, u32[]{:S(2)}) collective-permute-start(bf16[192,896]{1,0:T(8,128)(2,1)} %get-tuple-element.133), channel_id=1, source_target_pairs={{0,8},{4,12},{8,0},{12,4},{16,24},{20,28},{24,16},{28,20},{1,9},{5... | collective-permute-start | bytes 1032200 | tf_op jit(solution)/shard_map/ppermute | solution.py:569
  295.3 35.8 %collective-permute-start.29 = (bf16[192,896]{1,0:T(8,128)(2,1)S(1)}, bf16[192,896]{1,0:T(8,128)(2,1)}, u32[]{:S(2)}, u32[]{:S(2)}) collective-permute-start(bf16[192,896]{1,0:T(8,128)(2,1)S(1)} %get-tuple-element.132), channel_id=1, source_target_pairs={{0,16},{4,20},{8,24},{12,28},{16,0},{20,4},{24,8},{28,12},{1,17},{... | collective-permute-start | bytes 1032200 | tf_op jit(solution)/shard_map/ppermute | solution.py:569
  297.4 33.7 %collective-permute-start.30 = (bf16[192,896]{1,0:T(8,128)(2,1)S(1)}, bf16[192,896]{1,0:T(8,128)(2,1)}, u32[]{:S(2)}, u32[]{:S(2)}) collective-permute-start(bf16[192,896]{1,0:T(8,128)(2,1)S(1)} %get-tuple-element.131), channel_id=1, source_target_pairs={{0,24},{4,28},{8,16},{12,20},{16,8},{20,12},{24,0},{28,4},{1,25},{... | collective-permute-start | bytes 1032200 | tf_op jit(solution)/shard_map/ppermute | solution.py:569
  298.9 10.6 %collective-permute-start.39 = (f32[1,1,6500]{2,1,0:T(1,128)S(1)}, f32[1,1,6500]{2,1,0:T(1,128)S(1)}, u32[]{:S(2)}, u32[]{:S(2)}) collective-permute-start(f32[1,1,6500]{2,1,0:T(1,128)S(1)} %broadcast_in_dim_broadcast_in_dim.3), channel_id=1, source_target_pairs={{0,2},{1,3},{2,0},{3,1},{4,6},{5,7},{6,4},{7,5},{8,10},{9,11},{10,... | collective-permute-start | bytes 78008 | tf_op jit(solution)/shard_map/ppermute | solution.py:511
  309.6 1.3 collective-permute-start.40
  311.7 3.5 collective-permute-start.31
  315.2 5.0 %collective-permute-start.32 = (bf16[1,48,768]{2,1,0:T(8,128)(2,1)S(1)}, bf16[1,48,768]{2,1,0:T(8,128)(2,1)S(1)}, u32[]{:S(2)}, u32[]{:S(2)}) collective-permute-start(bf16[1,48,768]{2,1,0:T(8,128)(2,1)S(1)} %get-tuple-element.160), channel_id=1, source_target_pairs={{0,2},{1,3},{2,0},{3,1},{4,6},{5,7},{6,4},{7,5},{8,10},{9,11},{10,... | collective-permute-start | bytes 221192 | tf_op jit(solution)/shard_map/ppermute | solution.py:651
  318.0 12.2 %collective-permute-start.34 = (bf16[96,1536]{1,0:T(8,128)(2,1)S(1)}, bf16[96,1536]{1,0:T(8,128)(2,1)S(1)}, u32[]{:S(2)}, u32[]{:S(2)}) collective-permute-start(bf16[96,1536]{1,0:T(8,128)(2,1)S(1)} %bitcast.318), channel_id=1, source_target_pairs={{0,0},{4,1},{8,2},{12,3},{1,4},{5,5},{9,6},{13,7},{2,8},{6,9},{10,... | collective-permute-start | bytes 884744 | tf_op jit(solution)/shard_map/ppermute | solution.py:887
  320.3 9.8 %collective-permute-start.33 = (bf16[1,48,768]{2,1,0:T(8,128)(2,1)S(1)}, bf16[1,48,768]{2,1,0:T(8,128)(2,1)S(1)}, u32[]{:S(2)}, u32[]{:S(2)}) collective-permute-start(bf16[1,48,768]{2,1,0:T(8,128)(2,1)S(1)} %get-tuple-element.159), channel_id=1, source_target_pairs={{0,3},{1,2},{2,1},{3,0},{4,7},{5,6},{6,5},{7,4},{8,11},{9,10},{10,... | collective-permute-start | bytes 221192 | tf_op jit(solution)/shard_map/ppermute | solution.py:651
  332.6 20.6 %copy-start.7 = (bf16[1,256,1536]{2,1,0:T(8,128)(2,1)S(1)}, bf16[1,256,1536]{2,1,0:T(8,128)(2,1)}, u32[]{:S(2)}) copy-start(bf16[1,256,1536]{2,1,0:T(8,128)(2,1)} %param.14) | copy-start | bytes 2359300
  332.6 3.5 collective-permute-start.35
  332.9 7.7 %collective-permute-start.36 = (bf16[1,48,896]{2,1,0:T(8,128)(2,1)S(1)}, bf16[1,48,896]{2,1,0:T(8,128)(2,1)S(1)}, u32[]{:S(2)}, u32[]{:S(2)}) collective-permute-start(bf16[1,48,896]{2,1,0:T(8,128)(2,1)S(1)} %get-tuple-element.157), channel_id=1, source_target_pairs={{0,2},{1,3},{2,0},{3,1},{4,6},{5,7},{6,4},{7,5},{8,10},{9,11},{10,... | collective-permute-start | bytes 258056 | tf_op jit(solution)/shard_map/ppermute | solution.py:651
  335.4 8.6 %collective-permute-start.37 = (bf16[1,48,896]{2,1,0:T(8,128)(2,1)S(1)}, bf16[1,48,896]{2,1,0:T(8,128)(2,1)S(1)}, u32[]{:S(2)}, u32[]{:S(2)}) collective-permute-start(bf16[1,48,896]{2,1,0:T(8,128)(2,1)S(1)} %get-tuple-element.156), channel_id=1, source_target_pairs={{0,3},{1,2},{2,1},{3,0},{4,7},{5,6},{6,5},{7,4},{8,11},{9,10},{10,... | collective-permute-start | bytes 258056 | tf_op jit(solution)/shard_map/ppermute | solution.py:651
  (51 other events, 314.4 us)
Sparse Core Ops, SparseCore 0:
  70.9 83.9 all-gather.1
  193.2 104.1 reduce-scatter.2
  309.6 41.9 reduce-scatter.4
